TPU v7x, 256 devices: a whole 4x4x8 slice. The times are simulated.
256 devices in a mesh: slab: 16 (over x_lo, y, core), chan: 16 (over x_hi, z).
Axes of the slice: x: 4 (x_hi: 2, x_lo: 2; x = x_hi * 2 + x_lo), y: 4, z: 8, core: 2. Of those that a mesh axis runs over, the one named last changes fastest.
Arguments:
- field: bfloat16 [1, 128, 128, 128, 128], P(None, 'chan', 'slab'), may hold values from -6 to 6
- local_weight: bfloat16 [128, 128], replicated, may hold values from -0.5 to 0.5
- bias: float32 [128], replicated, may hold values from -3 to 3
- spec_weight: float32 [2, 128, 128, 4096], P(None, 'chan', None, 'slab'), may hold values from -4.2 to 4.2
Outputs:
- activated: bfloat16 [1, 128, 128, 128, 128], P(None, 'chan', 'slab')
All inputs are finite; a program needn't handle non-finite values.
Results may differ from a plain program's by a relative error of at most 0.0026.
Values may be sent and summed in bfloat16 or wider, within the bound.
No kernel may reach another device: no remote copies, remote signals or barrier semaphores. Data moves between devices by JAX's collectives and lax.ppermute only.
A program may use at most 64 MiB of HBM per device.

v0:
```python
import math

import jax
import jax.numpy as jnp
from jax import lax
from jax.sharding import PartitionSpec as P

GRID = 128
KEEP = 16
MODES = 4096


PRECISE = lax.Precision.HIGHEST


def mode_freqs(count, length):
    index = jnp.arange(count, dtype=jnp.int32)
    return jnp.where(index < count // 2, index, index + (length - count))


def phase_table(freqs, positions, length):
    product_int = freqs[:, None] * positions[None, :] % length
    return 2.0 * math.pi * product_int.astype(jnp.float32) / length


def build_tables(zcells):
    xfreq = mode_freqs(KEEP, GRID)
    zfreq = jnp.arange(KEEP, dtype=jnp.int32)
    cells = jnp.arange(GRID, dtype=jnp.int32)
    angle_x = phase_table(xfreq, cells, GRID)
    angle_z = phase_table(zfreq, zcells, GRID)
    cos_x, sin_x = (jnp.cos(angle_x), jnp.sin(angle_x))
    cos_z, sin_z = (jnp.cos(angle_z), jnp.sin(angle_z))
    table_x = jnp.concatenate([cos_x, -sin_x], 0).astype(jnp.bfloat16)
    fold_factor = jnp.where(zfreq == 0, 1.0, 2.0).astype(jnp.float32)
    return (cos_x, sin_x, cos_z, sin_z, table_x, fold_factor)


def product(form, left, right):
    return jnp.einsum(form, left, right, precision=PRECISE)


def on_device(field, local_weight, bias, spec_weight):
    samples, chan_local, zdepth = (field.shape[0], field.shape[1], field.shape[2])
    zcells = lax.axis_index("slab") * zdepth + jnp.arange(zdepth, dtype=jnp.int32)
    cos_x, sin_x, cos_z, sin_z, table_x, fold_factor = build_tables(zcells)
    section_x = jnp.einsum("kx,bczxy->bczky", table_x, field, preferred_element_type=jnp.float32)
    part_real = section_x[:, :, :, :KEEP]
    part_imag = section_x[:, :, :, KEEP:]
    wave_real = product("bczky,jy->bczkj", part_real, cos_x) + product(
        "bczky,jy->bczkj", part_imag, sin_x
    )
    wave_imag = product("bczky,jy->bczkj", part_imag, cos_x) - product(
        "bczky,jy->bczkj", part_real, sin_x
    )
    four_real = product("bczkj,lz->bckjl", wave_real, cos_z) + product(
        "bczkj,lz->bckjl", wave_imag, sin_z
    )
    four_imag = product("bczkj,lz->bckjl", wave_imag, cos_z) - product(
        "bczkj,lz->bckjl", wave_real, sin_z
    )
    partial_value = jnp.stack(
        [
            four_real.reshape(samples, chan_local, MODES),
            four_imag.reshape(samples, chan_local, MODES),
        ],
        1,
    )
    owned = lax.psum_scatter(partial_value, "slab", scatter_dimension=3, tiled=True)
    piece = lax.all_gather(owned, "chan", axis=2, tiled=True)
    weight_real = spec_weight[0]
    weight_imag = spec_weight[1]
    coef_real = piece[:, 0]
    coef_imag = piece[:, 1]
    mixed_real = product("bcm,ocm->bom", coef_real, weight_real) - product(
        "bcm,ocm->bom", coef_imag, weight_imag
    )
    mixed_imag = product("bcm,ocm->bom", coef_real, weight_imag) + product(
        "bcm,ocm->bom", coef_imag, weight_real
    )
    mixed = jnp.stack([mixed_real, mixed_imag], 1)
    spectrum = lax.all_gather(mixed, "slab", axis=3, tiled=True)
    spectral = spectrum.reshape(samples, 2, chan_local, KEEP, KEEP, KEEP) * fold_factor
    spectral_real, spectral_imag = (spectral[:, 0], spectral[:, 1])
    plane_real = product("bokjl,lz->bozkj", spectral_real, cos_z) - product(
        "bokjl,lz->bozkj", spectral_imag, sin_z
    )
    plane_imag = product("bokjl,lz->bozkj", spectral_imag, cos_z) + product(
        "bokjl,lz->bozkj", spectral_real, sin_z
    )
    line_real = product("bozkj,kx->bozxj", plane_real, cos_x) - product(
        "bozkj,kx->bozxj", plane_imag, sin_x
    )
    line_imag = product("bozkj,kx->bozxj", plane_imag, cos_x) + product(
        "bozkj,kx->bozxj", plane_real, sin_x
    )
    mapped = jnp.einsum(
        "oc,bczxy->bozxy",
        local_weight,
        lax.all_to_all(field, "chan", split_axis=3, concat_axis=1, tiled=True),
        preferred_element_type=jnp.float32,
    )
    local = lax.all_to_all(mapped, "chan", split_axis=1, concat_axis=3, tiled=True)
    inverse = (
        product("bozxj,jy->bozxy", line_real, cos_x) - product("bozxj,jy->bozxy", line_imag, sin_x)
    ) / GRID**3
    offset = lax.dynamic_slice_in_dim(bias, lax.axis_index("chan") * chan_local, chan_local, 0)
    total = inverse + local + offset[None, :, None, None, None]
    return jax.nn.gelu(total, approximate=False).astype(jnp.bfloat16)


def solution(mesh):
    placed = (P(None, "chan", "slab", None, None), P(), P(), P(None, "chan", None, "slab"))
    return jax.shard_map(
        on_device,
        mesh=mesh,
        in_specs=placed,
        out_specs=P(None, "chan", "slab", None, None),
        check_vma=False,
    )
```

profile of v0, /device:TPU:1, one launch (start us, length us, event | category | flops | bytes accessed | tf_op | source)
XLA Modules:
  0.0 312.5 jit_solution(12145251189520731102)
XLA Ops:
  6.5 3.0 copy.46
  9.5 60.4 %all_to_all.33 = bf16[1,8,8,128,128]{4,2,1,0,3:T(8,128)(2,1)S(1)} all-to-all(bf16[1,8,8,128,128]{4,2,1,0,3:T(8,128)(2,1)S(1)} %copy.46), channel_id=1, replica_groups=mesh['slab'=16,'chan'=16] {'chan'}, dimensions={3} | all-to-all | bytes 4194304 | tf_op jit(solution)/shard_map/all_to_all | solution.py:100
  69.8 1.4 copy.100
  71.8 4.5 %convolution_bitcast_fusion = f32[1,128,8,8,128]{1,4,3,2,0:T(8,128)} fusion(bf16[128,8,8,128]{3,2,1,0:T(8,128)(2,1)S(1)} %bitcast.190, bf16[128,128]{1,0:T(8,128)(2,1)S(1)} %copy-done), kind=kOutput, calls=%fused_computation.21 | convolution fusion | flops 268435456 | bytes 6324224 | tf_op jit(solution)/shard_map/oc,bczxy->bozxy/dot_general | solution.py:97
  76.3 5.4 %copy.50 = f32[1,128,8,8,128]{4,3,2,0,1:T(8,128)} copy(f32[1,128,8,8,128]{1,4,3,2,0:T(8,128)} %convolution_bitcast_fusion) | data formatting | bytes 8388608 | tf_op jit(solution)/shard_map/oc,bczxy->bozxy/transpose | solution.py:97
  81.7 6.3 %all-to-all-start.1 = ((f32[1,128,8,8,128]{4,3,2,0,1:T(8,128)}), f32[1,128,8,8,128]{4,3,2,0,1:T(8,128)}, u32[]{:S(2)}, u32[]{:S(2)}) async-start(f32[1,128,8,8,128]{4,3,2,0,1:T(8,128)} %copy.50), calls=%async_computation.2 | async-start | bytes 8388608 | tf_op jit(solution)/shard_map/all_to_all | solution.py:103
  88.8 0.7 fusion.29
  89.5 0.7 fusion.28
  90.2 0.7 convolution_subtract_fusion.3
  90.9 0.7 convolution_add_fusion.3
  91.5 1.9 fusion.34
  93.5 1.9 convolution_add_fusion
  95.4 0.6 stack_reshape.6
  96.0 1.9 fusion.30
  98.0 1.9 convolution_subtract_fusion
  100.5 0.7 pad_maximum_fusion
  101.4 67.8 %reduce-scatter.2.cloned.1.call-done = f32[1,2,8,256]{3,2,1,0:T(8,128)} async-done(((f32[1,2,8,4096]{3,2,1,0:T(8,128)}), f32[1,2,8,256]{3,2,1,0:T(8,128)}) %reduce-scatter.2.cloned.1.call-update) | async-done | bytes 16400 | tf_op jit(solution)/shard_map/reduce_scatter | solution.py:69
  169.1 41.9 %all_gather.6 = f32[1,2,128,256]{3,2,1,0:T(8,128)S(1)} all-gather(f32[1,2,8,256]{3,2,1,0:T(8,128)} %reduce-scatter.2.cloned.1.call-done), channel_id=1, replica_groups=mesh['slab'=16,'chan'=16] {'chan'}, dimensions={2}, use_global_device_ids=true | all-gather | bytes 278528 | tf_op jit(solution)/shard_map/all_gather | solution.py:70
  211.0 1.9 fusion.22
  212.9 27.9 %all_gather.7 = f32[1,2,8,4096]{3,2,1,0:T(8,128)S(1)} all-gather(f32[1,2,8,256]{3,2,1,0:T(8,128)S(1)} %pad_maximum_fusion.1), channel_id=1, replica_groups=mesh['slab'=16,'chan'=16] {'slab'}, dimensions={3}, use_global_device_ids=true | all-gather | bytes 278528 | tf_op jit(solution)/shard_map/all_gather | solution.py:82
  240.8 2.0 reshape.210
  242.9 1.8 broadcast_multiply_fusion
  244.7 7.5 %fusion.27 = f32[8,8,16,16]{3,0,2,1:T(8,128)S(1)} fusion(f32[1,2,8,16,16,16]{5,4,3,2,1,0:T(8,128)S(1)} %broadcast_multiply_fusion, s32[8]{0:T(128)S(1)} %iota_add_fusion), kind=kOutput, calls=%fused_computation.52 | convolution fusion | flops 3147520 | bytes 1114624 | tf_op jit(solution)/shard_map/bokjl,lz->bozkj/dot_general | solution.py:40
  252.2 7.5 %fusion.18 = f32[8,8,16,16]{3,1,2,0:T(8,128)S(1)} fusion(f32[8,8,16,16]{3,0,2,1:T(8,128)S(1)} %fusion.27, f32[1,2,8,16,16,16]{5,4,3,2,1,0:T(8,128)S(1)} %broadcast_multiply_fusion, s32[8]{0:T(128)S(1)} %iota_add_fusion), kind=kOutput, calls=%fused_computation.31 | convolution fusion | flops 3163904 | bytes 1638912 | tf_op jit(solution)/shard_map/bokjl,lz->bozkj/dot_general | solution.py:40
  259.9 7.5 %fusion.26 = f32[8,8,16,16]{3,0,2,1:T(8,128)S(1)} fusion(f32[1,2,8,16,16,16]{5,4,3,2,1,0:T(8,128)S(1)} %broadcast_multiply_fusion, s32[8]{0:T(128)S(1)} %iota_add_fusion), kind=kOutput, calls=%fused_computation.51 | convolution fusion | flops 3147520 | bytes 1114624 | tf_op jit(solution)/shard_map/bokjl,lz->bozkj/dot_general | solution.py:40
  267.4 7.7 %fusion.19 = f32[8,8,16,16]{3,1,2,0:T(8,128)S(1)} fusion(f32[8,8,16,16]{3,0,2,1:T(8,128)S(1)} %fusion.26, f32[1,2,8,16,16,16]{5,4,3,2,1,0:T(8,128)S(1)} %broadcast_multiply_fusion, s32[8]{0:T(128)S(1)} %iota_add_fusion), kind=kOutput, calls=%fused_computation.33 | convolution fusion | flops 3163904 | bytes 1638912 | tf_op jit(solution)/shard_map/bokjl,lz->bozkj/dot_general | solution.py:40
  275.3 0.7 fusion.47
  276.0 0.7 fusion.51
  276.7 0.7 fusion.20
  277.4 0.7 fusion.21
  278.1 8.2 %fusion.49 = f32[8,8,128,128]{3,2,1,0:T(8,128)} fusion(f32[8,8,128,16]{2,3,1,0:T(8,128)S(1)} %fusion.21, s32[16]{0:T(128)S(1)} %compare_select_fusion), kind=kOutput, calls=%fused_computation.84 | convolution fusion | flops 201355264 | bytes 4718656 | tf_op jit(solution)/shard_map/bozxj,jy->bozxy/dot_general | solution.py:40
  286.4 18.9 %fusion.14 = bf16[1,8,8,128,128]{4,3,2,1,0:T(8,128)(2,1)} fusion(f32[8]{0:T(128)S(1)} %dynamic_slice.3, f32[1,8,8,16,8,128]{5,4,2,1,3,0:T(8,128)} %bitcast.74, f32[8,8,128,128]{3,2,1,0:T(8,128)} %fusion.49, f32[8,8,128,16]{2,3,1,0:T(8,128)S(1)} %fusion.20, s32[16]{0:T(128)S(1)} %compare_select_fusion), kind=kOutput, calls=%fused_computation.26 | convolution fusion | flops 273707008 | bytes 11010144 | tf_op jit(solution)/shard_map/bozxj,jy->bozxy/dot_general | solution.py:40
  (22 shorter events, 2.6 us)
Async XLA Ops:
  6.5 65.3 %copy-start = (bf16[128,128]{1,0:T(8,128)(2,1)S(1)}, bf16[128,128]{1,0:T(8,128)(2,1)}, u32[]{:S(2)}) copy-start(bf16[128,128]{1,0:T(8,128)(2,1)} %param.5) | copy-start | bytes 98308
  81.7 6.7 %copy-start.1 = (bf16[1,8,8,128,128]{4,3,2,1,0:T(8,128)(2,1)S(1)}, bf16[1,8,8,128,128]{4,3,2,1,0:T(8,128)(2,1)}, u32[]{:S(2)}) copy-start(bf16[1,8,8,128,128]{4,3,2,1,0:T(8,128)(2,1)} %param.4) | copy-start | bytes 6291460
  81.7 204.6 %all-to-all-start.1 = ((f32[1,128,8,8,128]{4,3,2,0,1:T(8,128)}), f32[1,128,8,8,128]{4,3,2,0,1:T(8,128)}, u32[]{:S(2)}, u32[]{:S(2)}) async-start(f32[1,128,8,8,128]{4,3,2,0,1:T(8,128)} %copy.50), calls=%async_computation.2 | async-start | bytes 8388608 | tf_op jit(solution)/shard_map/all_to_all | solution.py:103
  88.0 81.1 %reduce-scatter.2.cloned.1.call-start = ((), (), s32[]{:S(2)}) async-start(), calls=%async_computation.3 | async-start | bytes 278528 | tf_op jit(solution)/shard_map/reduce_scatter | solution.py:69
  95.4 5.9 %copy-start.2 = (f32[128]{0:T(128)S(1)}, f32[128]{0:T(128)}, u32[]{:S(2)}) copy-start(f32[128]{0:T(128)} %param.6) | copy-start | bytes 1540
Sparse Core Ops, SparseCore 0:
  101.4 67.6 reduce-scatter.1
where the time goes:
time: 317 us; the launch traced here: 312 us
  blocking collectives  130 us (41%)
  matrix products  75.3 us (24%)
  waiting for transfers between devices  67.8 us (21%)
  local copies, waits for them, and re-layouts  14.1 us (4%)
  between operations  14.1 us (4%)
  starting transfers between devices  6.49 us (2%)
  other arithmetic  4.57 us (1%)
    dot_general x18, matrix products, product(): return jnp.einsum(form, left, right, precision=PRECISE)  70.4 us
    reduce_scatter x1, waiting for transfers between devices, on_device(): lax.psum_scatter(partial_value, 'slab', scatter_dimension=3, tiled=True)  67.8 us
    all_to_all x1, blocking collectives, on_device(): lax.all_to_all(field, 'chan', split_axis=3, concat_axis=1, tiled=True)  60.4 us
    all_gather x1, blocking collectives, on_device(): piece = lax.all_gather(owned, 'chan', axis=2, tiled=True)  41.9 us
    all_gather x1, blocking collectives, on_device(): spectrum = lax.all_gather(mixed, 'slab', axis=3, tiled=True)  27.9 us
  transfers between devices with their start and end apart: 2, of which 1 were waited for; matrix products, arithmetic and copies ran while one was open for 19% of the time, Pallas kernels for 0%

commit v1 on v0

v1 whole, which is shorter than its diff:
```python
import math

import jax
import jax.numpy as jnp
from jax import lax
from jax.experimental import pallas as pl
from jax.experimental.pallas import tpu as pltpu
from jax.sharding import PartitionSpec as P

GRID = 128
KEEP = 16
BLOCKS = 16
PRECISE = lax.Precision.HIGHEST
SCALE = 2.0**20


def mode_freqs(count, length):
    index = jnp.arange(count, dtype=jnp.int32)
    return jnp.where(index < count // 2, index, index + (length - count))


def phase_table(freqs, positions, length):
    product_int = freqs[:, None] * positions[None, :] % length
    return 2.0 * math.pi * product_int.astype(jnp.float32) / length


def build_tables(zcells):
    xfreq = mode_freqs(KEEP, GRID)
    zfreq = jnp.arange(KEEP, dtype=jnp.int32)
    cells = jnp.arange(GRID, dtype=jnp.int32)
    angle_x = phase_table(xfreq, cells, GRID)
    angle_z = phase_table(zfreq, zcells, GRID)
    cos_x, sin_x = (jnp.cos(angle_x), jnp.sin(angle_x))
    cos_z, sin_z = (jnp.cos(angle_z), jnp.sin(angle_z))
    fold_factor = jnp.where(zfreq == 0, 1.0, 2.0).astype(jnp.float32)
    return (cos_x, sin_x, cos_z, sin_z, fold_factor)


def product(form, left, right):
    return jnp.einsum(form, left, right, precision=PRECISE)


def exact_dot(left, right):
    return jnp.dot(left, right, precision=PRECISE, preferred_element_type=jnp.float32)


def slab_perm(dx, dy, dc):
    pairs = []
    for a in range(2):
        for b in range(4):
            for c in range(2):
                pairs.append(((a * 4 + b) * 2 + c, ((a ^ dx) * 4 + (b ^ dy)) * 2 + (c ^ dc)))
    return pairs


def halve(value, axis, bit, perm):
    own = lax.dynamic_index_in_dim(value, bit, axis, keepdims=False)
    other = lax.dynamic_index_in_dim(value, 1 - bit, axis, keepdims=False)
    return own + lax.ppermute(other, "slab", perm)


def slab_sum(partial):
    me = lax.axis_index("slab")
    rest = partial.shape[1:]
    value = partial.reshape(2, 2, 2, 2, *rest)
    value = halve(value, 3, me % 2, slab_perm(0, 0, 1))
    value = halve(value, 1, me // 4 % 2, slab_perm(0, 2, 0))
    value = halve(value, 1, me // 2 % 2, slab_perm(0, 1, 0))
    return halve(value, 0, me // 8, slab_perm(1, 0, 0))


def map_kernel(weight_ref, cells_ref, out_ref, hold_ref):
    rows = cells_ref.shape[1]
    for x in range(rows):
        block = cells_ref[:, x].reshape(128, 128)
        mapped = jnp.dot(weight_ref[...], block, preferred_element_type=jnp.float32) * SCALE
        square = mapped * mapped
        hold_ref[:, x, :] = mapped * jnp.abs(mapped) * square
    out_ref[...] = hold_ref[...].reshape(out_ref.shape).astype(jnp.bfloat16)


def pointwise_map(weight, cells):
    rows = 16
    return pl.pallas_call(
        map_kernel,
        out_shape=jax.ShapeDtypeStruct((BLOCKS, 8, 64, 128), jnp.bfloat16),
        grid=(64 // rows,),
        in_specs=[
            pl.BlockSpec((128, 128), lambda i: (0, 0)),
            pl.BlockSpec((BLOCKS, rows, 8, 128), lambda i: (0, i, 0, 0)),
        ],
        out_specs=pl.BlockSpec((BLOCKS, 8, rows, 128), lambda i: (0, 0, i, 0)),
        scratch_shapes=[pltpu.VMEM((128, rows, 128), jnp.float32)],
        name="pointwise_map",
    )(weight, cells)


def inverse_kernel(spec_ref, table_z_ref, table_x_ref, table_y_ref, out_ref, plane_ref, line_ref):
    real = exact_dot(spec_ref[:, 0].reshape(128, 256), table_z_ref[...])
    imag = exact_dot(spec_ref[:, 1].reshape(128, 256), table_z_ref[...])
    plane_ref[:16] = (real[:, :128] - imag[:, 128:]).reshape(16, 8, 128)
    plane_ref[16:] = (imag[:, :128] + real[:, 128:]).reshape(16, 8, 128)
    for o in range(8):
        line = exact_dot(table_x_ref[...], plane_ref[:, o, :])
        line_ref[pl.ds(o * 128, 128), :128] = line[:128]
        line_ref[pl.ds(o * 128, 128), 128:] = line[128:]
    for z in range(0, 8, 2):
        field = exact_dot(line_ref[...], table_y_ref[:, z * 128 : (z + 2) * 128])
        out_ref[:, z] = field[:, :128].reshape(8, 128, 128)
        out_ref[:, z + 1] = field[:, 128:].reshape(8, 128, 128)


def inverse_transform(spectrum, cos_x, sin_x, cos_z, sin_z, fold_factor):
    eye_k = jnp.eye(KEEP, dtype=jnp.float32)
    eye_z = jnp.eye(8, dtype=jnp.float32)
    weight = fold_factor / GRID**3
    waves_z = jnp.stack([cos_z, sin_z], 0) * weight[None, :, None]
    table_z = (eye_k[:, None, None, None, :] * waves_z.transpose(1, 0, 2)[None, :, :, :, None]).reshape(256, 256)
    table_x = jnp.concatenate(
        [
            jnp.concatenate([cos_x.T, -sin_x.T], 1),
            jnp.concatenate([sin_x.T, cos_x.T], 1),
        ],
        0,
    )
    waves_y = jnp.stack([cos_x, -sin_x], 0)
    table_y = (eye_z[None, :, None, :, None] * waves_y[:, None, :, None, :]).reshape(256, 1024)
    return pl.pallas_call(
        inverse_kernel,
        out_shape=jax.ShapeDtypeStruct((8, 8, 128, 128), jnp.float32),
        scratch_shapes=[pltpu.VMEM((32, 8, 128), jnp.float32), pltpu.VMEM((1024, 256), jnp.float32)],
        name="inverse_transform",
    )(spectrum, table_z, table_x, table_y)


def finish_kernel(bias_ref, coded_ref, inverse_ref, out_ref):
    coded = coded_ref[0].astype(jnp.float32)
    size = lax.rsqrt(lax.rsqrt(jnp.abs(coded))) * (1.0 / SCALE)
    local = jnp.where(coded < 0, -size, size)
    for o in range(8):
        total = local[o] + inverse_ref[o, 0] + bias_ref[o]
        active = 0.5 * total * (1.0 + lax.erf(total * math.sqrt(0.5)))
        out_ref[o, 0] = active.astype(jnp.bfloat16)


def finish(bias, coded, inverse):
    return pl.pallas_call(
        finish_kernel,
        out_shape=jax.ShapeDtypeStruct((8, 8, 128, 128), jnp.bfloat16),
        grid=(BLOCKS,),
        in_specs=[
            pl.BlockSpec(memory_space=pltpu.SMEM),
            pl.BlockSpec((1, 8, 64, 128), lambda p: (p, 0, 0, 0)),
            pl.BlockSpec((8, 1, 64, 128), lambda p: (0, p // 2, p % 2, 0)),
        ],
        out_specs=pl.BlockSpec((8, 1, 64, 128), lambda p: (0, p // 2, p % 2, 0)),
        name="finish",
    )(bias, coded, inverse)


def forward_transform(field, cos_x, sin_x, cos_z, sin_z):
    table_x = jnp.concatenate([cos_x, -sin_x], 0).astype(jnp.bfloat16)
    section_x = jnp.einsum("kx,czxy->czky", table_x, field, preferred_element_type=jnp.float32)
    part_real = section_x[:, :, :KEEP]
    part_imag = section_x[:, :, KEEP:]
    wave_real = product("czky,jy->czkj", part_real, cos_x) + product("czky,jy->czkj", part_imag, sin_x)
    wave_imag = product("czky,jy->czkj", part_imag, cos_x) - product("czky,jy->czkj", part_real, sin_x)
    four_real = product("czkj,lz->kcjl", wave_real, cos_z) + product("czkj,lz->kcjl", wave_imag, sin_z)
    four_imag = product("czkj,lz->kcjl", wave_imag, cos_z) - product("czkj,lz->kcjl", wave_real, sin_z)
    return jnp.stack([four_real.reshape(KEEP, 8, 256), four_imag.reshape(KEEP, 8, 256)], 1)


def mix(coef, spec_weight):
    real = coef[:, 0].reshape(128, 256)
    imag = coef[:, 1].reshape(128, 256)
    weight_real, weight_imag = spec_weight[0], spec_weight[1]
    mixed_real = jnp.sum(real * weight_real - imag * weight_imag, 1)
    mixed_imag = jnp.sum(real * weight_imag + imag * weight_real, 1)
    return jnp.stack([mixed_real, mixed_imag], 0)


def on_device(field, local_weight, bias, spec_weight):
    chan_local, zdepth = (field.shape[1], field.shape[2])
    zcells = lax.axis_index("slab") * zdepth + jnp.arange(zdepth, dtype=jnp.int32)
    cos_x, sin_x, cos_z, sin_z, fold_factor = build_tables(zcells)
    planes = field[0]
    cells = planes.transpose(1, 2, 0, 3).reshape(BLOCKS, 64, 8, 128)
    cells = lax.all_to_all(cells, "chan", 0, 0, tiled=True)
    partial = forward_transform(planes, cos_x, sin_x, cos_z, sin_z)
    owned = slab_sum(partial)
    spread = lax.optimization_barrier(jnp.broadcast_to(owned[None], (BLOCKS, 2, 8, 256)))
    coef = lax.all_to_all(spread, "chan", 0, 0, tiled=True)
    coded = pointwise_map(local_weight, cells)
    coded = lax.all_to_all(coded, "chan", 0, 0, tiled=True)
    mixed = mix(coef, spec_weight)
    spectrum = lax.all_gather(mixed, "slab", axis=0)
    inverse = inverse_transform(spectrum, cos_x, sin_x, cos_z, sin_z, fold_factor)
    offset = lax.dynamic_slice_in_dim(bias, lax.axis_index("chan") * chan_local, chan_local, 0)
    return finish(offset, coded, inverse)[None]


def solution(mesh):
    placed = (P(None, "chan", "slab", None, None), P(), P(), P(None, "chan", None, "slab"))
    return jax.shard_map(
        on_device,
        mesh=mesh,
        in_specs=placed,
        out_specs=P(None, "chan", "slab", None, None),
        check_vma=False,
    )
```

time: 317 us -> 151 us (0.48)
  blocking collectives: 130 us -> 23.3 us
  matrix products: 75.3 us -> 7.8 us
  Pallas kernels: 0 us -> 25.4 us
  starting transfers between devices: 6.49 us -> 30.3 us
  waiting for transfers between devices: 67.8 us -> 47.8 us
  between operations: 14.1 us -> 0.3 us
  local copies, waits for them, and re-layouts: 14.1 us -> 10.8 us
    reduce_scatter x1 -> x0, waiting for transfers between devices: 67.8 us -> none  [on_device(): lax.psum_scatter(partial_value, 'slab', scatter_dimension=3, tiled=True)]
    dot_general x18 -> x8, matrix products: 70.4 us -> 7.39 us  [product(): return jnp.einsum(form, left, right, precision=PRECISE)]
    all_to_all x1 -> x0, blocking collectives: 60.4 us -> none  [on_device(): lax.all_to_all(field, 'chan', split_axis=3, concat_axis=1, tiled=True)]
    all_gather x2 -> x1, blocking collectives: 69.8 us -> 23.3 us  [on_device(): spectrum = lax.all_gather(mixed, 'slab', axis=0)]
    all_to_all x1 -> x3, waiting for transfers between devices: 0.01 us -> 40.1 us  [the longest x1 25.1 us: on_device(): cells = lax.all_to_all(cells, 'chan', 0, 0, tiled=True)]
    pallas_call x0 -> x3, Pallas kernels: none -> 25.4 us  [the longest x1 11.4 us: finish(): pl.pallas_call(finish_kernel, out_shape=jax.ShapeDtypeStruct((8, 8, 128,...]
    all_to_all x1 -> x3, starting transfers between devices: 6.28 us -> 24.3 us  [the longest x1 11.8 us: on_device(): cells = lax.all_to_all(cells, 'chan', 0, 0, tiled=True)]
    ppermute x0 -> x4, waiting for transfers between devices: none -> 7.68 us  [halve(): return own + lax.ppermute(other, 'slab', perm)]
  transfers between devices with their start and end apart: 2 -> 7, of which waited for: 1 -> 7; matrix products, arithmetic and copies ran while one was open for 19% -> 12% of each run, Pallas kernels for 0% -> 9%
where the time goes in v1:
time: 151 us; the launch traced here: 149 us
  waiting for transfers between devices  47.8 us (32%)
  starting transfers between devices  30.3 us (20%)
  Pallas kernels  25.4 us (17%)
  blocking collectives  23.3 us (15%)
  local copies, waits for them, and re-layouts  10.8 us (7%)
  matrix products  7.8 us (5%)
  other arithmetic  2.85 us (2%)
    all_to_all x1, waiting for transfers between devices, on_device(): cells = lax.all_to_all(cells, 'chan', 0, 0, tiled=True)  25.1 us
    all_gather x1, blocking collectives, on_device(): spectrum = lax.all_gather(mixed, 'slab', axis=0)  23.3 us
    all_to_all x1, starting transfers between devices, on_device(): cells = lax.all_to_all(cells, 'chan', 0, 0, tiled=True)  11.8 us
    pallas_call x1, Pallas kernels, finish(): pl.pallas_call(finish_kernel, out_shape=jax.ShapeDtypeStruct((8, 8, 128,...  11.4 us
    all_to_all x1, waiting for transfers between devices, on_device(): coded = lax.all_to_all(coded, 'chan', 0, 0, tiled=True)  10.6 us
    pallas_call x1, Pallas kernels, inverse_transform(): pl.pallas_call(inverse_kernel, out_shape=jax.ShapeDtypeStruct((8, 8, 128,...  8.05 us
    ppermute x4, waiting for transfers between devices, halve(): return own + lax.ppermute(other, 'slab', perm)  7.68 us
    dot_general x8, matrix products, product(): return jnp.einsum(form, left, right, precision=PRECISE)  7.39 us
  transfers between devices with their start and end apart: 7, of which 7 were waited for; matrix products, arithmetic and copies ran while one was open for 12% of the time, Pallas kernels for 9%

profile of v1, /device:TPU:1, one launch (start us, length us, event | category | flops | bytes accessed | tf_op | source)
XLA Modules:
  0.0 148.5 jit_solution(13126775803099133983)
XLA Ops:
  0.0 4.3 %copy.35 = bf16[8,128,8,128]{3,2,1,0:T(8,128)(2,1)} copy(bf16[8,128,8,128]{3,1,0,2:T(8,128)(2,1)} %bitcast.103) | data formatting | bytes 4194304 | tf_op jit(solution)/shard_map/transpose | solution.py:187
  4.3 11.8 %all-to-all-start = ((bf16[16,64,8,128]{3,2,1,0:T(8,128)(2,1)}), bf16[16,64,8,128]{3,2,1,0:T(8,128)(2,1)}, u32[]{:S(2)}, u32[]{:S(2)}) async-start(bf16[16,64,8,128]{3,2,1,0:T(8,128)(2,1)} %bitcast.104), calls=%async_computation | async-start | bytes 4194304 | tf_op jit(solution)/shard_map/all_to_all | solution.py:188
  16.6 0.7 fusion.11
  17.3 0.7 fusion.15
  18.0 0.7 convolution_subtract_fusion.1
  18.7 0.7 convolution_add_fusion.1
  19.4 1.2 fusion.21
  20.5 1.2 fusion.6
  22.5 1.2 fusion.17
  23.7 1.2 fusion.5
  25.7 1.0 collective-permute-start
  26.8 1.0 collective-permute-done
  27.8 3.0 %collective-permute-start.1 = (f32[2,2,2,8,256]{4,3,2,0,1:T(8,128)S(1)}, f32[2,2,2,8,256]{4,3,2,0,1:T(8,128)S(1)}, u32[]{:S(2)}, u32[]{:S(2)}) collective-permute-start(f32[2,2,2,8,256]{4,3,2,0,1:T(8,128)S(1)} %bitcast.108), channel_id=1, source_target_pairs={{0,64},{16,80},{32,96},{48,112},{64,0},{80,16},{96,32},{112,48},{1... | collective-permute-start | bytes 196616 | tf_op jit(solution)/shard_map/ppermute | solution.py:59
  30.8 2.1 %collective-permute-done.1 = f32[2,2,2,8,256]{4,3,2,0,1:T(8,128)S(1)} collective-permute-done((f32[2,2,2,8,256]{4,3,2,0,1:T(8,128)S(1)}, f32[2,2,2,8,256]{4,3,2,0,1:T(8,128)S(1)}, u32[]{:S(2)}, u32[]{:S(2)}) %collective-permute-start.1) | collective-permute-done | bytes 65568 | tf_op jit(solution)/shard_map/ppermute | solution.py:59
  32.9 1.4 collective-permute-start.2
  34.3 1.9 %collective-permute-done.2 = f32[2,2,8,256]{3,2,1,0:T(8,128)S(1)} collective-permute-done((f32[2,2,8,256]{3,2,1,0:T(8,128)S(1)}, f32[2,2,8,256]{3,2,1,0:T(8,128)S(1)}, u32[]{:S(2)}, u32[]{:S(2)}) %collective-permute-start.2) | collective-permute-done | bytes 32800 | tf_op jit(solution)/shard_map/ppermute | solution.py:59
  36.8 2.7 %collective-permute-done.3 = f32[2,8,256]{2,1,0:T(8,128)S(1)} collective-permute-done((f32[2,8,256]{2,1,0:T(8,128)S(1)}, f32[2,8,256]{2,1,0:T(8,128)S(1)}, u32[]{:S(2)}, u32[]{:S(2)}) %collective-permute-start.3) | collective-permute-done | bytes 16416 | tf_op jit(solution)/shard_map/ppermute | solution.py:59
  39.5 0.7 broadcast_in_dim.12
  40.2 25.1 %all-to-all-done.cells_ref = bf16[16,64,8,128]{3,2,1,0:T(8,128)(2,1)} async-done(((bf16[16,64,8,128]{3,2,1,0:T(8,128)(2,1)}), bf16[16,64,8,128]{3,2,1,0:T(8,128)(2,1)}, u32[]{:S(2)}, u32[]{:S(2)}) %all-to-all-start) | async-done | bytes 2097184 | tf_op jit(solution)/shard_map/all_to_all | solution.py:188
  65.4 7.0 %all-to-all-start.2 = ((f32[16,2,8,256]{3,2,1,0:T(8,128)}), f32[16,2,8,256]{3,2,1,0:T(8,128)S(1)}, u32[]{:S(2)}, u32[]{:S(2)}) async-start(f32[16,2,8,256]{3,2,1,0:T(8,128)} %broadcast_in_dim.12), calls=%async_computation.2 | async-start | bytes 524288 | tf_op jit(solution)/shard_map/all_to_all | solution.py:192
  72.4 5.9 %pointwise_map.1 = bf16[16,8,64,128]{3,2,1,0:T(8,128)(2,1)} custom-call(bf16[128,128]{1,0:T(8,128)(2,1)} %weight_ref.1, bf16[16,64,8,128]{3,2,1,0:T(8,128)(2,1)} %all-to-all-done.cells_ref), custom_call_target="tpu_custom_call" | custom-call | tf_op jit(solution)/shard_map/pointwise_map/pallas_call | solution.py:84
  78.3 4.3 %all-to-all-done.2 = f32[16,2,8,256]{3,2,1,0:T(8,128)S(1)} async-done(((f32[16,2,8,256]{3,2,1,0:T(8,128)}), f32[16,2,8,256]{3,2,1,0:T(8,128)S(1)}, u32[]{:S(2)}, u32[]{:S(2)}) %all-to-all-start.2) | async-done | bytes 262176 | tf_op jit(solution)/shard_map/all_to_all | solution.py:192
  82.7 5.5 %all-to-all-start.1 = ((bf16[16,8,64,128]{3,2,1,0:T(8,128)(2,1)}), bf16[16,8,64,128]{3,2,1,0:T(8,128)(2,1)}, u32[]{:S(2)}, u32[]{:S(2)}) async-start(bf16[16,8,64,128]{3,2,1,0:T(8,128)(2,1)} %pointwise_map.1), calls=%async_computation.1 | async-start | bytes 4194304 | tf_op jit(solution)/shard_map/all_to_all | solution.py:194
  88.6 0.8 copy.45.table_x_ref
  89.7 1.2 copy.63
  91.1 1.5 %mul.230.table_z_ref = f32[256,256]{1,0:T(8,128)} reshape(f32[16,16,2,8,16]{4,3,2,1,0:T(8,128)S(1)} %broadcast_multiply_fusion) | data formatting | bytes 524288 | tf_op jit(solution)/shard_map/mul | solution.py:118
  92.7 0.6 dynamic_slice.31.bias_ref
  93.3 1.8 %fusion.8 = (f32[8,256]{1,0:T(8,128)S(1)}, f32[8,256]{1,0:T(8,128)S(1)}) fusion(f32[2,8,128,256]{3,2,1,0:T(8,128)} %param.7, f32[128,256]{1,0:T(8,128)S(1)} %get-tuple-element.8, f32[128,256]{1,0:T(8,128)S(1)} %get-tuple-element.7), kind=kLoop, calls=%fused_computation.13 | loop fusion | flops 2093056 | bytes 2375680 | tf_op jit(solution)/shard_map/reduce_sum | solution.py:177
  95.1 23.3 %all-gather = f32[32,8,256]{2,1,0:T(8,128)} all-gather(f32[2,8,256]{2,1,0:T(8,128)S(1)} %pad_maximum_fusion), channel_id=2, replica_groups=mesh['slab'=16,'chan'=16] {'slab'}, dimensions={0}, use_global_device_ids=true | all-gather | bytes 278528 | tf_op jit(solution)/shard_map/all_gather | solution.py:196
  118.5 8.1 %inverse_transform.1.inverse_ref = f32[8,8,128,128]{3,2,1,0:T(8,128)} custom-call(f32[16,2,8,256]{3,2,1,0:T(8,128)} %bitcast.107, f32[256,256]{1,0:T(8,128)} %mul.230.table_z_ref, f32[256,32]{1,0:T(8,128)} %copy.45.table_x_ref, f32[256,1024]{1,0:T(8,128)} %bitcast.106), custom_call_target="tpu_custom_call" | custom-call | tf_op jit(solution)/shard_map/inverse_transform/pallas_call | solution.py:128
  126.5 10.6 %all-to-all-done.1.coded_ref = bf16[16,8,64,128]{3,2,1,0:T(8,128)(2,1)} async-done(((bf16[16,8,64,128]{3,2,1,0:T(8,128)(2,1)}), bf16[16,8,64,128]{3,2,1,0:T(8,128)(2,1)}, u32[]{:S(2)}, u32[]{:S(2)}) %all-to-all-start.1) | async-done | bytes 2097184 | tf_op jit(solution)/shard_map/all_to_all | solution.py:194
  137.2 11.4 %finish.1 = bf16[8,8,128,128]{3,2,1,0:T(8,128)(2,1)} custom-call(f32[8]{0:T(128)} %dynamic_slice.31.bias_ref, bf16[16,8,64,128]{3,2,1,0:T(8,128)(2,1)} %all-to-all-done.1.coded_ref, f32[8,8,128,128]{3,2,1,0:T(8,128)} %inverse_transform.1.inverse_ref), custom_call_target="tpu_custom_call" | custom-call | tf_op jit(solution)/shard_map/finish/pallas_call | solution.py:147
  (38 shorter events, 3.7 us)
Async XLA Ops:
  4.3 11.9 %copy-start = (bf16[1,8,8,128,128]{4,3,2,1,0:T(8,128)(2,1)S(1)}, bf16[1,8,8,128,128]{4,3,2,1,0:T(8,128)(2,1)}, u32[]{:S(2)}) copy-start(bf16[1,8,8,128,128]{4,3,2,1,0:T(8,128)(2,1)} %param.4) | copy-start | bytes 6291460
  4.3 61.1 %all-to-all-start = ((bf16[16,64,8,128]{3,2,1,0:T(8,128)(2,1)}), bf16[16,64,8,128]{3,2,1,0:T(8,128)(2,1)}, u32[]{:S(2)}, u32[]{:S(2)}) async-start(bf16[16,64,8,128]{3,2,1,0:T(8,128)(2,1)} %bitcast.104), calls=%async_computation | async-start | bytes 4194304 | tf_op jit(solution)/shard_map/all_to_all | solution.py:188
  25.7 2.0 %collective-permute-start = (f32[2,2,2,2,8,256]{5,4,2,1,0,3:T(8,128)S(1)}, f32[2,2,2,2,8,256]{5,4,2,1,0,3:T(8,128)S(1)}, u32[]{:S(2)}, u32[]{:S(2)}) collective-permute-start(f32[2,2,2,2,8,256]{5,4,2,1,0,3:T(8,128)S(1)} %dynamic-slice_bitcast_fusion), channel_id=1, source_target_pairs={{0,16},{16,0},{32,48},{48,32},{64,80},{80,64},{96,112},{112,96},{1... | collective-permute-start | bytes 393224 | tf_op jit(solution)/shard_map/ppermute | solution.py:59
  27.8 5.1 %collective-permute-start.1 = (f32[2,2,2,8,256]{4,3,2,0,1:T(8,128)S(1)}, f32[2,2,2,8,256]{4,3,2,0,1:T(8,128)S(1)}, u32[]{:S(2)}, u32[]{:S(2)}) collective-permute-start(f32[2,2,2,8,256]{4,3,2,0,1:T(8,128)S(1)} %bitcast.108), channel_id=1, source_target_pairs={{0,64},{16,80},{32,96},{48,112},{64,0},{80,16},{96,32},{112,48},{1... | collective-permute-start | bytes 196616 | tf_op jit(solution)/shard_map/ppermute | solution.py:59
  32.9 3.3 %collective-permute-start.2 = (f32[2,2,8,256]{3,2,1,0:T(8,128)S(1)}, f32[2,2,8,256]{3,2,1,0:T(8,128)S(1)}, u32[]{:S(2)}, u32[]{:S(2)}) collective-permute-start(f32[2,2,8,256]{3,2,1,0:T(8,128)S(1)} %dynamic-slice_bitcast_fusion.1), channel_id=1, source_target_pairs={{0,32},{16,48},{32,0},{48,16},{64,96},{80,112},{96,64},{112,80},{1... | collective-permute-start | bytes 98312 | tf_op jit(solution)/shard_map/ppermute | solution.py:59
  36.2 3.3 %collective-permute-start.3 = (f32[2,8,256]{2,1,0:T(8,128)S(1)}, f32[2,8,256]{2,1,0:T(8,128)S(1)}, u32[]{:S(2)}, u32[]{:S(2)}) collective-permute-start(f32[2,8,256]{2,1,0:T(8,128)S(1)} %dynamic-slice_bitcast_fusion.2), channel_id=1, source_target_pairs={{0,128},{16,144},{32,160},{48,176},{64,192},{80,208},{96,224},{112... | collective-permute-start | bytes 49160 | tf_op jit(solution)/shard_map/ppermute | solution.py:59
  65.4 17.3 %all-to-all-start.2 = ((f32[16,2,8,256]{3,2,1,0:T(8,128)}), f32[16,2,8,256]{3,2,1,0:T(8,128)S(1)}, u32[]{:S(2)}, u32[]{:S(2)}) async-start(f32[16,2,8,256]{3,2,1,0:T(8,128)} %broadcast_in_dim.12), calls=%async_computation.2 | async-start | bytes 524288 | tf_op jit(solution)/shard_map/all_to_all | solution.py:192
  82.7 54.5 %all-to-all-start.1 = ((bf16[16,8,64,128]{3,2,1,0:T(8,128)(2,1)}), bf16[16,8,64,128]{3,2,1,0:T(8,128)(2,1)}, u32[]{:S(2)}, u32[]{:S(2)}) async-start(bf16[16,8,64,128]{3,2,1,0:T(8,128)(2,1)} %pointwise_map.1), calls=%async_computation.1 | async-start | bytes 4194304 | tf_op jit(solution)/shard_map/all_to_all | solution.py:194
  90.9 1.8 %copy-start.1 = (f32[128]{0:T(128)S(1)}, f32[128]{0:T(128)}, u32[]{:S(2)}) copy-start(f32[128]{0:T(128)} %param.6) | copy-start | bytes 1540

commit v2 on v1

--- a/solution.py
+++ b/solution.py
@@ -7,11 +7,23 @@
 from jax.experimental.pallas import tpu as pltpu
 from jax.sharding import PartitionSpec as P
 
+
 GRID = 128
 KEEP = 16
 BLOCKS = 16
 PRECISE = lax.Precision.HIGHEST
 SCALE = 2.0**20
+TAIL = (
+    -0.9999999035727548,
+    -1.1511097265121628,
+    -0.4591722285969747,
+    -0.05260302599382617,
+    0.007216363464760431,
+    -0.0002534202677215224,
+    -0.0001380938713349715,
+    2.9273017695886588e-05,
+    -1.9919727297239597e-06,
+)
 
 
 def mode_freqs(count, length):
@@ -69,14 +81,16 @@
     return halve(value, 0, me // 8, slab_perm(1, 0, 0))
 
 
-def map_kernel(weight_ref, cells_ref, out_ref, hold_ref):
+def map_kernel(weight_ref, cells_ref, out_ref):
     rows = cells_ref.shape[1]
-    for x in range(rows):
-        block = cells_ref[:, x].reshape(128, 128)
-        mapped = jnp.dot(weight_ref[...], block, preferred_element_type=jnp.float32) * SCALE
-        square = mapped * mapped
-        hold_ref[:, x, :] = mapped * jnp.abs(mapped) * square
-    out_ref[...] = hold_ref[...].reshape(out_ref.shape).astype(jnp.bfloat16)
+    for first in range(0, rows, 8):
+        coded = []
+        for x in range(first, first + 8):
+            block = cells_ref[:, x].reshape(128, 128)
+            mapped = jnp.dot(weight_ref[...], block, preferred_element_type=jnp.float32) * SCALE
+            coded.append(mapped * jnp.abs(mapped) * (mapped * mapped))
+        turned = jnp.stack(coded, 0).transpose(1, 0, 2)
+        out_ref[:, :, pl.ds(first, 8), :] = turned.reshape(BLOCKS, 8, 8, 128).astype(jnp.bfloat16)
 
 
 def pointwise_map(weight, cells):
@@ -90,7 +104,6 @@
             pl.BlockSpec((BLOCKS, rows, 8, 128), lambda i: (0, i, 0, 0)),
         ],
         out_specs=pl.BlockSpec((BLOCKS, 8, rows, 128), lambda i: (0, 0, i, 0)),
-        scratch_shapes=[pltpu.VMEM((128, rows, 128), jnp.float32)],
         name="pointwise_map",
     )(weight, cells)
 
@@ -134,26 +147,35 @@
 
 
 def finish_kernel(bias_ref, coded_ref, inverse_ref, out_ref):
-    coded = coded_ref[0].astype(jnp.float32)
-    size = lax.rsqrt(lax.rsqrt(jnp.abs(coded))) * (1.0 / SCALE)
-    local = jnp.where(coded < 0, -size, size)
+    depth = inverse_ref.shape[1]
     for o in range(8):
-        total = local[o] + inverse_ref[o, 0] + bias_ref[o]
-        active = 0.5 * total * (1.0 + lax.erf(total * math.sqrt(0.5)))
-        out_ref[o, 0] = active.astype(jnp.bfloat16)
+        for z in range(depth):
+            for half in range(2):
+                coded = coded_ref[z * 2 + half, o].astype(jnp.float32)
+                size = lax.rsqrt(lax.rsqrt(jnp.abs(coded))) * (1.0 / SCALE)
+                local = jnp.where(coded < 0, -size, size)
+                rows = pl.ds(half * 64, 64)
+                total = local + (inverse_ref[o, z, rows, :] + bias_ref[o])
+                size = jnp.abs(total)
+                power = TAIL[-1]
+                for factor in TAIL[-2::-1]:
+                    power = power * size + factor
+                active = jnp.maximum(total, 0.0) - size * jnp.exp2(power)
+                out_ref[o, z, rows, :] = active.astype(jnp.bfloat16)
 
 
 def finish(bias, coded, inverse):
+    depth = 2
     return pl.pallas_call(
         finish_kernel,
         out_shape=jax.ShapeDtypeStruct((8, 8, 128, 128), jnp.bfloat16),
-        grid=(BLOCKS,),
+        grid=(8 // depth,),
         in_specs=[
             pl.BlockSpec(memory_space=pltpu.SMEM),
-            pl.BlockSpec((1, 8, 64, 128), lambda p: (p, 0, 0, 0)),
-            pl.BlockSpec((8, 1, 64, 128), lambda p: (0, p // 2, p % 2, 0)),
+            pl.BlockSpec((2 * depth, 8, 64, 128), lambda z: (z, 0, 0, 0)),
+            pl.BlockSpec((8, depth, 128, 128), lambda z: (0, z, 0, 0)),
         ],
-        out_specs=pl.BlockSpec((8, 1, 64, 128), lambda p: (0, p // 2, p % 2, 0)),
+        out_specs=pl.BlockSpec((8, depth, 128, 128), lambda z: (0, z, 0, 0)),
         name="finish",
     )(bias, coded, inverse)
 
@@ -170,13 +192,47 @@
     return jnp.stack([four_real.reshape(KEEP, 8, 256), four_imag.reshape(KEEP, 8, 256)], 1)
 
 
-def mix(coef, spec_weight):
-    real = coef[:, 0].reshape(128, 256)
-    imag = coef[:, 1].reshape(128, 256)
-    weight_real, weight_imag = spec_weight[0], spec_weight[1]
-    mixed_real = jnp.sum(real * weight_real - imag * weight_imag, 1)
-    mixed_imag = jnp.sum(real * weight_imag + imag * weight_real, 1)
-    return jnp.stack([mixed_real, mixed_imag], 0)
+def chan_perm(dx, dz):
+    return [(h * 8 + z, (h ^ dx) * 8 + (z + dz) % 8) for h in range(2) for z in range(8)]
+
+
+def coef_gather(owned):
+    other = lax.ppermute(owned, "chan", chan_perm(1, 0))
+    first = lax.axis_index("chan") < 8
+    pair = jnp.stack([jnp.where(first, owned, other), jnp.where(first, other, owned)], 0)
+    return [pair] + [lax.ppermute(pair, "chan", chan_perm(0, k)) for k in range(1, 8)]
+
+
+def mix_kernel(place_ref, *refs):
+    coefs, weight_ref, out_ref = refs[:8], refs[8], refs[9]
+    zpos = place_ref[0]
+    for o in range(8):
+        real = jnp.zeros((8, 256), jnp.float32)
+        imag = jnp.zeros((8, 256), jnp.float32)
+        for k in range(8):
+            source = lax.rem(zpos + (8 - k), 8)
+            for h in range(2):
+                rows = pl.ds(pl.multiple_of(h * 64 + source * 8, 8), 8)
+                weight_real = weight_ref[0, o, rows, :]
+                weight_imag = weight_ref[1, o, rows, :]
+                coef_real = coefs[k][h, 0]
+                coef_imag = coefs[k][h, 1]
+                real += coef_real * weight_real - coef_imag * weight_imag
+                imag += coef_real * weight_imag + coef_imag * weight_real
+        out_ref[0, pl.ds(o, 1), :] = jnp.sum(real, 0, keepdims=True)
+        out_ref[1, pl.ds(o, 1), :] = jnp.sum(imag, 0, keepdims=True)
+
+
+def mix(coefs, spec_weight):
+    place = jnp.reshape(lax.axis_index("chan") % 8, (1,)).astype(jnp.int32)
+    whole = pl.BlockSpec(memory_space=pltpu.VMEM)
+    return pl.pallas_call(
+        mix_kernel,
+        out_shape=jax.ShapeDtypeStruct((2, 8, 256), jnp.float32),
+        in_specs=[pl.BlockSpec(memory_space=pltpu.SMEM)] + [whole] * 9,
+        out_specs=whole,
+        name="mix",
+    )(place, *coefs, spec_weight)
 
 
 def on_device(field, local_weight, bias, spec_weight):
@@ -188,8 +244,7 @@
     cells = lax.all_to_all(cells, "chan", 0, 0, tiled=True)
     partial = forward_transform(planes, cos_x, sin_x, cos_z, sin_z)
     owned = slab_sum(partial)
-    spread = lax.optimization_barrier(jnp.broadcast_to(owned[None], (BLOCKS, 2, 8, 256)))
-    coef = lax.all_to_all(spread, "chan", 0, 0, tiled=True)
+    coef = coef_gather(owned)
     coded = pointwise_map(local_weight, cells)
     coded = lax.all_to_all(coded, "chan", 0, 0, tiled=True)
     mixed = mix(coef, spec_weight)

time: 151 us -> 177 us (1.17)
  waiting for transfers between devices: 47.8 us -> 66.2 us
  starting transfers between devices: 30.3 us -> 43.2 us
  Pallas kernels: 25.4 us -> 22.8 us
  other arithmetic: 2.85 us -> 1.01 us
    ppermute x0 -> x8, waiting for transfers between devices: none -> 19.4 us  [the longest x7 18.2 us: coef_gather(): lax.ppermute(pair, 'chan', chan_perm(0, k))]
    ppermute x0 -> x8, starting transfers between devices: none -> 18.6 us  [the longest x7 15.4 us: coef_gather(): lax.ppermute(pair, 'chan', chan_perm(0, k))]
    all_to_all x1, waiting for transfers between devices: 25.1 us -> 39.7 us  [on_device(): cells = lax.all_to_all(cells, 'chan', 0, 0, tiled=True)]
    all_to_all x1, waiting for transfers between devices: 10.6 us -> 0.01 us  [on_device(): coded = lax.all_to_all(coded, 'chan', 0, 0, tiled=True)]
    all_to_all x1 -> x0, starting transfers between devices: 7.01 us -> none  [on_device(): coef = lax.all_to_all(spread, 'chan', 0, 0, tiled=True)]
    all_to_all x1 -> x0, waiting for transfers between devices: 4.34 us -> none  [on_device(): coef = lax.all_to_all(spread, 'chan', 0, 0, tiled=True)]
    pallas_call x1, Pallas kernels: 11.4 us -> 7.2 us  [finish(): pl.pallas_call(finish_kernel, out_shape=jax.ShapeDtypeStruct((8, 8, 128,...]
    pallas_call x0 -> x1, Pallas kernels: none -> 2.73 us  [mix(): pl.pallas_call(mix_kernel, out_shape=jax.ShapeDtypeStruct((2, 8, 256), jn...]
  transfers between devices with their start and end apart: 7 -> 14, of which waited for: 7 -> 8; matrix products, arithmetic and copies ran while one was open for 12% -> 8% of each run, Pallas kernels for 9% -> 6%
where the time goes in v2:
time: 177 us; the launch traced here: 176 us
  waiting for transfers between devices  66.2 us (37%)
  starting transfers between devices  43.2 us (24%)
  blocking collectives  24.1 us (14%)
  Pallas kernels  22.8 us (13%)
  local copies, waits for them, and re-layouts  10.7 us (6%)
  matrix products  7.76 us (4%)
    all_to_all x1, waiting for transfers between devices, on_device(): cells = lax.all_to_all(cells, 'chan', 0, 0, tiled=True)  39.7 us
    all_gather x1, blocking collectives, on_device(): spectrum = lax.all_gather(mixed, 'slab', axis=0)  24.1 us
    ppermute x7, waiting for transfers between devices, coef_gather(): lax.ppermute(pair, 'chan', chan_perm(0, k))  18.2 us
    ppermute x7, starting transfers between devices, coef_gather(): lax.ppermute(pair, 'chan', chan_perm(0, k))  15.4 us
    all_to_all x1, starting transfers between devices, on_device(): cells = lax.all_to_all(cells, 'chan', 0, 0, tiled=True)  11.8 us
    pallas_call x1, Pallas kernels, inverse_transform(): pl.pallas_call(inverse_kernel, out_shape=jax.ShapeDtypeStruct((8, 8, 128,...  8.08 us
    dot_general x8, matrix products, product(): return jnp.einsum(form, left, right, precision=PRECISE)  7.35 us
    pallas_call x1, Pallas kernels, finish(): pl.pallas_call(finish_kernel, out_shape=jax.ShapeDtypeStruct((8, 8, 128,...  7.2 us
  transfers between devices with their start and end apart: 14, of which 8 were waited for; matrix products, arithmetic and copies ran while one was open for 8% of the time, Pallas kernels for 6%

profile of v2, /device:TPU:1, one launch (start us, length us, event | category | flops | bytes accessed | tf_op | source)
XLA Modules:
  0.0 176.2 jit_solution(10308752302205193251)
XLA Ops:
  0.0 4.3 %copy.43 = bf16[8,128,8,128]{3,2,1,0:T(8,128)(2,1)} copy(bf16[8,128,8,128]{3,1,0,2:T(8,128)(2,1)} %bitcast.84) | data formatting | bytes 4194304 | tf_op jit(solution)/shard_map/transpose | solution.py:243
  4.3 11.8 %all-to-all-start = ((bf16[16,64,8,128]{3,2,1,0:T(8,128)(2,1)}), bf16[16,64,8,128]{3,2,1,0:T(8,128)(2,1)}, u32[]{:S(2)}, u32[]{:S(2)}) async-start(bf16[16,64,8,128]{3,2,1,0:T(8,128)(2,1)} %bitcast.85), calls=%async_computation | async-start | bytes 4194304 | tf_op jit(solution)/shard_map/all_to_all | solution.py:244
  19.4 1.2 fusion.17
  20.5 1.2 fusion.6
  22.5 1.2 fusion.13
  23.7 1.2 fusion.5
  25.6 39.7 %all-to-all-done.cells_ref = bf16[16,64,8,128]{3,2,1,0:T(8,128)(2,1)} async-done(((bf16[16,64,8,128]{3,2,1,0:T(8,128)(2,1)}), bf16[16,64,8,128]{3,2,1,0:T(8,128)(2,1)}, u32[]{:S(2)}, u32[]{:S(2)}) %all-to-all-start) | async-done | bytes 2097184 | tf_op jit(solution)/shard_map/all_to_all | solution.py:244
  65.4 4.8 %pointwise_map.1 = bf16[16,8,64,128]{3,2,1,0:T(8,128)(2,1)} custom-call(bf16[128,128]{1,0:T(8,128)(2,1)} %weight_ref.1, bf16[16,64,8,128]{3,2,1,0:T(8,128)(2,1)} %all-to-all-done.cells_ref), custom_call_target="tpu_custom_call" | custom-call | tf_op jit(solution)/shard_map/pointwise_map/pallas_call | solution.py:98
  70.2 7.1 %all-to-all-start.1 = ((bf16[16,8,64,128]{3,2,1,0:T(8,128)(2,1)}), bf16[16,8,64,128]{3,2,1,0:T(8,128)(2,1)}, u32[]{:S(2)}, u32[]{:S(2)}) async-start(bf16[16,8,64,128]{3,2,1,0:T(8,128)(2,1)} %pointwise_map.1), calls=%async_computation.1 | async-start | bytes 4194304 | tf_op jit(solution)/shard_map/all_to_all | solution.py:249
  77.3 0.9 collective-permute-start
  79.3 3.2 %collective-permute-start.1 = (f32[2,2,2,8,256]{4,3,2,1,0:T(8,128)S(1)}, f32[2,2,2,8,256]{4,3,2,1,0:T(8,128)S(1)}, u32[]{:S(2)}, u32[]{:S(2)}) collective-permute-start(f32[2,2,2,8,256]{4,3,2,1,0:T(8,128)S(1)} %dynamic-slice_bitcast_fusion), channel_id=1, source_target_pairs={{0,64},{16,80},{32,96},{48,112},{64,0},{80,16},{96,32},{112,48},{1... | collective-permute-start | bytes 196616 | tf_op jit(solution)/shard_map/ppermute | solution.py:71
  82.7 1.9 %collective-permute-done.1 = f32[2,2,2,8,256]{4,3,2,1,0:T(8,128)S(1)} collective-permute-done((f32[2,2,2,8,256]{4,3,2,1,0:T(8,128)S(1)}, f32[2,2,2,8,256]{4,3,2,1,0:T(8,128)S(1)}, u32[]{:S(2)}, u32[]{:S(2)}) %collective-permute-start.1) | collective-permute-done | bytes 65568 | tf_op jit(solution)/shard_map/ppermute | solution.py:71
  84.6 1.4 collective-permute-start.2
  86.0 1.9 %collective-permute-done.2 = f32[2,2,8,256]{3,2,1,0:T(8,128)S(1)} collective-permute-done((f32[2,2,8,256]{3,2,1,0:T(8,128)S(1)}, f32[2,2,8,256]{3,2,1,0:T(8,128)S(1)}, u32[]{:S(2)}, u32[]{:S(2)}) %collective-permute-start.2) | collective-permute-done | bytes 32800 | tf_op jit(solution)/shard_map/ppermute | solution.py:71
  88.1 2.8 %collective-permute-done.3 = f32[2,8,256]{2,1,0:T(8,128)S(1)} collective-permute-done((f32[2,8,256]{2,1,0:T(8,128)S(1)}, f32[2,8,256]{2,1,0:T(8,128)S(1)}, u32[]{:S(2)}, u32[]{:S(2)}) %collective-permute-start.3) | collective-permute-done | bytes 16416 | tf_op jit(solution)/shard_map/ppermute | solution.py:71
  91.0 3.2 %collective-permute-start.4 = (f32[2,8,256]{2,1,0:T(8,128)S(1)}, f32[2,8,256]{2,1,0:T(8,128)S(1)}, u32[]{:S(2)}, u32[]{:S(2)}) collective-permute-start(f32[2,8,256]{2,1,0:T(8,128)S(1)} %bitcast_add_fusion.3), channel_id=1, source_target_pairs={{0,8},{1,9},{2,10},{3,11},{4,12},{5,13},{6,14},{7,15},{8,0},{9,1},... | collective-permute-start | bytes 49160 | tf_op jit(solution)/shard_map/ppermute | solution.py:200
  94.3 1.2 collective-permute-done.4
  95.5 3.1 %collective-permute-start.11 = (f32[2,2,8,256]{3,2,1,0:T(8,128)S(1)}, f32[2,2,8,256]{3,2,1,0:T(8,128)S(1)}, u32[]{:S(2)}, u32[]{:S(2)}) collective-permute-start(f32[2,2,8,256]{3,2,1,0:T(8,128)S(1)} %pad_maximum_fusion.refs_0_), channel_id=1, source_target_pairs={{0,7},{1,0},{2,1},{3,2},{4,3},{5,4},{6,5},{7,6},{8,15},{9,8},{10,9... | collective-permute-start | bytes 98312 | tf_op jit(solution)/shard_map/ppermute | solution.py:203
  98.6 3.0 %collective-permute-start.10 = (f32[2,2,8,256]{3,2,1,0:T(8,128)S(1)}, f32[2,2,8,256]{3,2,1,0:T(8,128)S(1)}, u32[]{:S(2)}, u32[]{:S(2)}) collective-permute-start(f32[2,2,8,256]{3,2,1,0:T(8,128)S(1)} %pad_maximum_fusion.refs_0_), channel_id=1, source_target_pairs={{0,6},{1,7},{2,0},{3,1},{4,2},{5,3},{6,4},{7,5},{8,14},{9,15},{10,... | collective-permute-start | bytes 98312 | tf_op jit(solution)/shard_map/ppermute | solution.py:203
  101.7 1.6 collective-permute-start.9
  103.3 4.0 %collective-permute-start.8 = (f32[2,2,8,256]{3,2,1,0:T(8,128)S(1)}, f32[2,2,8,256]{3,2,1,0:T(8,128)S(1)}, u32[]{:S(2)}, u32[]{:S(2)}) collective-permute-start(f32[2,2,8,256]{3,2,1,0:T(8,128)S(1)} %pad_maximum_fusion.refs_0_), channel_id=1, source_target_pairs={{0,4},{1,5},{2,6},{3,7},{4,0},{5,1},{6,2},{7,3},{8,12},{9,13},{10,... | collective-permute-start | bytes 98312 | tf_op jit(solution)/shard_map/ppermute | solution.py:203
  107.3 17.5 %collective-permute-done.11.refs_7_ = f32[2,2,8,256]{3,2,1,0:T(8,128)S(1)} collective-permute-done((f32[2,2,8,256]{3,2,1,0:T(8,128)S(1)}, f32[2,2,8,256]{3,2,1,0:T(8,128)S(1)}, u32[]{:S(2)}, u32[]{:S(2)}) %collective-permute-start.11) | collective-permute-done | bytes 32800 | tf_op jit(solution)/shard_map/ppermute | solution.py:203
  124.8 1.8 %collective-permute-start.6 = (f32[2,2,8,256]{3,2,1,0:T(8,128)S(1)}, f32[2,2,8,256]{3,2,1,0:T(8,128)S(1)}, u32[]{:S(2)}, u32[]{:S(2)}) collective-permute-start(f32[2,2,8,256]{3,2,1,0:T(8,128)S(1)} %pad_maximum_fusion.refs_0_), channel_id=1, source_target_pairs={{0,2},{1,3},{2,4},{3,5},{4,6},{5,7},{6,0},{7,1},{8,10},{9,11},{10,... | collective-permute-start | bytes 98312 | tf_op jit(solution)/shard_map/ppermute | solution.py:203
  126.6 0.7 collective-permute-done.10.refs_6_
  127.3 2.0 %collective-permute-start.5 = (f32[2,2,8,256]{3,2,1,0:T(8,128)S(1)}, f32[2,2,8,256]{3,2,1,0:T(8,128)S(1)}, u32[]{:S(2)}, u32[]{:S(2)}) collective-permute-start(f32[2,2,8,256]{3,2,1,0:T(8,128)S(1)} %pad_maximum_fusion.refs_0_), channel_id=1, source_target_pairs={{0,1},{1,2},{2,3},{3,4},{4,5},{5,6},{6,7},{7,0},{8,9},{9,10},{10,1... | collective-permute-start | bytes 98312 | tf_op jit(solution)/shard_map/ppermute | solution.py:203
  129.3 0.8 copy.53.table_x_ref
  130.0 1.2 copy.71
  131.2 1.5 mul.190.table_z_ref
  134.1 2.7 %mix.1 = f32[2,8,256]{2,1,0:T(8,128)} custom-call(s32[1]{0:T(128)} %bitcast.3.place_ref, f32[2,2,8,256]{3,2,1,0:T(8,128)} %copy-done.1, f32[2,2,8,256]{3,2,1,0:T(8,128)} %copy-done.8, f32[2,2,8,256]{3,2,1,0:T(8,128)} %copy-done.7, f32[2,2,8,256]{3,2,1,0:T(8,128)} %copy-done.6, f32[2,2,8,256]{3,2,1,0:T(8,128)} %copy-done.5, f32[2,2,8,256]{3,2,1,0:T(8,128)} %copy-done.4, ...), custom_call_target="tpu_custom_call" | custom-call | tf_op jit(solution)/shard_map/mix/pallas_call | solution.py:229
  136.8 24.1 %all-gather = f32[32,8,256]{2,1,0:T(8,128)} all-gather(f32[2,8,256]{2,1,0:T(8,128)} %mix.1), channel_id=2, replica_groups=mesh['slab'=16,'chan'=16] {'slab'}, dimensions={0}, use_global_device_ids=true | all-gather | bytes 278528 | tf_op jit(solution)/shard_map/all_gather | solution.py:251
  160.9 8.1 %inverse_transform.1.inverse_ref = f32[8,8,128,128]{3,2,1,0:T(8,128)} custom-call(f32[16,2,8,256]{3,2,1,0:T(8,128)} %bitcast.88, f32[256,256]{1,0:T(8,128)} %mul.190.table_z_ref, f32[256,32]{1,0:T(8,128)} %copy.53.table_x_ref, f32[256,1024]{1,0:T(8,128)} %bitcast.87), custom_call_target="tpu_custom_call" | custom-call | tf_op jit(solution)/shard_map/inverse_transform/pallas_call | solution.py:141
  169.0 7.2 %finish.1 = bf16[8,8,128,128]{3,2,1,0:T(8,128)(2,1)} custom-call(f32[8]{0:T(128)} %dynamic_slice.31.bias_ref, bf16[16,8,64,128]{3,2,1,0:T(8,128)(2,1)} %all-to-all-done.1.coded_ref, f32[8,8,128,128]{3,2,1,0:T(8,128)} %inverse_transform.1.inverse_ref), custom_call_target="tpu_custom_call" | custom-call | tf_op jit(solution)/shard_map/finish/pallas_call | solution.py:169
  (67 shorter events, 7.8 us)
Async XLA Ops:
  4.3 11.9 %copy-start = (bf16[1,8,8,128,128]{4,3,2,1,0:T(8,128)(2,1)S(1)}, bf16[1,8,8,128,128]{4,3,2,1,0:T(8,128)(2,1)}, u32[]{:S(2)}) copy-start(bf16[1,8,8,128,128]{4,3,2,1,0:T(8,128)(2,1)} %param.4) | copy-start | bytes 6291460
  4.3 61.1 %all-to-all-start = ((bf16[16,64,8,128]{3,2,1,0:T(8,128)(2,1)}), bf16[16,64,8,128]{3,2,1,0:T(8,128)(2,1)}, u32[]{:S(2)}, u32[]{:S(2)}) async-start(bf16[16,64,8,128]{3,2,1,0:T(8,128)(2,1)} %bitcast.85), calls=%async_computation | async-start | bytes 4194304 | tf_op jit(solution)/shard_map/all_to_all | solution.py:244
  70.2 98.8 %all-to-all-start.1 = ((bf16[16,8,64,128]{3,2,1,0:T(8,128)(2,1)}), bf16[16,8,64,128]{3,2,1,0:T(8,128)(2,1)}, u32[]{:S(2)}, u32[]{:S(2)}) async-start(bf16[16,8,64,128]{3,2,1,0:T(8,128)(2,1)} %pointwise_map.1), calls=%async_computation.1 | async-start | bytes 4194304 | tf_op jit(solution)/shard_map/all_to_all | solution.py:249
  77.3 1.9 %collective-permute-start = (f32[2,2,2,2,8,256]{5,4,3,2,1,0:T(8,128)S(1)}, f32[2,2,2,2,8,256]{5,4,3,2,1,0:T(8,128)S(1)}, u32[]{:S(2)}, u32[]{:S(2)}) collective-permute-start(f32[2,2,2,2,8,256]{5,4,3,2,1,0:T(8,128)S(1)} %bitcast.89), channel_id=1, source_target_pairs={{0,16},{16,0},{32,48},{48,32},{64,80},{80,64},{96,112},{112,96},{1... | collective-permute-start | bytes 393224 | tf_op jit(solution)/shard_map/ppermute | solution.py:71
  79.3 5.3 %collective-permute-start.1 = (f32[2,2,2,8,256]{4,3,2,1,0:T(8,128)S(1)}, f32[2,2,2,8,256]{4,3,2,1,0:T(8,128)S(1)}, u32[]{:S(2)}, u32[]{:S(2)}) collective-permute-start(f32[2,2,2,8,256]{4,3,2,1,0:T(8,128)S(1)} %dynamic-slice_bitcast_fusion), channel_id=1, source_target_pairs={{0,64},{16,80},{32,96},{48,112},{64,0},{80,16},{96,32},{112,48},{1... | collective-permute-start | bytes 196616 | tf_op jit(solution)/shard_map/ppermute | solution.py:71
  84.6 3.3 %collective-permute-start.2 = (f32[2,2,8,256]{3,2,1,0:T(8,128)S(1)}, f32[2,2,8,256]{3,2,1,0:T(8,128)S(1)}, u32[]{:S(2)}, u32[]{:S(2)}) collective-permute-start(f32[2,2,8,256]{3,2,1,0:T(8,128)S(1)} %dynamic-slice_bitcast_fusion.1), channel_id=1, source_target_pairs={{0,32},{16,48},{32,0},{48,16},{64,96},{80,112},{96,64},{112,80},{1... | collective-permute-start | bytes 98312 | tf_op jit(solution)/shard_map/ppermute | solution.py:71
  87.9 3.1 %collective-permute-start.3 = (f32[2,8,256]{2,1,0:T(8,128)S(1)}, f32[2,8,256]{2,1,0:T(8,128)S(1)}, u32[]{:S(2)}, u32[]{:S(2)}) collective-permute-start(f32[2,8,256]{2,1,0:T(8,128)S(1)} %dynamic-slice_bitcast_fusion.2), channel_id=1, source_target_pairs={{0,128},{16,144},{32,160},{48,176},{64,192},{80,208},{96,224},{112... | collective-permute-start | bytes 49160 | tf_op jit(solution)/shard_map/ppermute | solution.py:71
  91.0 4.5 %collective-permute-start.4 = (f32[2,8,256]{2,1,0:T(8,128)S(1)}, f32[2,8,256]{2,1,0:T(8,128)S(1)}, u32[]{:S(2)}, u32[]{:S(2)}) collective-permute-start(f32[2,8,256]{2,1,0:T(8,128)S(1)} %bitcast_add_fusion.3), channel_id=1, source_target_pairs={{0,8},{1,9},{2,10},{3,11},{4,12},{5,13},{6,14},{7,15},{8,0},{9,1},... | collective-permute-start | bytes 49160 | tf_op jit(solution)/shard_map/ppermute | solution.py:200
  95.5 37.2 %copy-start.1 = (f32[2,2,8,256]{3,2,1,0:T(8,128)}, f32[2,2,8,256]{3,2,1,0:T(8,128)S(1)}, u32[]{:S(2)}) copy-start(f32[2,2,8,256]{3,2,1,0:T(8,128)S(1)} %pad_maximum_fusion.refs_0_) | copy-start | bytes 98308
  95.5 29.2 %collective-permute-start.11 = (f32[2,2,8,256]{3,2,1,0:T(8,128)S(1)}, f32[2,2,8,256]{3,2,1,0:T(8,128)S(1)}, u32[]{:S(2)}, u32[]{:S(2)}) collective-permute-start(f32[2,2,8,256]{3,2,1,0:T(8,128)S(1)} %pad_maximum_fusion.refs_0_), channel_id=1, source_target_pairs={{0,7},{1,0},{2,1},{3,2},{4,3},{5,4},{6,5},{7,6},{8,15},{9,8},{10,9... | collective-permute-start | bytes 98312 | tf_op jit(solution)/shard_map/ppermute | solution.py:203
  98.6 28.7 %collective-permute-start.10 = (f32[2,2,8,256]{3,2,1,0:T(8,128)S(1)}, f32[2,2,8,256]{3,2,1,0:T(8,128)S(1)}, u32[]{:S(2)}, u32[]{:S(2)}) collective-permute-start(f32[2,2,8,256]{3,2,1,0:T(8,128)S(1)} %pad_maximum_fusion.refs_0_), channel_id=1, source_target_pairs={{0,6},{1,7},{2,0},{3,1},{4,2},{5,3},{6,4},{7,5},{8,14},{9,15},{10,... | collective-permute-start | bytes 98312 | tf_op jit(solution)/shard_map/ppermute | solution.py:203
  101.7 31.7 %collective-permute-start.9 = (f32[2,2,8,256]{3,2,1,0:T(8,128)S(1)}, f32[2,2,8,256]{3,2,1,0:T(8,128)S(1)}, u32[]{:S(2)}, u32[]{:S(2)}) collective-permute-start(f32[2,2,8,256]{3,2,1,0:T(8,128)S(1)} %pad_maximum_fusion.refs_0_), channel_id=1, source_target_pairs={{0,5},{1,6},{2,7},{3,0},{4,1},{5,2},{6,3},{7,4},{8,13},{9,14},{10,... | collective-permute-start | bytes 98312 | tf_op jit(solution)/shard_map/ppermute | solution.py:203
  103.3 30.1 %collective-permute-start.8 = (f32[2,2,8,256]{3,2,1,0:T(8,128)S(1)}, f32[2,2,8,256]{3,2,1,0:T(8,128)S(1)}, u32[]{:S(2)}, u32[]{:S(2)}) collective-permute-start(f32[2,2,8,256]{3,2,1,0:T(8,128)S(1)} %pad_maximum_fusion.refs_0_), channel_id=1, source_target_pairs={{0,4},{1,5},{2,6},{3,7},{4,0},{5,1},{6,2},{7,3},{8,12},{9,13},{10,... | collective-permute-start | bytes 98312 | tf_op jit(solution)/shard_map/ppermute | solution.py:203
  107.3 26.1 %collective-permute-start.7 = (f32[2,2,8,256]{3,2,1,0:T(8,128)S(1)}, f32[2,2,8,256]{3,2,1,0:T(8,128)S(1)}, u32[]{:S(2)}, u32[]{:S(2)}) collective-permute-start(f32[2,2,8,256]{3,2,1,0:T(8,128)S(1)} %pad_maximum_fusion.refs_0_), channel_id=1, source_target_pairs={{0,3},{1,4},{2,5},{3,6},{4,7},{5,0},{6,1},{7,2},{8,11},{9,12},{10,... | collective-permute-start | bytes 98312 | tf_op jit(solution)/shard_map/ppermute | solution.py:203
  124.8 8.0 %copy-start.2 = (f32[2,2,8,256]{3,2,1,0:T(8,128)}, f32[2,2,8,256]{3,2,1,0:T(8,128)S(1)}, u32[]{:S(2)}) copy-start(f32[2,2,8,256]{3,2,1,0:T(8,128)S(1)} %collective-permute-done.11.refs_7_) | copy-start | bytes 98308
  124.8 8.7 %collective-permute-start.6 = (f32[2,2,8,256]{3,2,1,0:T(8,128)S(1)}, f32[2,2,8,256]{3,2,1,0:T(8,128)S(1)}, u32[]{:S(2)}, u32[]{:S(2)}) collective-permute-start(f32[2,2,8,256]{3,2,1,0:T(8,128)S(1)} %pad_maximum_fusion.refs_0_), channel_id=1, source_target_pairs={{0,2},{1,3},{2,4},{3,5},{4,6},{5,7},{6,0},{7,1},{8,10},{9,11},{10,... | collective-permute-start | bytes 98312 | tf_op jit(solution)/shard_map/ppermute | solution.py:203
  127.3 5.4 %copy-start.3 = (f32[2,2,8,256]{3,2,1,0:T(8,128)}, f32[2,2,8,256]{3,2,1,0:T(8,128)S(1)}, u32[]{:S(2)}) copy-start(f32[2,2,8,256]{3,2,1,0:T(8,128)S(1)} %collective-permute-done.10.refs_6_) | copy-start | bytes 98308
  127.3 6.1 %collective-permute-start.5 = (f32[2,2,8,256]{3,2,1,0:T(8,128)S(1)}, f32[2,2,8,256]{3,2,1,0:T(8,128)S(1)}, u32[]{:S(2)}, u32[]{:S(2)}) collective-permute-start(f32[2,2,8,256]{3,2,1,0:T(8,128)S(1)} %pad_maximum_fusion.refs_0_), channel_id=1, source_target_pairs={{0,1},{1,2},{2,3},{3,4},{4,5},{5,6},{6,7},{7,0},{8,9},{9,10},{10,1... | collective-permute-start | bytes 98312 | tf_op jit(solution)/shard_map/ppermute | solution.py:203
  130.0 2.7 %copy-start.9 = (f32[128]{0:T(128)S(1)}, f32[128]{0:T(128)}, u32[]{:S(2)}) copy-start(f32[128]{0:T(128)} %param.6) | copy-start | bytes 1540
  133.4 0.6 copy-start.4
  133.4 0.6 copy-start.5
  133.4 0.6 copy-start.6
  133.4 0.6 copy-start.7
  133.5 0.6 copy-start.8

commit v3 on v1

v3 whole, which is shorter than its diff:
```python
import math

import jax
import jax.numpy as jnp
import numpy as np
from jax import lax
from jax.experimental import pallas as pl
from jax.experimental.pallas import tpu as pltpu
from jax.sharding import PartitionSpec as P


GRID = 128
KEEP = 16
BLOCKS = 16
PRECISE = lax.Precision.HIGHEST
CELL_SCALE = 2.0**20
COEF_SCALE = 2.0**6
WHOLE = pl.BlockSpec(memory_space=pltpu.VMEM)
SCALARS = pl.BlockSpec(memory_space=pltpu.SMEM)


def waves(freqs, positions):
    angle = 2.0 * math.pi * (freqs * positions % GRID).astype(np.float32) / np.float32(GRID)
    return np.cos(angle).astype(np.float32), np.sin(angle).astype(np.float32)


def plane_waves():
    index = np.arange(KEEP)
    freqs = np.where(index < KEEP // 2, index, index + GRID - KEEP)
    return waves(freqs[:, None], np.arange(GRID)[None, :])


def depth_angle(first_cell, shape, mode, cell):
    row = lax.broadcasted_iota(jnp.int32, shape, 0)
    lane = lax.broadcasted_iota(jnp.int32, shape, 1)
    turns = mode(row, lane) * (first_cell + cell(row, lane)) % GRID
    return 2.0 * math.pi * turns.astype(jnp.float32) / GRID, row, lane


def exact_dot(left, right):
    return jnp.dot(left, right, precision=PRECISE, preferred_element_type=jnp.float32)


def split(value):
    high = value.astype(jnp.bfloat16)
    return high, (value - high.astype(jnp.float32)).astype(jnp.bfloat16)


def encode(value, scale):
    value = value * scale
    return (value * jnp.abs(value) * (value * value)).astype(jnp.bfloat16)


def decode(coded, scale):
    coded = coded.astype(jnp.float32)
    size = lax.rsqrt(lax.rsqrt(jnp.abs(coded)))
    if scale != 1.0:
        size = size * (1.0 / scale)
    return jnp.where(coded < 0, -size, size)


def slab_perm(dx, dy, dc):
    pairs = []
    for a in range(2):
        for b in range(4):
            for c in range(2):
                pairs.append(((a * 4 + b) * 2 + c, ((a ^ dx) * 4 + (b ^ dy)) * 2 + (c ^ dc)))
    return pairs


def chan_perm(dx, dz):
    return [(h * 8 + z, (h ^ dx) * 8 + (z + dz) % 8) for h in range(2) for z in range(8)]


def halve(value, axis, bit, perm):
    own = lax.dynamic_index_in_dim(value, bit, axis, keepdims=False)
    other = lax.dynamic_index_in_dim(value, 1 - bit, axis, keepdims=False)
    return own + lax.ppermute(other, "slab", perm)


def slab_sum(partial):
    me = lax.axis_index("slab")
    value = partial.reshape(2, 2, 2, 2, *partial.shape[1:])
    value = halve(value, 3, me % 2, slab_perm(0, 0, 1))
    value = halve(value, 1, me // 4 % 2, slab_perm(0, 2, 0))
    value = halve(value, 1, me // 2 % 2, slab_perm(0, 1, 0))
    return halve(value, 0, me // 8, slab_perm(1, 0, 0))


def slab_gather(value):
    value = value[None]
    for step in ((1, 0, 0), (0, 1, 0), (0, 2, 0), (0, 0, 1)):
        value = jnp.concatenate([value, lax.ppermute(value, "slab", slab_perm(*step))], 0)
    return value


MIXED = tuple((e & 1) * 8 | (e >> 1 & 1) * 2 | (e >> 2 & 1) * 4 | e >> 3 for e in range(16))


def forward_kernel(field_ref, table_x_ref, table_y_ref, depth_ref, out_ref, wave_ref, table_z_ref):
    table_y = table_y_ref[...]
    lane = lax.broadcasted_iota(jnp.int32, (KEEP, 512), 1)
    row = lax.broadcasted_iota(jnp.int32, (KEEP, 512), 0)
    same_mode = lane // KEEP % KEEP == row
    for z in range(8):
        sections = []
        for c in range(8):
            section = jnp.dot(table_x_ref[...], field_ref[c, z], preferred_element_type=jnp.float32)
            sections.append(jnp.concatenate([section[:KEEP], section[KEEP:]], 1))
        wave_ref[:, pl.ds(z * 32, 32)] = exact_dot(jnp.concatenate(sections, 0), table_y)
        for part in range(2):
            rows = pl.ds(z * 32 + part * KEEP, KEEP)
            depth = jnp.broadcast_to(depth_ref[pl.ds(z * 2 + part, 1), :], (KEEP, 512))
            table_z_ref[rows, :] = jnp.where(same_mode, depth, 0.0)
    coefs = exact_dot(wave_ref[...], table_z_ref[...]).reshape(8, KEEP, 512).transpose(1, 0, 2)
    out_ref[:, 0] = coefs[:, :, :256]
    out_ref[:, 1] = coefs[:, :, 256:]


def forward_transform(field, first_cell):
    cos_x, sin_x = plane_waves()
    table_x = jnp.asarray(np.concatenate([cos_x, -sin_x], 0)).astype(jnp.bfloat16)
    table_y = jnp.asarray(
        np.concatenate([np.concatenate([cos_x.T, -sin_x.T], 1), np.concatenate([sin_x.T, cos_x.T], 1)], 0)
    )
    angle, row, lane = depth_angle(first_cell, (16, 512), lambda r, n: n % 16, lambda r, n: r // 2)
    from_part, to_part = row % 2, lane // 256
    turned = jnp.where(from_part == 1, jnp.sin(angle), -jnp.sin(angle))
    depth = jnp.where(from_part == to_part, jnp.cos(angle), turned)
    return pl.pallas_call(
        forward_kernel,
        out_shape=jax.ShapeDtypeStruct((KEEP, 2, 8, 256), jnp.float32),
        in_specs=[WHOLE] * 4,
        out_specs=WHOLE,
        scratch_shapes=[pltpu.VMEM((128, 256), jnp.float32), pltpu.VMEM((256, 512), jnp.float32)],
        cost_estimate=pl.CostEstimate(flops=200_000_000, bytes_accessed=3_000_000, transcendentals=0),
        compiler_params=pltpu.CompilerParams(vmem_limit_bytes=12 << 20),
        name="forward_transform",
    )(field, table_x, table_y, depth)


def cut_kernel(field_ref, out_ref, block_ref, turned_ref, fetched, stored):
    parts = fetched.shape[0]
    span = BLOCKS // parts
    fetches, stores = [], []
    for part in range(parts):
        blocks = pl.ds(part * span, span)
        fetches.append(pltpu.make_async_copy(field_ref.at[:, blocks], block_ref.at[:, blocks], fetched.at[part]))
        fetches[part].start()
    for part in range(parts):
        fetches[part].wait()
        for p in range(part * span, (part + 1) * span):
            block = block_ref[:, p].astype(jnp.float32)
            turned_ref[p] = block.transpose(1, 0, 2).astype(jnp.bfloat16)
        blocks = pl.ds(part * span, span)
        stores.append(pltpu.make_async_copy(turned_ref.at[blocks], out_ref.at[blocks], stored.at[part]))
        stores[part].start()
    for store in stores:
        store.wait()


def cut(blocks):
    parts = 8
    in_place = pl.BlockSpec(memory_space=pltpu.HBM)
    return pl.pallas_call(
        cut_kernel,
        out_shape=pltpu.HBM((BLOCKS, 64, 8, 128), jnp.bfloat16),
        in_specs=[in_place],
        out_specs=in_place,
        scratch_shapes=[
            pltpu.VMEM((8, BLOCKS, 64, 128), jnp.bfloat16),
            pltpu.VMEM((BLOCKS, 64, 8, 128), jnp.bfloat16),
            pltpu.SemaphoreType.DMA((parts,)),
            pltpu.SemaphoreType.DMA((parts,)),
        ],
        cost_estimate=pl.CostEstimate(flops=1_000_000, bytes_accessed=4_000_000, transcendentals=0),
        compiler_params=pltpu.CompilerParams(vmem_limit_bytes=60 << 20),
        name="cut",
    )(blocks)


def map_kernel(weight_ref, cells_ref, out_ref, kept_ref, block_ref, held_ref, fetched, stored):
    del kept_ref
    parts = fetched.shape[0]
    rows = 64 // parts
    fetches, stores = [], []
    for part in range(parts):
        span = pl.ds(part * rows, rows)
        fetches.append(pltpu.make_async_copy(cells_ref.at[:, span], block_ref.at[:, span], fetched.at[part]))
        fetches[part].start()
    for part in range(parts):
        fetches[part].wait()
        for first in range(part * rows, (part + 1) * rows, 8):
            coded = []
            for x in range(first, first + 8, 2):
                pair = [block_ref[:, x + near].reshape(128, 128) for near in range(2)]
                mapped = jnp.dot(weight_ref[...], jnp.concatenate(pair, 1), preferred_element_type=jnp.float32)
                mapped = mapped * jnp.abs(mapped) * (mapped * mapped)
                coded += [mapped[:, :128], mapped[:, 128:]]
            turned = jnp.stack(coded, 0).transpose(1, 0, 2)
            held_ref[:, :, pl.ds(first, 8), :] = turned.reshape(BLOCKS, 8, 8, 128).astype(jnp.bfloat16)
        span = pl.ds(part * rows, rows)
        stores.append(
            pltpu.make_async_copy(held_ref.at[:, :, span, :], out_ref.at[:, :, span, :], stored.at[part])
        )
        stores[part].start()
    for store in stores:
        store.wait()


def pointwise_map(weight, cells):
    parts = 4
    in_place = pl.BlockSpec(memory_space=pltpu.HBM)
    return pl.pallas_call(
        map_kernel,
        out_shape=[
            pltpu.HBM((BLOCKS, 8, 64, 128), jnp.bfloat16),
            pltpu.HBM((BLOCKS, 64, 8, 128), jnp.bfloat16),
        ],
        in_specs=[WHOLE, in_place],
        out_specs=[in_place] * 2,
        scratch_shapes=[
            pltpu.VMEM((BLOCKS, 64, 8, 128), jnp.bfloat16),
            pltpu.VMEM((BLOCKS, 8, 64, 128), jnp.bfloat16),
            pltpu.SemaphoreType.DMA((parts,)),
            pltpu.SemaphoreType.DMA((parts,)),
        ],
        input_output_aliases={1: 1},
        cost_estimate=pl.CostEstimate(flops=270_000_000, bytes_accessed=4_000_000, transcendentals=0),
        compiler_params=pltpu.CompilerParams(vmem_limit_bytes=10 << 20),
        name="pointwise_map",
    )(weight * jnp.bfloat16(CELL_SCALE), cells)[0]


def source_block(place_ref, k, h):
    return lax.bitwise_xor(place_ref[1], h) * 8 + lax.rem(place_ref[0] + (8 - k), 8)


def mix_kernel(place_ref, *refs):
    letters, weight_ref, out_ref, coef_ref = refs[:8], refs[8], refs[9], refs[10]
    for k in range(8):
        for h in range(2):
            for part in range(2):
                for side in range(2):
                    coded = letters[k][h, part * 2 + side]
                    coef_ref[k * 2 + h, part, :, pl.ds(side * 128, 128)] = decode(coded, COEF_SCALE)
    for o in range(8):
        real = jnp.zeros((8, 256), jnp.float32)
        imag = jnp.zeros((8, 256), jnp.float32)
        for k in range(8):
            for h in range(2):
                rows = pl.ds(pl.multiple_of(source_block(place_ref, k, h) * 8, 8), 8)
                weight_real = weight_ref[0, o, rows, :]
                weight_imag = weight_ref[1, o, rows, :]
                coef_real = coef_ref[k * 2 + h, 0]
                coef_imag = coef_ref[k * 2 + h, 1]
                real += coef_real * weight_real - coef_imag * weight_imag
                imag += coef_real * weight_imag + coef_imag * weight_real
        out_ref[0, pl.ds(o, 1), :] = jnp.sum(real, 0, keepdims=True)
        out_ref[1, pl.ds(o, 1), :] = jnp.sum(imag, 0, keepdims=True)


def mix(place, letters, spec_weight):
    return pl.pallas_call(
        mix_kernel,
        out_shape=jax.ShapeDtypeStruct((2, 8, 256), jnp.float32),
        in_specs=[SCALARS] + [WHOLE] * 9,
        out_specs=WHOLE,
        scratch_shapes=[pltpu.VMEM((BLOCKS, 2, 8, 256), jnp.float32)],
        cost_estimate=pl.CostEstimate(flops=5_000_000, bytes_accessed=3_000_000, transcendentals=0),
        compiler_params=pltpu.CompilerParams(vmem_limit_bytes=8 << 20),
        name="mix",
    )(place, *letters, spec_weight)


def inverse_kernel(me_ref, bias_ref, spec_ref, depth_ref, table_x_ref, waves_y_ref, out_ref, plane_ref, line_ref, table_ref):
    row = lax.broadcasted_iota(jnp.int32, (256, 256), 0)
    lane = lax.broadcasted_iota(jnp.int32, (256, 256), 1)
    table_z = jnp.where(row // KEEP == lane % KEEP, jnp.concatenate([depth_ref[...]] * KEEP, 0), 0.0)
    real = exact_dot(spec_ref[:, 0].reshape(128, 256), table_z)
    imag = exact_dot(spec_ref[:, 1].reshape(128, 256), table_z)
    plane_real = (real[:, :128] - imag[:, 128:]).reshape(16, 8, 128)
    plane_imag = (imag[:, :128] + real[:, 128:]).reshape(16, 8, 128)
    for e in range(16):
        j = lax.bitwise_xor(me_ref[0], MIXED[e])
        plane_ref[j] = plane_real[e]
        plane_ref[16 + j] = plane_imag[e]
    for o in range(8):
        line = exact_dot(table_x_ref[...], plane_ref[:, o, :])
        line_ref[pl.ds(o * 128, 128), :] = jnp.concatenate([line[:128], line[128:]], 1)
    table_ref[...] = jnp.zeros_like(table_ref)
    for z in range(8):
        for part in range(2):
            table_ref[pl.ds(part * 128 + z * 16, 16), pl.ds(z * 128, 128)] = waves_y_ref[part]
    line_high, line_low = split(line_ref[...])
    for z in range(0, 8, 2):
        high, low = split(table_ref[:, z * 128 : (z + 2) * 128])
        field = jnp.dot(line_high, low, preferred_element_type=jnp.float32)
        field += jnp.dot(line_low, high, preferred_element_type=jnp.float32)
        field += jnp.dot(line_high, high, preferred_element_type=jnp.float32)
        for o in range(8):
            rows = slice(o * 128, (o + 1) * 128)
            out_ref[o, z] = field[rows, :128] + bias_ref[o]
            out_ref[o, z + 1] = field[rows, 128:] + bias_ref[o]


def inverse_transform(me, bias, spectrum, first_cell):
    cos_x, sin_x = plane_waves()
    table_x = jnp.asarray(
        np.concatenate([np.concatenate([cos_x.T, -sin_x.T], 1), np.concatenate([sin_x.T, cos_x.T], 1)], 0)
    )
    waves_y = jnp.asarray(np.stack([cos_x, -sin_x], 0))
    angle, row, lane = depth_angle(first_cell, (16, 256), lambda r, n: r, lambda r, n: n // 16 % 8)
    fold = jnp.where(row == 0, 1.0, 2.0) * (CELL_SCALE / GRID**3)
    depth = jnp.where(lane < 128, jnp.cos(angle), jnp.sin(angle)) * fold
    return pl.pallas_call(
        inverse_kernel,
        out_shape=pltpu.HBM((8, 8, 128, 128), jnp.float32),
        in_specs=[SCALARS] * 2 + [WHOLE] * 4,
        out_specs=WHOLE,
        scratch_shapes=[
            pltpu.VMEM((32, 8, 128), jnp.float32),
            pltpu.VMEM((1024, 256), jnp.float32),
            pltpu.VMEM((256, 1024), jnp.float32),
        ],
        cost_estimate=pl.CostEstimate(flops=2_000_000_000, bytes_accessed=5_000_000, transcendentals=0),
        compiler_params=pltpu.CompilerParams(vmem_limit_bytes=16 << 20),
        name="inverse_transform",
    )(me, bias * CELL_SCALE, spectrum, depth, table_x, waves_y)


def activate(coded, inverse):
    total = decode(coded, 1.0) + inverse
    half = total * (0.5 / CELL_SCALE)
    return (half + half * lax.erf(total * (math.sqrt(0.5) / CELL_SCALE))).astype(jnp.bfloat16)


def finish_kernel(coded_ref, inverse_ref, out_ref, kept_ref, field_ref, done_ref, fetched, stored):
    del kept_ref
    parts = fetched.shape[0]
    span = BLOCKS // parts
    fetches, stores = [], []
    for part in range(parts):
        blocks = pl.ds(part * span, span)
        fetches.append(pltpu.make_async_copy(inverse_ref.at[:, blocks], field_ref.at[:, blocks], fetched.at[part]))
        fetches[part].start()
    for part in range(parts):
        fetches[part].wait()
        for o in range(8):
            for p in range(part * span, (part + 1) * span):
                done_ref[o, p] = activate(coded_ref[p, o], field_ref[o, p])
        blocks = pl.ds(part * span, span)
        stores.append(pltpu.make_async_copy(done_ref.at[:, blocks], out_ref.at[:, blocks], stored.at[part]))
        stores[part].start()
    for store in stores:
        store.wait()


def finish(coded, inverse):
    parts = 8
    in_place = pl.BlockSpec(memory_space=pltpu.HBM)
    return pl.pallas_call(
        finish_kernel,
        out_shape=[
            pltpu.HBM((8, BLOCKS, 64, 128), jnp.bfloat16),
            pltpu.HBM((8, BLOCKS, 64, 128), jnp.float32),
        ],
        in_specs=[WHOLE, in_place],
        out_specs=[in_place] * 2,
        scratch_shapes=[
            pltpu.VMEM((8, BLOCKS, 64, 128), jnp.float32),
            pltpu.VMEM((8, BLOCKS, 64, 128), jnp.bfloat16),
            pltpu.SemaphoreType.DMA((parts,)),
            pltpu.SemaphoreType.DMA((parts,)),
        ],
        input_output_aliases={1: 1},
        cost_estimate=pl.CostEstimate(flops=30_000_000, bytes_accessed=8_000_000, transcendentals=0),
        compiler_params=pltpu.CompilerParams(vmem_limit_bytes=12 << 20),
        name="finish",
    )(coded, inverse)[0]


def on_device(field, local_weight, bias, spec_weight):
    slab, chan = lax.axis_index("slab"), lax.axis_index("chan")
    first_cell = slab * 8
    x_hi = chan // 8
    place = jnp.stack([chan % 8, x_hi]).astype(jnp.int32)
    planes = field[0]
    blocks = planes.reshape(8, BLOCKS, 64, 128)
    cells = lax.all_to_all(cut(blocks), "chan", 0, 0, tiled=True)
    partial = forward_transform(planes, first_cell)
    owned = slab_sum(partial)
    own_coef = encode(owned, COEF_SCALE).reshape(2, 8, 2, 128).transpose(0, 2, 1, 3).reshape(4, 8, 128)
    other_coef = lax.ppermute(own_coef, "chan", chan_perm(1, 0))
    letter = jnp.stack([own_coef, other_coef], 0)
    letters = [letter] + [lax.ppermute(letter, "chan", chan_perm(0, k)) for k in range(1, 8)]
    coded = pointwise_map(local_weight, cells)
    coded = lax.all_to_all(coded, "chan", 0, 0, tiled=True)
    mixed = mix(place, letters, spec_weight)
    spectrum = slab_gather(mixed)
    me = jnp.reshape(slab, (1,)).astype(jnp.int32)
    offset = lax.dynamic_slice_in_dim(bias, chan * 8, 8, 0)
    inverse = inverse_transform(me, offset, spectrum, first_cell).reshape(8, BLOCKS, 64, 128)
    done = finish(coded, inverse)
    return done.reshape(1, 8, 8, 128, 128)


def solution(mesh):
    placed = (P(None, "chan", "slab", None, None), P(), P(), P(None, "chan", None, "slab"))
    return jax.shard_map(
        on_device,
        mesh=mesh,
        in_specs=placed,
        out_specs=P(None, "chan", "slab", None, None),
        check_vma=False,
    )
```

time: 151 us -> 160 us (1.060); the launches traced: 149 us -> 160 us
  waiting for transfers between devices: 47.8 us -> 80.3 us
  starting transfers between devices: 30.3 us -> 53.8 us
  blocking collectives: 23.3 us -> 0 us
  matrix products: 7.8 us -> 0 us
  local copies, waits for them, and re-layouts: 10.8 us -> 4.6 us
  Pallas kernels: 25.4 us -> 19.8 us
  other arithmetic: 2.85 us -> 0.59 us
    ppermute x0 -> x12, starting transfers between devices: none -> 29.3 us  [the longest x7 14.2 us: on_device(): lax.ppermute(letter, 'chan', chan_perm(0, k))]
    ppermute x0 -> x12, waiting for transfers between devices: none -> 23.8 us  [the longest x7 16.1 us: on_device(): lax.ppermute(letter, 'chan', chan_perm(0, k))]
    all_gather x1 -> x0, blocking collectives: 23.3 us -> none  [on_device(): spectrum = lax.all_gather(mixed, 'slab', axis=0)]
    all_to_all x2 -> x1, waiting for transfers between devices: 29.5 us -> 49.2 us  [on_device(): cells = lax.all_to_all(cut(blocks), 'chan', 0, 0, tiled=True)]
    all_to_all x1, waiting for transfers between devices: 10.6 us -> 0.01 us  [on_device(): coded = lax.all_to_all(coded, 'chan', 0, 0, tiled=True)]
    dot_general x9 -> x0, matrix products: 7.8 us -> none  [the longest x8 7.39 us: product(): return jnp.einsum(form, left, right, precision=PRECISE)]
    all_to_all x2 -> x1, starting transfers between devices: 18.8 us -> 11.6 us  [on_device(): cells = lax.all_to_all(cut(blocks), 'chan', 0, 0, tiled=True)]
    pallas_call x3 -> x6, Pallas kernels: 25.4 us -> 19.8 us  [the longest x1 5.56 us: inverse_transform(): pl.pallas_call(inverse_kernel, out_shape=pltpu.HBM((8, 8, 128, 128), jnp....]
  transfers between devices with their start and end apart: 7 -> 18, of which waited for: 7 -> 14; matrix products, arithmetic and copies ran while one was open for 12% -> 0% of each run, Pallas kernels for 9% -> 6%
where the time goes in v3:
time: 160 us
  waiting for transfers between devices  80.3 us (50%)
  starting transfers between devices  53.8 us (34%)
  Pallas kernels  19.8 us (12%)
  local copies, waits for them, and re-layouts  4.6 us (3%)
    all_to_all x1, waiting for transfers between devices, on_device(): cells = lax.all_to_all(cut(blocks), 'chan', 0, 0, tiled=True)  49.2 us
    ppermute x7, waiting for transfers between devices, on_device(): lax.ppermute(letter, 'chan', chan_perm(0, k))  16.1 us
    ppermute x7, starting transfers between devices, on_device(): lax.ppermute(letter, 'chan', chan_perm(0, k))  14.2 us
    ppermute x4, starting transfers between devices, slab_gather(): lax.ppermute(value, 'slab', slab_perm(*step))  11.9 us
    all_to_all x1, starting transfers between devices, on_device(): cells = lax.all_to_all(cut(blocks), 'chan', 0, 0, tiled=True)  11.6 us
    ppermute x4, waiting for transfers between devices, halve(): return own + lax.ppermute(other, 'slab', perm)  7.31 us
    all_to_all x1, starting transfers between devices, on_device(): coded = lax.all_to_all(coded, 'chan', 0, 0, tiled=True)  7.16 us
    ppermute x4, waiting for transfers between devices, slab_gather(): lax.ppermute(value, 'slab', slab_perm(*step))  6.34 us
  transfers between devices with their start and end apart: 18, of which 14 were waited for; matrix products, arithmetic and copies ran while one was open for 0% of the time, Pallas kernels for 6%

profile of v3, /device:TPU:1, one launch (start us, length us, event | category | flops | bytes accessed | tf_op | source)
XLA Modules:
  0.0 159.6 jit_solution(17721916095040462618)
XLA Ops:
  0.0 2.7 %cut.1 = bf16[16,64,8,128]{3,2,1,0:T(8,128)(2,1)} custom-call(bf16[8,16,64,128]{3,2,1,0:T(8,128)(2,1)} %bitcast.38), custom_call_target="tpu_custom_call" | custom-call | flops 1000000 | bytes 4000000 | tf_op jit(solution)/shard_map/cut/pallas_call | solution.py:165
  2.7 11.6 %all-to-all-start = ((bf16[16,64,8,128]{3,2,1,0:T(8,128)(2,1)}), bf16[16,64,8,128]{3,2,1,0:T(8,128)(2,1)S(1)}, u32[]{:S(2)}, u32[]{:S(2)}) async-start(bf16[16,64,8,128]{3,2,1,0:T(8,128)(2,1)} %cut.1), calls=%async_computation | async-start | bytes 4194304 | tf_op jit(solution)/shard_map/all_to_all | solution.py:390
  14.4 49.2 %all-to-all-done.cells_ref = bf16[16,64,8,128]{3,2,1,0:T(8,128)(2,1)S(1)} async-done(((bf16[16,64,8,128]{3,2,1,0:T(8,128)(2,1)}), bf16[16,64,8,128]{3,2,1,0:T(8,128)(2,1)S(1)}, u32[]{:S(2)}, u32[]{:S(2)}) %all-to-all-start) | async-done | bytes 2097184 | tf_op jit(solution)/shard_map/all_to_all | solution.py:390
  63.6 1.3 copy-done.5
  64.9 4.1 %pointwise_map.1 = (bf16[16,8,64,128]{3,2,1,0:T(8,128)(2,1)}, bf16[16,64,8,128]{3,2,1,0:T(8,128)(2,1)}) custom-call(bf16[128,128]{1,0:T(8,128)(2,1)S(1)} %broadcast_multiply_fusion.weight_ref, bf16[16,64,8,128]{3,2,1,0:T(8,128)(2,1)} %copy-done.5), custom_call_target="tpu_custom_call", output_to_operand_aliasing={{1}: (1, {})} | custom-call | flops 270000000 | bytes 4000000 | tf_op jit(solution)/shard_map/pointwise_map/pallas_call | solution.py:214
  69.0 7.2 %all-to-all-start.1 = ((bf16[16,8,64,128]{3,2,1,0:T(8,128)(2,1)}), bf16[16,8,64,128]{3,2,1,0:T(8,128)(2,1)S(1)}, u32[]{:S(2)}, u32[]{:S(2)}) async-start(bf16[16,8,64,128]{3,2,1,0:T(8,128)(2,1)} %get-tuple-element.7), calls=%async_computation.1 | async-start | bytes 4194304 | tf_op jit(solution)/shard_map/all_to_all | solution.py:398
  76.5 1.6 copy-done
  78.0 2.6 %forward_transform.1 = f32[16,2,8,256]{3,2,1,0:T(8,128)S(1)} custom-call(bf16[8,8,128,128]{3,2,1,0:T(8,128)(2,1)S(1)} %bitcast.39, bf16[32,128]{1,0:T(8,128)(2,1)S(1)} %copy-done.3, f32[256,32]{1,0:T(8,128)S(1)} %copy-done.2, f32[16,512]{1,0:T(8,128)S(1)} %fusion.3.depth_ref), custom_call_target="tpu_custom_call" | custom-call | flops 200000000 | bytes 3000000 | tf_op jit(solution)/shard_map/forward_transform/pallas_call | solution.py:130
  81.6 1.0 collective-permute-done
  82.7 3.0 %collective-permute-start.1 = (f32[2,2,2,8,256]{4,3,2,1,0:T(8,128)S(1)}, f32[2,2,2,8,256]{4,3,2,1,0:T(8,128)S(1)}, u32[]{:S(2)}, u32[]{:S(2)}) collective-permute-start(f32[2,2,2,8,256]{4,3,2,1,0:T(8,128)S(1)} %dynamic-slice_bitcast_fusion.1), channel_id=1, source_target_pairs={{0,64},{16,80},{32,96},{48,112},{64,0},{80,16},{96,32},{112,48},{1... | collective-permute-start | bytes 196616 | tf_op jit(solution)/shard_map/ppermute | solution.py:78
  85.7 2.0 %collective-permute-done.1 = f32[2,2,2,8,256]{4,3,2,1,0:T(8,128)S(1)} collective-permute-done((f32[2,2,2,8,256]{4,3,2,1,0:T(8,128)S(1)}, f32[2,2,2,8,256]{4,3,2,1,0:T(8,128)S(1)}, u32[]{:S(2)}, u32[]{:S(2)}) %collective-permute-start.1) | collective-permute-done | bytes 65568 | tf_op jit(solution)/shard_map/ppermute | solution.py:78
  87.7 1.4 collective-permute-start.2
  89.1 1.8 %collective-permute-done.2 = f32[2,2,8,256]{3,2,1,0:T(8,128)S(1)} collective-permute-done((f32[2,2,8,256]{3,2,1,0:T(8,128)S(1)}, f32[2,2,8,256]{3,2,1,0:T(8,128)S(1)}, u32[]{:S(2)}, u32[]{:S(2)}) %collective-permute-start.2) | collective-permute-done | bytes 32800 | tf_op jit(solution)/shard_map/ppermute | solution.py:78
  91.3 2.6 %collective-permute-done.3 = f32[2,8,256]{2,1,0:T(8,128)S(1)} collective-permute-done((f32[2,8,256]{2,1,0:T(8,128)S(1)}, f32[2,8,256]{2,1,0:T(8,128)S(1)}, u32[]{:S(2)}, u32[]{:S(2)}) %collective-permute-start.3) | collective-permute-done | bytes 16416 | tf_op jit(solution)/shard_map/ppermute | solution.py:78
  93.8 3.2 %collective-permute-start.4 = (bf16[4,8,128]{2,1,0:T(8,128)(2,1)S(1)}, bf16[4,8,128]{2,1,0:T(8,128)(2,1)S(1)}, u32[]{:S(2)}, u32[]{:S(2)}) collective-permute-start(bf16[4,8,128]{2,1,0:T(8,128)(2,1)S(1)} %bitcast.47), channel_id=1, source_target_pairs={{0,8},{1,9},{2,10},{3,11},{4,12},{5,13},{6,14},{7,15},{8,0},{9,1},... | collective-permute-start | bytes 24584 | tf_op jit(solution)/shard_map/ppermute | solution.py:394
  97.1 1.3 collective-permute-done.4
  98.4 3.1 %collective-permute-start.11 = (bf16[2,4,8,128]{3,2,1,0:T(8,128)(2,1)S(1)}, bf16[2,4,8,128]{3,2,1,0:T(8,128)(2,1)S(1)}, u32[]{:S(2)}, u32[]{:S(2)}) collective-permute-start(bf16[2,4,8,128]{3,2,1,0:T(8,128)(2,1)S(1)} %pad_maximum_fusion.3.refs_0_), channel_id=1, source_target_pairs={{0,7},{1,0},{2,1},{3,2},{4,3},{5,4},{6,5},{7,6},{8,15},{9,8},{10,9... | collective-permute-start | bytes 49160 | tf_op jit(solution)/shard_map/ppermute | solution.py:396
  101.5 1.7 %collective-permute-start.10 = (bf16[2,4,8,128]{3,2,1,0:T(8,128)(2,1)S(1)}, bf16[2,4,8,128]{3,2,1,0:T(8,128)(2,1)S(1)}, u32[]{:S(2)}, u32[]{:S(2)}) collective-permute-start(bf16[2,4,8,128]{3,2,1,0:T(8,128)(2,1)S(1)} %pad_maximum_fusion.3.refs_0_), channel_id=1, source_target_pairs={{0,6},{1,7},{2,0},{3,1},{4,2},{5,3},{6,4},{7,5},{8,14},{9,15},{10,... | collective-permute-start | bytes 49160 | tf_op jit(solution)/shard_map/ppermute | solution.py:396
  103.4 1.2 collective-permute-start.9
  104.5 3.8 %collective-permute-start.8 = (bf16[2,4,8,128]{3,2,1,0:T(8,128)(2,1)S(1)}, bf16[2,4,8,128]{3,2,1,0:T(8,128)(2,1)S(1)}, u32[]{:S(2)}, u32[]{:S(2)}) collective-permute-start(bf16[2,4,8,128]{3,2,1,0:T(8,128)(2,1)S(1)} %pad_maximum_fusion.3.refs_0_), channel_id=1, source_target_pairs={{0,4},{1,5},{2,6},{3,7},{4,0},{5,1},{6,2},{7,3},{8,12},{9,13},{10,... | collective-permute-start | bytes 49160 | tf_op jit(solution)/shard_map/ppermute | solution.py:396
  108.4 14.9 %collective-permute-done.11.refs_7_ = bf16[2,4,8,128]{3,2,1,0:T(8,128)(2,1)S(1)} collective-permute-done((bf16[2,4,8,128]{3,2,1,0:T(8,128)(2,1)S(1)}, bf16[2,4,8,128]{3,2,1,0:T(8,128)(2,1)S(1)}, u32[]{:S(2)}, u32[]{:S(2)}) %collective-permute-start.11) | collective-permute-done | bytes 16416 | tf_op jit(solution)/shard_map/ppermute | solution.py:396
  123.3 1.6 %collective-permute-start.6 = (bf16[2,4,8,128]{3,2,1,0:T(8,128)(2,1)S(1)}, bf16[2,4,8,128]{3,2,1,0:T(8,128)(2,1)S(1)}, u32[]{:S(2)}, u32[]{:S(2)}) collective-permute-start(bf16[2,4,8,128]{3,2,1,0:T(8,128)(2,1)S(1)} %pad_maximum_fusion.3.refs_0_), channel_id=1, source_target_pairs={{0,2},{1,3},{2,4},{3,5},{4,6},{5,7},{6,0},{7,1},{8,10},{9,11},{10,... | collective-permute-start | bytes 49160 | tf_op jit(solution)/shard_map/ppermute | solution.py:396
  125.1 2.7 %collective-permute-start.5 = (bf16[2,4,8,128]{3,2,1,0:T(8,128)(2,1)S(1)}, bf16[2,4,8,128]{3,2,1,0:T(8,128)(2,1)S(1)}, u32[]{:S(2)}, u32[]{:S(2)}) collective-permute-start(bf16[2,4,8,128]{3,2,1,0:T(8,128)(2,1)S(1)} %pad_maximum_fusion.3.refs_0_), channel_id=1, source_target_pairs={{0,1},{1,2},{2,3},{3,4},{4,5},{5,6},{6,7},{7,0},{8,9},{9,10},{10,1... | collective-permute-start | bytes 49160 | tf_op jit(solution)/shard_map/ppermute | solution.py:396
  128.9 1.6 copy-done.1
  131.9 2.2 %collective-permute-done.12 = f32[1,2,8,256]{3,2,1,0:T(8,128)S(1)} collective-permute-done((f32[1,2,8,256]{3,2,1,0:T(8,128)S(1)}, f32[1,2,8,256]{3,2,1,0:T(8,128)S(1)}, u32[]{:S(2)}, u32[]{:S(2)}) %collective-permute-start.12) | collective-permute-done | bytes 16416 | tf_op jit(solution)/shard_map/ppermute | solution.py:93
  134.1 1.3 collective-permute-start.13
  135.4 1.5 collective-permute-done.13
  136.9 2.9 %collective-permute-start.14 = (f32[4,2,8,256]{3,2,1,0:T(8,128)S(1)}, f32[4,2,8,256]{3,2,1,0:T(8,128)S(1)}, u32[]{:S(2)}, u32[]{:S(2)}) collective-permute-start(f32[4,2,8,256]{3,2,1,0:T(8,128)S(1)} %pad_maximum_fusion.1), channel_id=1, source_target_pairs={{0,64},{16,80},{32,96},{48,112},{64,0},{80,16},{96,32},{112,48},{1... | collective-permute-start | bytes 196616 | tf_op jit(solution)/shard_map/ppermute | solution.py:93
  139.8 1.7 %collective-permute-done.14 = f32[4,2,8,256]{3,2,1,0:T(8,128)S(1)} collective-permute-done((f32[4,2,8,256]{3,2,1,0:T(8,128)S(1)}, f32[4,2,8,256]{3,2,1,0:T(8,128)S(1)}, u32[]{:S(2)}, u32[]{:S(2)}) %collective-permute-start.14) | collective-permute-done | bytes 65568 | tf_op jit(solution)/shard_map/ppermute | solution.py:93
  141.5 7.3 %collective-permute-start.15 = (f32[8,2,8,256]{3,2,1,0:T(8,128)S(1)}, f32[8,2,8,256]{3,2,1,0:T(8,128)S(1)}, u32[]{:S(2)}, u32[]{:S(2)}) collective-permute-start(f32[8,2,8,256]{3,2,1,0:T(8,128)S(1)} %pad_maximum_fusion), channel_id=1, source_target_pairs={{0,16},{16,0},{32,48},{48,32},{64,80},{80,64},{96,112},{112,96},{1... | collective-permute-start | bytes 393224 | tf_op jit(solution)/shard_map/ppermute | solution.py:93
  149.9 5.6 %inverse_transform.1 = f32[8,8,128,128]{3,2,1,0:T(8,128)} custom-call(s32[1]{0:T(128)} %bitcast.1.me_ref, f32[8]{0:T(128)S(1)} %dynamic-slice_multiply_fusion.bias_ref, f32[16,2,8,256]{3,2,1,0:T(8,128)S(1)} %constant_dynamic-update-slice_fusion.spec_ref, f32[16,256]{1,0:T(8,128)S(1)} %select_multiply_fusion.depth_ref, f32[256,32]{1,0:T(8,128)S(1)} %copy-done.2, ...), custom_call_target="tpu_custom_call" | custom-call | flops 2000000000 | bytes 5000000 | tf_op jit(solution)/shard_map/inverse_transform/pallas_call | solution.py:316
  155.4 4.0 %finish.1 = (bf16[8,16,64,128]{3,2,1,0:T(8,128)(2,1)}, f32[8,16,64,128]{3,2,1,0:T(8,128)}) custom-call(bf16[16,8,64,128]{3,2,1,0:T(8,128)(2,1)S(1)} %all-to-all-done.1.coded_ref, f32[8,16,64,128]{3,2,1,0:T(8,128)} %bitcast.46), custom_call_target="tpu_custom_call", output_to_operand_aliasing={{1}: (1, {})} | custom-call | flops 30000000 | bytes 8000000 | tf_op jit(solution)/shard_map/finish/pallas_call | solution.py:362
  (57 shorter events, 5.6 us)
Async XLA Ops:
  2.7 11.7 %copy-start.6 = (bf16[128,128]{1,0:T(8,128)(2,1)S(1)}, bf16[128,128]{1,0:T(8,128)(2,1)}, u32[]{:S(2)}) copy-start(bf16[128,128]{1,0:T(8,128)(2,1)} %param.9) | copy-start | bytes 98308
  2.7 60.9 %all-to-all-start = ((bf16[16,64,8,128]{3,2,1,0:T(8,128)(2,1)}), bf16[16,64,8,128]{3,2,1,0:T(8,128)(2,1)S(1)}, u32[]{:S(2)}, u32[]{:S(2)}) async-start(bf16[16,64,8,128]{3,2,1,0:T(8,128)(2,1)} %cut.1), calls=%async_computation | async-start | bytes 4194304 | tf_op jit(solution)/shard_map/all_to_all | solution.py:390
  63.6 1.3 copy-start.5
  69.0 7.5 %copy-start.2 = (f32[256,32]{1,0:T(8,128)S(1)}, f32[256,32]{1,0:T(8,128)}, u32[]{:S(2)}) copy-start(f32[256,32]{1,0:T(8,128)} %constant.218.clone.table_y_ref.table_x_ref) | copy-start | bytes 98308
  69.0 7.5 %copy-start.3 = (bf16[32,128]{1,0:T(8,128)(2,1)S(1)}, bf16[32,128]{1,0:T(8,128)(2,1)}, u32[]{:S(2)}) copy-start(bf16[32,128]{1,0:T(8,128)(2,1)} %constant.222.table_x_ref) | copy-start | bytes 24580
  69.0 86.4 %all-to-all-start.1 = ((bf16[16,8,64,128]{3,2,1,0:T(8,128)(2,1)}), bf16[16,8,64,128]{3,2,1,0:T(8,128)(2,1)S(1)}, u32[]{:S(2)}, u32[]{:S(2)}) async-start(bf16[16,8,64,128]{3,2,1,0:T(8,128)(2,1)} %get-tuple-element.7), calls=%async_computation.1 | async-start | bytes 4194304 | tf_op jit(solution)/shard_map/all_to_all | solution.py:398
  76.4 1.6 copy-start
  80.6 51.2 %copy-start.7 = (f32[128]{0:T(128)S(1)}, f32[128]{0:T(128)}, u32[]{:S(2)}) copy-start(f32[128]{0:T(128)} %param.10) | copy-start | bytes 1540
  80.7 1.9 %collective-permute-start = (f32[2,2,2,2,8,256]{5,4,3,2,1,0:T(8,128)S(1)}, f32[2,2,2,2,8,256]{5,4,3,2,1,0:T(8,128)S(1)}, u32[]{:S(2)}, u32[]{:S(2)}) collective-permute-start(f32[2,2,2,2,8,256]{5,4,3,2,1,0:T(8,128)S(1)} %dynamic-slice_bitcast_fusion), channel_id=1, source_target_pairs={{0,16},{16,0},{32,48},{48,32},{64,80},{80,64},{96,112},{112,96},{1... | collective-permute-start | bytes 393224 | tf_op jit(solution)/shard_map/ppermute | solution.py:78
  82.6 67.2 %copy-start.4 = (f32[2,16,128]{2,1,0:T(8,128)S(1)}, f32[2,16,128]{2,1,0:T(8,128)}, u32[]{:S(2)}) copy-start(f32[2,16,128]{2,1,0:T(8,128)} %constant.219.clone.waves_y_ref) | copy-start | bytes 49156
  82.7 5.0 %collective-permute-start.1 = (f32[2,2,2,8,256]{4,3,2,1,0:T(8,128)S(1)}, f32[2,2,2,8,256]{4,3,2,1,0:T(8,128)S(1)}, u32[]{:S(2)}, u32[]{:S(2)}) collective-permute-start(f32[2,2,2,8,256]{4,3,2,1,0:T(8,128)S(1)} %dynamic-slice_bitcast_fusion.1), channel_id=1, source_target_pairs={{0,64},{16,80},{32,96},{48,112},{64,0},{80,16},{96,32},{112,48},{1... | collective-permute-start | bytes 196616 | tf_op jit(solution)/shard_map/ppermute | solution.py:78
  87.7 3.1 %collective-permute-start.2 = (f32[2,2,8,256]{3,2,1,0:T(8,128)S(1)}, f32[2,2,8,256]{3,2,1,0:T(8,128)S(1)}, u32[]{:S(2)}, u32[]{:S(2)}) collective-permute-start(f32[2,2,8,256]{3,2,1,0:T(8,128)S(1)} %dynamic-slice_bitcast_fusion.2), channel_id=1, source_target_pairs={{0,32},{16,48},{32,0},{48,16},{64,96},{80,112},{96,64},{112,80},{1... | collective-permute-start | bytes 98312 | tf_op jit(solution)/shard_map/ppermute | solution.py:78
  90.9 3.0 %collective-permute-start.3 = (f32[2,8,256]{2,1,0:T(8,128)S(1)}, f32[2,8,256]{2,1,0:T(8,128)S(1)}, u32[]{:S(2)}, u32[]{:S(2)}) collective-permute-start(f32[2,8,256]{2,1,0:T(8,128)S(1)} %dynamic-slice_bitcast_fusion.3), channel_id=1, source_target_pairs={{0,128},{16,144},{32,160},{48,176},{64,192},{80,208},{96,224},{112... | collective-permute-start | bytes 49160 | tf_op jit(solution)/shard_map/ppermute | solution.py:78
  93.8 4.6 %collective-permute-start.4 = (bf16[4,8,128]{2,1,0:T(8,128)(2,1)S(1)}, bf16[4,8,128]{2,1,0:T(8,128)(2,1)S(1)}, u32[]{:S(2)}, u32[]{:S(2)}) collective-permute-start(bf16[4,8,128]{2,1,0:T(8,128)(2,1)S(1)} %bitcast.47), channel_id=1, source_target_pairs={{0,8},{1,9},{2,10},{3,11},{4,12},{5,13},{6,14},{7,15},{8,0},{9,1},... | collective-permute-start | bytes 24584 | tf_op jit(solution)/shard_map/ppermute | solution.py:394
  98.4 24.8 %collective-permute-start.11 = (bf16[2,4,8,128]{3,2,1,0:T(8,128)(2,1)S(1)}, bf16[2,4,8,128]{3,2,1,0:T(8,128)(2,1)S(1)}, u32[]{:S(2)}, u32[]{:S(2)}) collective-permute-start(bf16[2,4,8,128]{3,2,1,0:T(8,128)(2,1)S(1)} %pad_maximum_fusion.3.refs_0_), channel_id=1, source_target_pairs={{0,7},{1,0},{2,1},{3,2},{4,3},{5,4},{6,5},{7,6},{8,15},{9,8},{10,9... | collective-permute-start | bytes 49160 | tf_op jit(solution)/shard_map/ppermute | solution.py:396
  101.5 23.6 %collective-permute-start.10 = (bf16[2,4,8,128]{3,2,1,0:T(8,128)(2,1)S(1)}, bf16[2,4,8,128]{3,2,1,0:T(8,128)(2,1)S(1)}, u32[]{:S(2)}, u32[]{:S(2)}) collective-permute-start(bf16[2,4,8,128]{3,2,1,0:T(8,128)(2,1)S(1)} %pad_maximum_fusion.3.refs_0_), channel_id=1, source_target_pairs={{0,6},{1,7},{2,0},{3,1},{4,2},{5,3},{6,4},{7,5},{8,14},{9,15},{10,... | collective-permute-start | bytes 49160 | tf_op jit(solution)/shard_map/ppermute | solution.py:396
  103.4 24.5 %collective-permute-start.9 = (bf16[2,4,8,128]{3,2,1,0:T(8,128)(2,1)S(1)}, bf16[2,4,8,128]{3,2,1,0:T(8,128)(2,1)S(1)}, u32[]{:S(2)}, u32[]{:S(2)}) collective-permute-start(bf16[2,4,8,128]{3,2,1,0:T(8,128)(2,1)S(1)} %pad_maximum_fusion.3.refs_0_), channel_id=1, source_target_pairs={{0,5},{1,6},{2,7},{3,0},{4,1},{5,2},{6,3},{7,4},{8,13},{9,14},{10,... | collective-permute-start | bytes 49160 | tf_op jit(solution)/shard_map/ppermute | solution.py:396
  104.5 23.3 %collective-permute-start.8 = (bf16[2,4,8,128]{3,2,1,0:T(8,128)(2,1)S(1)}, bf16[2,4,8,128]{3,2,1,0:T(8,128)(2,1)S(1)}, u32[]{:S(2)}, u32[]{:S(2)}) collective-permute-start(bf16[2,4,8,128]{3,2,1,0:T(8,128)(2,1)S(1)} %pad_maximum_fusion.3.refs_0_), channel_id=1, source_target_pairs={{0,4},{1,5},{2,6},{3,7},{4,0},{5,1},{6,2},{7,3},{8,12},{9,13},{10,... | collective-permute-start | bytes 49160 | tf_op jit(solution)/shard_map/ppermute | solution.py:396
  108.4 19.5 %collective-permute-start.7 = (bf16[2,4,8,128]{3,2,1,0:T(8,128)(2,1)S(1)}, bf16[2,4,8,128]{3,2,1,0:T(8,128)(2,1)S(1)}, u32[]{:S(2)}, u32[]{:S(2)}) collective-permute-start(bf16[2,4,8,128]{3,2,1,0:T(8,128)(2,1)S(1)} %pad_maximum_fusion.3.refs_0_), channel_id=1, source_target_pairs={{0,3},{1,4},{2,5},{3,6},{4,7},{5,0},{6,1},{7,2},{8,11},{9,12},{10,... | collective-permute-start | bytes 49160 | tf_op jit(solution)/shard_map/ppermute | solution.py:396
  123.3 5.0 %collective-permute-start.6 = (bf16[2,4,8,128]{3,2,1,0:T(8,128)(2,1)S(1)}, bf16[2,4,8,128]{3,2,1,0:T(8,128)(2,1)S(1)}, u32[]{:S(2)}, u32[]{:S(2)}) collective-permute-start(bf16[2,4,8,128]{3,2,1,0:T(8,128)(2,1)S(1)} %pad_maximum_fusion.3.refs_0_), channel_id=1, source_target_pairs={{0,2},{1,3},{2,4},{3,5},{4,6},{5,7},{6,0},{7,1},{8,10},{9,11},{10,... | collective-permute-start | bytes 49160 | tf_op jit(solution)/shard_map/ppermute | solution.py:396
  125.1 3.8 %collective-permute-start.5 = (bf16[2,4,8,128]{3,2,1,0:T(8,128)(2,1)S(1)}, bf16[2,4,8,128]{3,2,1,0:T(8,128)(2,1)S(1)}, u32[]{:S(2)}, u32[]{:S(2)}) collective-permute-start(bf16[2,4,8,128]{3,2,1,0:T(8,128)(2,1)S(1)} %pad_maximum_fusion.3.refs_0_), channel_id=1, source_target_pairs={{0,1},{1,2},{2,3},{3,4},{4,5},{5,6},{6,7},{7,0},{8,9},{9,10},{10,1... | collective-permute-start | bytes 49160 | tf_op jit(solution)/shard_map/ppermute | solution.py:396
  128.9 1.6 copy-start.1
  131.5 2.7 %collective-permute-start.12 = (f32[1,2,8,256]{3,2,1,0:T(8,128)S(1)}, f32[1,2,8,256]{3,2,1,0:T(8,128)S(1)}, u32[]{:S(2)}, u32[]{:S(2)}) collective-permute-start(f32[1,2,8,256]{3,2,1,0:T(8,128)S(1)} %bitcast.42), channel_id=1, source_target_pairs={{0,128},{16,144},{32,160},{48,176},{64,192},{80,208},{96,224},{112... | collective-permute-start | bytes 49160 | tf_op jit(solution)/shard_map/ppermute | solution.py:93
  134.1 2.8 %collective-permute-start.13 = (f32[2,2,8,256]{3,2,1,0:T(8,128)S(1)}, f32[2,2,8,256]{3,2,1,0:T(8,128)S(1)}, u32[]{:S(2)}, u32[]{:S(2)}) collective-permute-start(f32[2,2,8,256]{3,2,1,0:T(8,128)S(1)} %pad_maximum_fusion.2), channel_id=1, source_target_pairs={{0,32},{16,48},{32,0},{48,16},{64,96},{80,112},{96,64},{112,80},{1... | collective-permute-start | bytes 98312 | tf_op jit(solution)/shard_map/ppermute | solution.py:93
  136.9 4.6 %collective-permute-start.14 = (f32[4,2,8,256]{3,2,1,0:T(8,128)S(1)}, f32[4,2,8,256]{3,2,1,0:T(8,128)S(1)}, u32[]{:S(2)}, u32[]{:S(2)}) collective-permute-start(f32[4,2,8,256]{3,2,1,0:T(8,128)S(1)} %pad_maximum_fusion.1), channel_id=1, source_target_pairs={{0,64},{16,80},{32,96},{48,112},{64,0},{80,16},{96,32},{112,48},{1... | collective-permute-start | bytes 196616 | tf_op jit(solution)/shard_map/ppermute | solution.py:93
  141.5 8.3 %collective-permute-start.15 = (f32[8,2,8,256]{3,2,1,0:T(8,128)S(1)}, f32[8,2,8,256]{3,2,1,0:T(8,128)S(1)}, u32[]{:S(2)}, u32[]{:S(2)}) collective-permute-start(f32[8,2,8,256]{3,2,1,0:T(8,128)S(1)} %pad_maximum_fusion), channel_id=1, source_target_pairs={{0,16},{16,0},{32,48},{48,32},{64,80},{80,64},{96,112},{112,96},{1... | collective-permute-start | bytes 393224 | tf_op jit(solution)/shard_map/ppermute | solution.py:93

commit v4 on v3

--- a/solution.py
+++ b/solution.py
@@ -12,6 +12,8 @@
 GRID = 128
 KEEP = 16
 BLOCKS = 16
+LATE = 16
+EARLY = 64 - LATE
 PRECISE = lax.Precision.HIGHEST
 CELL_SCALE = 2.0**20
 COEF_SCALE = 2.0**6
@@ -90,7 +92,8 @@
 def slab_gather(value):
     value = value[None]
     for step in ((1, 0, 0), (0, 1, 0), (0, 2, 0), (0, 0, 1)):
-        value = jnp.concatenate([value, lax.ppermute(value, "slab", slab_perm(*step))], 0)
+        other = lax.ppermute(value, "slab", slab_perm(*step))
+        value = jnp.concatenate([value, other], 0)
     return value
 
 
@@ -139,7 +142,8 @@
     )(field, table_x, table_y, depth)
 
 
-def cut_kernel(field_ref, out_ref, block_ref, turned_ref, fetched, stored):
+def cut_kernel(field_ref, early_ref, own_ref, other_ref, block_ref, turned_ref, late_ref, fetched, stored):
+    x_hi = lax.shift_right_logical(lax.axis_index("chan"), 3)
     parts = fetched.shape[0]
     span = BLOCKS // parts
     fetches, stores = [], []
@@ -151,10 +155,14 @@
         fetches[part].wait()
         for p in range(part * span, (part + 1) * span):
             block = block_ref[:, p].astype(jnp.float32)
-            turned_ref[p] = block.transpose(1, 0, 2).astype(jnp.bfloat16)
+            turned = block.transpose(1, 0, 2).astype(jnp.bfloat16)
+            turned_ref[p] = turned[:EARLY]
+            late_ref[lax.bitwise_xor(x_hi, p // 8), p % 8] = turned[EARLY:]
         blocks = pl.ds(part * span, span)
-        stores.append(pltpu.make_async_copy(turned_ref.at[blocks], out_ref.at[blocks], stored.at[part]))
+        stores.append(pltpu.make_async_copy(turned_ref.at[blocks], early_ref.at[blocks], stored.at[part]))
         stores[part].start()
+    own_ref[...] = late_ref[0]
+    other_ref[...] = late_ref[1]
     for store in stores:
         store.wait()
 
@@ -164,12 +172,14 @@
     in_place = pl.BlockSpec(memory_space=pltpu.HBM)
     return pl.pallas_call(
         cut_kernel,
-        out_shape=pltpu.HBM((BLOCKS, 64, 8, 128), jnp.bfloat16),
+        out_shape=[pltpu.HBM((BLOCKS, EARLY, 8, 128), jnp.bfloat16)]
+        + [jax.ShapeDtypeStruct((8, LATE, 8, 128), jnp.bfloat16)] * 2,
         in_specs=[in_place],
-        out_specs=in_place,
+        out_specs=[in_place, WHOLE, WHOLE],
         scratch_shapes=[
             pltpu.VMEM((8, BLOCKS, 64, 128), jnp.bfloat16),
-            pltpu.VMEM((BLOCKS, 64, 8, 128), jnp.bfloat16),
+            pltpu.VMEM((BLOCKS, EARLY, 8, 128), jnp.bfloat16),
+            pltpu.VMEM((2, 8, LATE, 8, 128), jnp.bfloat16),
             pltpu.SemaphoreType.DMA((parts,)),
             pltpu.SemaphoreType.DMA((parts,)),
         ],
@@ -179,27 +189,30 @@
     )(blocks)
 
 
+def map_rows(weight_ref, cells_ref, first):
+    coded = []
+    for x in range(first, first + 8, 2):
+        pair = [cells_ref[:, x + near].reshape(128, 128) for near in range(2)]
+        mapped = jnp.dot(weight_ref[...], jnp.concatenate(pair, 1), preferred_element_type=jnp.float32)
+        mapped = mapped * jnp.abs(mapped) * (mapped * mapped)
+        coded += [mapped[:, :128], mapped[:, 128:]]
+    turned = jnp.stack(coded, 0).transpose(1, 0, 2)
+    return turned.reshape(BLOCKS, 8, 8, 128).astype(jnp.bfloat16)
+
+
 def map_kernel(weight_ref, cells_ref, out_ref, kept_ref, block_ref, held_ref, fetched, stored):
     del kept_ref
-    parts = fetched.shape[0]
-    rows = 64 // parts
     fetches, stores = [], []
-    for part in range(parts):
-        span = pl.ds(part * rows, rows)
+    spans = [(0, EARLY % 16)] * (EARLY % 16 > 0) + [(first, 16) for first in range(EARLY % 16, EARLY, 16)]
+    for part, (first, rows) in enumerate(spans):
+        span = pl.ds(first, rows)
         fetches.append(pltpu.make_async_copy(cells_ref.at[:, span], block_ref.at[:, span], fetched.at[part]))
         fetches[part].start()
-    for part in range(parts):
+    for part, (start, rows) in enumerate(spans):
         fetches[part].wait()
-        for first in range(part * rows, (part + 1) * rows, 8):
-            coded = []
-            for x in range(first, first + 8, 2):
-                pair = [block_ref[:, x + near].reshape(128, 128) for near in range(2)]
-                mapped = jnp.dot(weight_ref[...], jnp.concatenate(pair, 1), preferred_element_type=jnp.float32)
-                mapped = mapped * jnp.abs(mapped) * (mapped * mapped)
-                coded += [mapped[:, :128], mapped[:, 128:]]
-            turned = jnp.stack(coded, 0).transpose(1, 0, 2)
-            held_ref[:, :, pl.ds(first, 8), :] = turned.reshape(BLOCKS, 8, 8, 128).astype(jnp.bfloat16)
-        span = pl.ds(part * rows, rows)
+        for first in range(start, start + rows, 8):
+            held_ref[:, :, pl.ds(first, 8), :] = map_rows(weight_ref, block_ref, first)
+        span = pl.ds(start, rows)
         stores.append(
             pltpu.make_async_copy(held_ref.at[:, :, span, :], out_ref.at[:, :, span, :], stored.at[part])
         )
@@ -208,32 +221,99 @@
         store.wait()
 
 
-def pointwise_map(weight, cells):
-    parts = 4
+def map_early(weight, cells):
     in_place = pl.BlockSpec(memory_space=pltpu.HBM)
     return pl.pallas_call(
         map_kernel,
         out_shape=[
-            pltpu.HBM((BLOCKS, 8, 64, 128), jnp.bfloat16),
-            pltpu.HBM((BLOCKS, 64, 8, 128), jnp.bfloat16),
+            pltpu.HBM((BLOCKS, 8, EARLY, 128), jnp.bfloat16),
+            pltpu.HBM((BLOCKS, EARLY, 8, 128), jnp.bfloat16),
         ],
         in_specs=[WHOLE, in_place],
         out_specs=[in_place] * 2,
         scratch_shapes=[
-            pltpu.VMEM((BLOCKS, 64, 8, 128), jnp.bfloat16),
-            pltpu.VMEM((BLOCKS, 8, 64, 128), jnp.bfloat16),
-            pltpu.SemaphoreType.DMA((parts,)),
-            pltpu.SemaphoreType.DMA((parts,)),
+            pltpu.VMEM((BLOCKS, EARLY, 8, 128), jnp.bfloat16),
+            pltpu.VMEM((BLOCKS, 8, EARLY, 128), jnp.bfloat16),
+            pltpu.SemaphoreType.DMA((4,)),
+            pltpu.SemaphoreType.DMA((4,)),
         ],
         input_output_aliases={1: 1},
         cost_estimate=pl.CostEstimate(flops=270_000_000, bytes_accessed=4_000_000, transcendentals=0),
         compiler_params=pltpu.CompilerParams(vmem_limit_bytes=10 << 20),
-        name="pointwise_map",
-    )(weight * jnp.bfloat16(CELL_SCALE), cells)[0]
+        name="map_early",
+    )(weight, cells)[0]
 
 
 def source_block(place_ref, k, h):
     return lax.bitwise_xor(place_ref[1], h) * 8 + lax.rem(place_ref[0] + (8 - k), 8)
+
+
+def pack_kernel(place_ref, own_cells_ref, other_cells_ref, own_coef_ref, other_coef_ref, *letters):
+    for k in range(8):
+        target = lax.rem(place_ref[0] + k, 8)
+        for h, (cells_ref, coef_ref) in enumerate(
+            ((own_cells_ref, own_coef_ref), (other_cells_ref, other_coef_ref))
+        ):
+            letters[k][h, :LATE] = cells_ref[target]
+            letters[k][h, LATE:] = coef_ref[...]
+
+
+def pack(place, own_cells, other_cells, own_coef, other_coef):
+    return pl.pallas_call(
+        pack_kernel,
+        out_shape=[jax.ShapeDtypeStruct((2, LATE + 4, 8, 128), jnp.bfloat16)] * 8,
+        in_specs=[SCALARS] + [WHOLE] * 4,
+        out_specs=[WHOLE] * 8,
+        cost_estimate=pl.CostEstimate(flops=0, bytes_accessed=800_000, transcendentals=0),
+        compiler_params=pltpu.CompilerParams(vmem_limit_bytes=4 << 20),
+        name="pack",
+    )(place, own_cells, other_cells, own_coef, other_coef)
+
+
+def map_late_kernel(place_ref, weight_ref, *refs):
+    letters, own_ref, other_ref, cells_ref, held_ref = refs[:8], refs[8], refs[9], refs[10], refs[11]
+    for k in range(8):
+        for h in range(2):
+            cells_ref[source_block(place_ref, k, h)] = letters[k][h, :LATE]
+    for first in range(0, LATE, 8):
+        held_ref[:, :, pl.ds(first, 8), :] = map_rows(weight_ref, cells_ref, first)
+    own_ref[...] = held_ref[pl.ds(place_ref[1] * 8, 8)]
+    other_ref[...] = held_ref[pl.ds(8 - place_ref[1] * 8, 8)]
+
+
+def map_late(place, weight, letters):
+    return pl.pallas_call(
+        map_late_kernel,
+        out_shape=[jax.ShapeDtypeStruct((8, 8, LATE, 128), jnp.bfloat16)] * 2,
+        in_specs=[SCALARS] + [WHOLE] * 9,
+        out_specs=[WHOLE] * 2,
+        scratch_shapes=[
+            pltpu.VMEM((BLOCKS, LATE, 8, 128), jnp.bfloat16),
+            pltpu.VMEM((BLOCKS, 8, LATE, 128), jnp.bfloat16),
+        ],
+        cost_estimate=pl.CostEstimate(flops=40_000_000, bytes_accessed=600_000, transcendentals=0),
+        compiler_params=pltpu.CompilerParams(vmem_limit_bytes=6 << 20),
+        name="map_late",
+    )(place, weight, *letters)
+
+
+def sort_kernel(place_ref, own_ref, other_ref, *letters):
+    for k in range(8):
+        target = lax.rem(place_ref[0] + k, 8)
+        letters[k][0] = own_ref[target]
+        letters[k][1] = other_ref[target]
+
+
+def sort(place, own, other):
+    return pl.pallas_call(
+        sort_kernel,
+        out_shape=[jax.ShapeDtypeStruct((2, 8, LATE, 128), jnp.bfloat16)] * 8,
+        in_specs=[SCALARS] + [WHOLE] * 2,
+        out_specs=[WHOLE] * 8,
+        cost_estimate=pl.CostEstimate(flops=0, bytes_accessed=600_000, transcendentals=0),
+        compiler_params=pltpu.CompilerParams(vmem_limit_bytes=4 << 20),
+        name="sort",
+    )(place, own, other)
 
 
 def mix_kernel(place_ref, *refs):
@@ -242,7 +322,7 @@
         for h in range(2):
             for part in range(2):
                 for side in range(2):
-                    coded = letters[k][h, part * 2 + side]
+                    coded = letters[k][h, LATE + part * 2 + side]
                     coef_ref[k * 2 + h, part, :, pl.ds(side * 128, 128)] = decode(coded, COEF_SCALE)
     for o in range(8):
         real = jnp.zeros((8, 256), jnp.float32)
@@ -273,7 +353,8 @@
     )(place, *letters, spec_weight)
 
 
-def inverse_kernel(me_ref, bias_ref, spec_ref, depth_ref, table_x_ref, waves_y_ref, out_ref, plane_ref, line_ref, table_ref):
+def inverse_kernel(me_ref, bias_ref, spec_ref, depth_ref, table_x_ref, waves_y_ref, out_ref, late_ref, *scratch):
+    plane_ref, line_ref, table_ref, held_ref, stored = scratch
     row = lax.broadcasted_iota(jnp.int32, (256, 256), 0)
     lane = lax.broadcasted_iota(jnp.int32, (256, 256), 1)
     table_z = jnp.where(row // KEEP == lane % KEEP, jnp.concatenate([depth_ref[...]] * KEEP, 0), 0.0)
@@ -293,6 +374,7 @@
         for part in range(2):
             table_ref[pl.ds(part * 128 + z * 16, 16), pl.ds(z * 128, 128)] = waves_y_ref[part]
     line_high, line_low = split(line_ref[...])
+    stores = []
     for z in range(0, 8, 2):
         high, low = split(table_ref[:, z * 128 : (z + 2) * 128])
         field = jnp.dot(line_high, low, preferred_element_type=jnp.float32)
@@ -300,8 +382,17 @@
         field += jnp.dot(line_high, high, preferred_element_type=jnp.float32)
         for o in range(8):
             rows = slice(o * 128, (o + 1) * 128)
-            out_ref[o, z] = field[rows, :128] + bias_ref[o]
-            out_ref[o, z + 1] = field[rows, 128:] + bias_ref[o]
+            for near in range(2):
+                plane = field[rows, near * 128 : (near + 1) * 128] + bias_ref[o]
+                for half in range(2):
+                    block = (z + near) * 2 + half
+                    held_ref[o, block] = plane[half * 64 : half * 64 + EARLY]
+                    late_ref[o, block] = plane[half * 64 + EARLY : (half + 1) * 64]
+        blocks = pl.ds(z * 2, 4)
+        stores.append(pltpu.make_async_copy(held_ref.at[:, blocks], out_ref.at[:, blocks], stored.at[z // 2]))
+        stores[z // 2].start()
+    for store in stores:
+        store.wait()
 
 
 def inverse_transform(me, bias, spectrum, first_cell):
@@ -315,13 +406,18 @@
     depth = jnp.where(lane < 128, jnp.cos(angle), jnp.sin(angle)) * fold
     return pl.pallas_call(
         inverse_kernel,
-        out_shape=pltpu.HBM((8, 8, 128, 128), jnp.float32),
+        out_shape=[
+            pltpu.HBM((8, BLOCKS, EARLY, 128), jnp.float32),
+            jax.ShapeDtypeStruct((8, BLOCKS, LATE, 128), jnp.float32),
+        ],
         in_specs=[SCALARS] * 2 + [WHOLE] * 4,
-        out_specs=WHOLE,
+        out_specs=[pl.BlockSpec(memory_space=pltpu.HBM), WHOLE],
         scratch_shapes=[
             pltpu.VMEM((32, 8, 128), jnp.float32),
             pltpu.VMEM((1024, 256), jnp.float32),
             pltpu.VMEM((256, 1024), jnp.float32),
+            pltpu.VMEM((8, BLOCKS, EARLY, 128), jnp.float32),
+            pltpu.SemaphoreType.DMA((4,)),
         ],
         cost_estimate=pl.CostEstimate(flops=2_000_000_000, bytes_accessed=5_000_000, transcendentals=0),
         compiler_params=pltpu.CompilerParams(vmem_limit_bytes=16 << 20),
@@ -335,7 +431,7 @@
     return (half + half * lax.erf(total * (math.sqrt(0.5) / CELL_SCALE))).astype(jnp.bfloat16)
 
 
-def finish_kernel(coded_ref, inverse_ref, out_ref, kept_ref, field_ref, done_ref, fetched, stored):
+def finish_early_kernel(coded_ref, inverse_ref, out_ref, kept_ref, field_ref, done_ref, fetched, stored):
     del kept_ref
     parts = fetched.shape[0]
     span = BLOCKS // parts
@@ -350,34 +446,69 @@
             for p in range(part * span, (part + 1) * span):
                 done_ref[o, p] = activate(coded_ref[p, o], field_ref[o, p])
         blocks = pl.ds(part * span, span)
-        stores.append(pltpu.make_async_copy(done_ref.at[:, blocks], out_ref.at[:, blocks], stored.at[part]))
+        target = out_ref.at[:, blocks, pl.ds(0, EARLY), :]
+        stores.append(pltpu.make_async_copy(done_ref.at[:, blocks], target, stored.at[part]))
         stores[part].start()
     for store in stores:
         store.wait()
 
 
-def finish(coded, inverse):
+def finish_early(coded, inverse):
     parts = 8
     in_place = pl.BlockSpec(memory_space=pltpu.HBM)
     return pl.pallas_call(
-        finish_kernel,
+        finish_early_kernel,
         out_shape=[
             pltpu.HBM((8, BLOCKS, 64, 128), jnp.bfloat16),
-            pltpu.HBM((8, BLOCKS, 64, 128), jnp.float32),
+            pltpu.HBM((8, BLOCKS, EARLY, 128), jnp.float32),
         ],
         in_specs=[WHOLE, in_place],
         out_specs=[in_place] * 2,
         scratch_shapes=[
-            pltpu.VMEM((8, BLOCKS, 64, 128), jnp.float32),
-            pltpu.VMEM((8, BLOCKS, 64, 128), jnp.bfloat16),
+            pltpu.VMEM((8, BLOCKS, EARLY, 128), jnp.float32),
+            pltpu.VMEM((8, BLOCKS, EARLY, 128), jnp.bfloat16),
             pltpu.SemaphoreType.DMA((parts,)),
             pltpu.SemaphoreType.DMA((parts,)),
         ],
         input_output_aliases={1: 1},
         cost_estimate=pl.CostEstimate(flops=30_000_000, bytes_accessed=8_000_000, transcendentals=0),
         compiler_params=pltpu.CompilerParams(vmem_limit_bytes=12 << 20),
-        name="finish",
+        name="finish_early",
     )(coded, inverse)[0]
+
+
+def finish_late_kernel(place_ref, inverse_ref, *refs):
+    letters, out_ref, done_ref, stored = refs[:8], refs[9], refs[10], refs[11]
+    for k in range(8):
+        for h in range(2):
+            block = source_block(place_ref, k, h)
+            for o in range(8):
+                done_ref[o, block] = activate(letters[k][h, o], inverse_ref[o, block])
+    store = pltpu.make_async_copy(done_ref, out_ref.at[:, :, pl.ds(EARLY, LATE), :], stored)
+    store.start()
+    store.wait()
+
+
+def finish_late(place, inverse, letters, partial):
+    in_place = pl.BlockSpec(memory_space=pltpu.HBM)
+    return pl.pallas_call(
+        finish_late_kernel,
+        out_shape=pltpu.HBM((8, BLOCKS, 64, 128), jnp.bfloat16),
+        in_specs=[SCALARS] + [WHOLE] * 9 + [in_place],
+        out_specs=in_place,
+        scratch_shapes=[pltpu.VMEM((8, BLOCKS, LATE, 128), jnp.bfloat16), pltpu.SemaphoreType.DMA],
+        input_output_aliases={10: 0},
+        cost_estimate=pl.CostEstimate(flops=4_000_000, bytes_accessed=1_200_000, transcendentals=0),
+        compiler_params=pltpu.CompilerParams(vmem_limit_bytes=6 << 20),
+        name="finish_late",
+    )(place, inverse, *letters, partial)
+
+
+def z_letters(letters):
+    arrived = [letters[0]]
+    for k in range(1, 8):
+        arrived.append(lax.ppermute(letters[k], "chan", chan_perm(0, k)))
+    return arrived
 
 
 def on_device(field, local_weight, bias, spec_weight):
@@ -387,21 +518,29 @@
     place = jnp.stack([chan % 8, x_hi]).astype(jnp.int32)
     planes = field[0]
     blocks = planes.reshape(8, BLOCKS, 64, 128)
-    cells = lax.all_to_all(cut(blocks), "chan", 0, 0, tiled=True)
+    weight = local_weight * jnp.bfloat16(CELL_SCALE)
+    cells, own_cells, other_cells = cut(blocks)
+    cells = lax.all_to_all(cells, "chan", 0, 0, tiled=True)
+    other_cells = lax.ppermute(other_cells, "chan", chan_perm(1, 0))
     partial = forward_transform(planes, first_cell)
     owned = slab_sum(partial)
     own_coef = encode(owned, COEF_SCALE).reshape(2, 8, 2, 128).transpose(0, 2, 1, 3).reshape(4, 8, 128)
     other_coef = lax.ppermute(own_coef, "chan", chan_perm(1, 0))
-    letter = jnp.stack([own_coef, other_coef], 0)
-    letters = [letter] + [lax.ppermute(letter, "chan", chan_perm(0, k)) for k in range(1, 8)]
-    coded = pointwise_map(local_weight, cells)
+    letters = pack(place, own_cells, other_cells, own_coef, other_coef)
+    letters = z_letters(letters)
+    coded = map_early(weight, cells)
     coded = lax.all_to_all(coded, "chan", 0, 0, tiled=True)
     mixed = mix(place, letters, spec_weight)
+    own_late, other_late = map_late(place, weight, letters)
+    other_late = lax.ppermute(other_late, "chan", chan_perm(1, 0))
+    answers = sort(place, own_late, other_late)
+    answers = z_letters(answers)
     spectrum = slab_gather(mixed)
     me = jnp.reshape(slab, (1,)).astype(jnp.int32)
     offset = lax.dynamic_slice_in_dim(bias, chan * 8, 8, 0)
-    inverse = inverse_transform(me, offset, spectrum, first_cell).reshape(8, BLOCKS, 64, 128)
-    done = finish(coded, inverse)
+    inverse, inverse_late = inverse_transform(me, offset, spectrum, first_cell)
+    done = finish_early(coded, inverse)
+    done = finish_late(place, inverse_late, answers, done)
     return done.reshape(1, 8, 8, 128, 128)
 
 

time: 160 us -> 159 us (level)
  waiting for transfers between devices: 80.3 us -> 64.1 us
  starting transfers between devices: 53.8 us -> 67.8 us
  Pallas kernels: 19.8 us -> 23.5 us
  local copies, waits for them, and re-layouts: 4.6 us -> 1.73 us
    all_to_all x1, waiting for transfers between devices: 49.2 us -> 25.6 us  [on_device(): cells = lax.all_to_all(cells, 'chan', 0, 0, tiled=True)]
    ppermute x11 -> x20, starting transfers between devices: 26.1 us -> 40.5 us  [the longest x14 24.9 us: z_letters(): arrived.append(lax.ppermute(letters[k], 'chan', chan_perm(0, k)))]
    ppermute x11 -> x20, waiting for transfers between devices: 22.4 us -> 30.2 us  [the longest x14 26 us: z_letters(): arrived.append(lax.ppermute(letters[k], 'chan', chan_perm(0, k)))]
    pallas_call x4 -> x8, Pallas kernels: 16.3 us -> 20 us  [the longest x1 4.88 us: inverse_transform(): pl.pallas_call(inverse_kernel, out_shape=[pltpu.HBM((8, BLOCKS, EARLY, 12...]
    unnamed x20 -> x22, local copies, waits for them, and re-layouts: 4.54 us -> 1.64 us
  transfers between devices with their start and end apart: 18 -> 27, of which waited for: 14 -> 11; matrix products, arithmetic and copies ran while one was open for 0% -> 0% of each run, Pallas kernels for 6% -> 12%
where the time goes in v4:
time: 159 us; the launch traced here: 158 us
  starting transfers between devices  67.8 us (43%)
  waiting for transfers between devices  64.1 us (40%)
  Pallas kernels  23.5 us (15%)
  local copies, waits for them, and re-layouts  1.73 us (1%)
    ppermute x14, waiting for transfers between devices, z_letters(): arrived.append(lax.ppermute(letters[k], 'chan', chan_perm(0, k)))  26 us
    all_to_all x1, waiting for transfers between devices, on_device(): cells = lax.all_to_all(cells, 'chan', 0, 0, tiled=True)  25.6 us
    ppermute x14, starting transfers between devices, z_letters(): arrived.append(lax.ppermute(letters[k], 'chan', chan_perm(0, k)))  24.9 us
    all_to_all x1, starting transfers between devices, on_device(): cells = lax.all_to_all(cells, 'chan', 0, 0, tiled=True)  11.8 us
    ppermute x4, starting transfers between devices, slab_gather(): other = lax.ppermute(value, 'slab', slab_perm(*step))  9.9 us
    all_to_all x1, starting transfers between devices, on_device(): coded = lax.all_to_all(coded, 'chan', 0, 0, tiled=True)  6.76 us
    ppermute x4, waiting for transfers between devices, halve(): return own + lax.ppermute(other, 'slab', perm)  6.13 us
    ppermute x4, starting transfers between devices, halve(): return own + lax.ppermute(other, 'slab', perm)  5.83 us
  transfers between devices with their start and end apart: 27, of which 11 were waited for; matrix products, arithmetic and copies ran while one was open for 0% of the time, Pallas kernels for 12%

profile of v4, /device:TPU:1, one launch (start us, length us, event | category | flops | bytes accessed | tf_op | source)
XLA Modules:
  0.0 158.3 jit_solution(16491351304950966776)
XLA Ops:
  0.0 3.5 %cut.1 = (bf16[16,48,8,128]{3,2,1,0:T(8,128)(2,1)}, bf16[8,16,8,128]{3,2,1,0:T(8,128)(2,1)}, bf16[8,16,8,128]{3,2,1,0:T(8,128)(2,1)}) custom-call(bf16[8,16,64,128]{3,2,1,0:T(8,128)(2,1)} %bitcast.31), custom_call_target="tpu_custom_call" | custom-call | flops 1000000 | bytes 4000000 | tf_op jit(solution)/shard_map/cut/pallas_call | solution.py:173
  3.5 11.8 %all-to-all-start = ((bf16[16,48,8,128]{3,2,1,0:T(8,128)(2,1)}), bf16[16,48,8,128]{3,2,1,0:T(8,128)(2,1)}, u32[]{:S(2)}, u32[]{:S(2)}) async-start(bf16[16,48,8,128]{3,2,1,0:T(8,128)(2,1)} %get-tuple-element.51), calls=%async_computation | async-start | bytes 3145728 | tf_op jit(solution)/shard_map/all_to_all | solution.py:523
  15.7 2.6 %forward_transform.1 = f32[16,2,8,256]{3,2,1,0:T(8,128)S(1)} custom-call(bf16[8,8,128,128]{3,2,1,0:T(8,128)(2,1)S(1)} %bitcast.32, bf16[32,128]{1,0:T(8,128)(2,1)S(1)} %copy-done.4, f32[256,32]{1,0:T(8,128)S(1)} %copy-done.3, f32[16,512]{1,0:T(8,128)S(1)} %fusion.3.depth_ref), custom_call_target="tpu_custom_call" | custom-call | flops 200000000 | bytes 3000000 | tf_op jit(solution)/shard_map/forward_transform/pallas_call | solution.py:133
  19.3 3.1 %collective-permute-start = (bf16[8,16,8,128]{3,2,1,0:T(8,128)(2,1)S(1)}, bf16[8,16,8,128]{3,2,1,0:T(8,128)(2,1)S(1)}, u32[]{:S(2)}, u32[]{:S(2)}) collective-permute-start(bf16[8,16,8,128]{3,2,1,0:T(8,128)(2,1)S(1)} %copy-done.7), channel_id=1, source_target_pairs={{0,8},{1,9},{2,10},{3,11},{4,12},{5,13},{6,14},{7,15},{8,0},{9,1},... | collective-permute-start | bytes 786440 | tf_op jit(solution)/shard_map/ppermute | solution.py:524
  22.5 3.0 %collective-permute-start.2 = (f32[2,2,2,8,256]{4,3,2,1,0:T(8,128)S(1)}, f32[2,2,2,8,256]{4,3,2,1,0:T(8,128)S(1)}, u32[]{:S(2)}, u32[]{:S(2)}) collective-permute-start(f32[2,2,2,8,256]{4,3,2,1,0:T(8,128)S(1)} %dynamic-slice_bitcast_fusion), channel_id=1, source_target_pairs={{0,64},{16,80},{32,96},{48,112},{64,0},{80,16},{96,32},{112,48},{1... | collective-permute-start | bytes 196616 | tf_op jit(solution)/shard_map/ppermute | solution.py:80
  25.5 2.1 %collective-permute-done.2 = f32[2,2,2,8,256]{4,3,2,1,0:T(8,128)S(1)} collective-permute-done((f32[2,2,2,8,256]{4,3,2,1,0:T(8,128)S(1)}, f32[2,2,2,8,256]{4,3,2,1,0:T(8,128)S(1)}, u32[]{:S(2)}, u32[]{:S(2)}) %collective-permute-start.2) | collective-permute-done | bytes 65568 | tf_op jit(solution)/shard_map/ppermute | solution.py:80
  27.6 25.6 %all-to-all-done.cells_ref = bf16[16,48,8,128]{3,2,1,0:T(8,128)(2,1)} async-done(((bf16[16,48,8,128]{3,2,1,0:T(8,128)(2,1)}), bf16[16,48,8,128]{3,2,1,0:T(8,128)(2,1)}, u32[]{:S(2)}, u32[]{:S(2)}) %all-to-all-start) | async-done | bytes 1572896 | tf_op jit(solution)/shard_map/all_to_all | solution.py:523
  53.2 3.4 %map_early.1 = (bf16[16,8,48,128]{3,2,1,0:T(8,128)(2,1)}, bf16[16,48,8,128]{3,2,1,0:T(8,128)(2,1)}) custom-call(bf16[128,128]{1,0:T(8,128)(2,1)S(1)} %broadcast_multiply_fusion.weight_ref, bf16[16,48,8,128]{3,2,1,0:T(8,128)(2,1)} %all-to-all-done.cells_ref), custom_call_target="tpu_custom_call", output_to_operand_aliasing={{1}: (1, {})} | custom-call | flops 270000000 | bytes 4000000 | tf_op jit(solution)/shard_map/map_early/pallas_call | solution.py:226
  56.6 6.8 %all-to-all-start.1 = ((bf16[16,8,48,128]{3,2,1,0:T(8,128)(2,1)}), bf16[16,8,48,128]{3,2,1,0:T(8,128)(2,1)S(1)}, u32[]{:S(2)}, u32[]{:S(2)}) async-start(bf16[16,8,48,128]{3,2,1,0:T(8,128)(2,1)} %get-tuple-element.52), calls=%async_computation.1 | async-start | bytes 3145728 | tf_op jit(solution)/shard_map/all_to_all | solution.py:532
  66.7 2.6 %collective-permute-done.4 = f32[2,8,256]{2,1,0:T(8,128)S(1)} collective-permute-done((f32[2,8,256]{2,1,0:T(8,128)S(1)}, f32[2,8,256]{2,1,0:T(8,128)S(1)}, u32[]{:S(2)}, u32[]{:S(2)}) %collective-permute-start.4) | collective-permute-done | bytes 16416 | tf_op jit(solution)/shard_map/ppermute | solution.py:80
  69.3 3.0 %collective-permute-start.5 = (bf16[4,8,128]{2,1,0:T(8,128)(2,1)S(1)}, bf16[4,8,128]{2,1,0:T(8,128)(2,1)S(1)}, u32[]{:S(2)}, u32[]{:S(2)}) collective-permute-start(bf16[4,8,128]{2,1,0:T(8,128)(2,1)S(1)} %bitcast.38), channel_id=1, source_target_pairs={{0,8},{1,9},{2,10},{3,11},{4,12},{5,13},{6,14},{7,15},{8,0},{9,1},... | collective-permute-start | bytes 24584 | tf_op jit(solution)/shard_map/ppermute | solution.py:528
  72.3 2.2 %collective-permute-done.5.other_coef_ref = bf16[4,8,128]{2,1,0:T(8,128)(2,1)S(1)} collective-permute-done((bf16[4,8,128]{2,1,0:T(8,128)(2,1)S(1)}, bf16[4,8,128]{2,1,0:T(8,128)(2,1)S(1)}, u32[]{:S(2)}, u32[]{:S(2)}) %collective-permute-start.5) | collective-permute-done | bytes 8224 | tf_op jit(solution)/shard_map/ppermute | solution.py:528
  75.9 4.1 %collective-permute-start.7 = (bf16[2,20,8,128]{3,2,1,0:T(8,128)(2,1)S(1)}, bf16[2,20,8,128]{3,2,1,0:T(8,128)(2,1)S(1)}, u32[]{:S(2)}, u32[]{:S(2)}) collective-permute-start(bf16[2,20,8,128]{3,2,1,0:T(8,128)(2,1)S(1)} %get-tuple-element.34), channel_id=1, source_target_pairs={{0,2},{1,3},{2,4},{3,5},{4,6},{5,7},{6,0},{7,1},{8,10},{9,11},{10,... | collective-permute-start | bytes 245768 | tf_op jit(solution)/shard_map/ppermute | solution.py:510
  80.6 5.0 %collective-permute-start.9 = (bf16[2,20,8,128]{3,2,1,0:T(8,128)(2,1)S(1)}, bf16[2,20,8,128]{3,2,1,0:T(8,128)(2,1)S(1)}, u32[]{:S(2)}, u32[]{:S(2)}) collective-permute-start(bf16[2,20,8,128]{3,2,1,0:T(8,128)(2,1)S(1)} %get-tuple-element.36), channel_id=1, source_target_pairs={{0,4},{1,5},{2,6},{3,7},{4,0},{5,1},{6,2},{7,3},{8,12},{9,13},{10,... | collective-permute-start | bytes 245768 | tf_op jit(solution)/shard_map/ppermute | solution.py:510
  85.6 15.9 %collective-permute-done.6.refs_1_ = bf16[2,20,8,128]{3,2,1,0:T(8,128)(2,1)S(1)} collective-permute-done((bf16[2,20,8,128]{3,2,1,0:T(8,128)(2,1)S(1)}, bf16[2,20,8,128]{3,2,1,0:T(8,128)(2,1)S(1)}, u32[]{:S(2)}, u32[]{:S(2)}) %collective-permute-start.6) | collective-permute-done | bytes 81952 | tf_op jit(solution)/shard_map/ppermute | solution.py:510
  101.5 1.8 %collective-permute-start.11 = (bf16[2,20,8,128]{3,2,1,0:T(8,128)(2,1)S(1)}, bf16[2,20,8,128]{3,2,1,0:T(8,128)(2,1)S(1)}, u32[]{:S(2)}, u32[]{:S(2)}) collective-permute-start(bf16[2,20,8,128]{3,2,1,0:T(8,128)(2,1)S(1)} %get-tuple-element.38), channel_id=1, source_target_pairs={{0,6},{1,7},{2,0},{3,1},{4,2},{5,3},{6,4},{7,5},{8,14},{9,15},{10,... | collective-permute-start | bytes 245768 | tf_op jit(solution)/shard_map/ppermute | solution.py:510
  103.3 1.8 %collective-permute-done.7.refs_2_ = bf16[2,20,8,128]{3,2,1,0:T(8,128)(2,1)S(1)} collective-permute-done((bf16[2,20,8,128]{3,2,1,0:T(8,128)(2,1)S(1)}, bf16[2,20,8,128]{3,2,1,0:T(8,128)(2,1)S(1)}, u32[]{:S(2)}, u32[]{:S(2)}) %collective-permute-start.7) | collective-permute-done | bytes 81952 | tf_op jit(solution)/shard_map/ppermute | solution.py:510
  106.5 1.7 %collective-permute-done.8.refs_3_ = bf16[2,20,8,128]{3,2,1,0:T(8,128)(2,1)S(1)} collective-permute-done((bf16[2,20,8,128]{3,2,1,0:T(8,128)(2,1)S(1)}, bf16[2,20,8,128]{3,2,1,0:T(8,128)(2,1)S(1)}, u32[]{:S(2)}, u32[]{:S(2)}) %collective-permute-start.8) | collective-permute-done | bytes 81952 | tf_op jit(solution)/shard_map/ppermute | solution.py:510
  108.2 6.6 %collective-permute-done.9.refs_4_ = bf16[2,20,8,128]{3,2,1,0:T(8,128)(2,1)S(1)} collective-permute-done((bf16[2,20,8,128]{3,2,1,0:T(8,128)(2,1)S(1)}, bf16[2,20,8,128]{3,2,1,0:T(8,128)(2,1)S(1)}, u32[]{:S(2)}, u32[]{:S(2)}) %collective-permute-start.9) | collective-permute-done | bytes 81952 | tf_op jit(solution)/shard_map/ppermute | solution.py:510
  117.9 2.2 %collective-permute-done.13 = f32[1,2,8,256]{3,2,1,0:T(8,128)S(1)} collective-permute-done((f32[1,2,8,256]{3,2,1,0:T(8,128)S(1)}, f32[1,2,8,256]{3,2,1,0:T(8,128)S(1)}, u32[]{:S(2)}, u32[]{:S(2)}) %collective-permute-start.13) | collective-permute-done | bytes 16416 | tf_op jit(solution)/shard_map/ppermute | solution.py:95
  122.5 2.5 %collective-permute-start.17 = (bf16[8,8,16,128]{3,2,1,0:T(8,128)(2,1)S(1)}, bf16[8,8,16,128]{3,2,1,0:T(8,128)(2,1)S(1)}, u32[]{:S(2)}, u32[]{:S(2)}) collective-permute-start(bf16[8,8,16,128]{3,2,1,0:T(8,128)(2,1)S(1)} %get-tuple-element.42), channel_id=1, source_target_pairs={{0,8},{1,9},{2,10},{3,11},{4,12},{5,13},{6,14},{7,15},{8,0},{9,1},... | collective-permute-start | bytes 786440 | tf_op jit(solution)/shard_map/ppermute | solution.py:535
  125.0 2.7 %collective-permute-start.15 = (f32[4,2,8,256]{3,2,1,0:T(8,128)S(1)}, f32[4,2,8,256]{3,2,1,0:T(8,128)S(1)}, u32[]{:S(2)}, u32[]{:S(2)}) collective-permute-start(f32[4,2,8,256]{3,2,1,0:T(8,128)S(1)} %pad_maximum_fusion.1), channel_id=1, source_target_pairs={{0,64},{16,80},{32,96},{48,112},{64,0},{80,16},{96,32},{112,48},{1... | collective-permute-start | bytes 196616 | tf_op jit(solution)/shard_map/ppermute | solution.py:95
  127.7 2.0 %collective-permute-done.15 = f32[4,2,8,256]{3,2,1,0:T(8,128)S(1)} collective-permute-done((f32[4,2,8,256]{3,2,1,0:T(8,128)S(1)}, f32[4,2,8,256]{3,2,1,0:T(8,128)S(1)}, u32[]{:S(2)}, u32[]{:S(2)}) %collective-permute-start.15) | collective-permute-done | bytes 65568 | tf_op jit(solution)/shard_map/ppermute | solution.py:95
  129.7 5.5 %collective-permute-start.16 = (f32[8,2,8,256]{3,2,1,0:T(8,128)S(1)}, f32[8,2,8,256]{3,2,1,0:T(8,128)S(1)}, u32[]{:S(2)}, u32[]{:S(2)}) collective-permute-start(f32[8,2,8,256]{3,2,1,0:T(8,128)S(1)} %pad_maximum_fusion), channel_id=1, source_target_pairs={{0,16},{16,0},{32,48},{48,32},{64,80},{80,64},{96,112},{112,96},{1... | collective-permute-start | bytes 393224 | tf_op jit(solution)/shard_map/ppermute | solution.py:95
  136.5 1.8 %collective-permute-start.19 = (bf16[2,8,16,128]{3,2,1,0:T(8,128)(2,1)S(1)}, bf16[2,8,16,128]{3,2,1,0:T(8,128)(2,1)S(1)}, u32[]{:S(2)}, u32[]{:S(2)}) collective-permute-start(bf16[2,8,16,128]{3,2,1,0:T(8,128)(2,1)S(1)} %get-tuple-element.45), channel_id=1, source_target_pairs={{0,2},{1,3},{2,4},{3,5},{4,6},{5,7},{6,0},{7,1},{8,10},{9,11},{10,... | collective-permute-start | bytes 196616 | tf_op jit(solution)/shard_map/ppermute | solution.py:510
  138.3 2.4 %collective-permute-start.20 = (bf16[2,8,16,128]{3,2,1,0:T(8,128)(2,1)}, bf16[2,8,16,128]{3,2,1,0:T(8,128)(2,1)S(1)}, u32[]{:S(2)}, u32[]{:S(2)}) collective-permute-start(bf16[2,8,16,128]{3,2,1,0:T(8,128)(2,1)} %get-tuple-element.46), channel_id=1, source_target_pairs={{0,3},{1,4},{2,5},{3,6},{4,7},{5,0},{6,1},{7,2},{8,11},{9,12},{10,... | collective-permute-start | bytes 196616 | tf_op jit(solution)/shard_map/ppermute | solution.py:510
  140.7 2.3 %collective-permute-start.21 = (bf16[2,8,16,128]{3,2,1,0:T(8,128)(2,1)}, bf16[2,8,16,128]{3,2,1,0:T(8,128)(2,1)S(1)}, u32[]{:S(2)}, u32[]{:S(2)}) collective-permute-start(bf16[2,8,16,128]{3,2,1,0:T(8,128)(2,1)} %get-tuple-element.47), channel_id=1, source_target_pairs={{0,4},{1,5},{2,6},{3,7},{4,0},{5,1},{6,2},{7,3},{8,12},{9,13},{10,... | collective-permute-start | bytes 196616 | tf_op jit(solution)/shard_map/ppermute | solution.py:510
  142.9 1.9 %collective-permute-start.22 = (bf16[2,8,16,128]{3,2,1,0:T(8,128)(2,1)S(1)}, bf16[2,8,16,128]{3,2,1,0:T(8,128)(2,1)S(1)}, u32[]{:S(2)}, u32[]{:S(2)}) collective-permute-start(bf16[2,8,16,128]{3,2,1,0:T(8,128)(2,1)S(1)} %get-tuple-element.48), channel_id=1, source_target_pairs={{0,5},{1,6},{2,7},{3,0},{4,1},{5,2},{6,3},{7,4},{8,13},{9,14},{10,... | collective-permute-start | bytes 196616 | tf_op jit(solution)/shard_map/ppermute | solution.py:510
  144.9 1.6 %collective-permute-start.23 = (bf16[2,8,16,128]{3,2,1,0:T(8,128)(2,1)S(1)}, bf16[2,8,16,128]{3,2,1,0:T(8,128)(2,1)S(1)}, u32[]{:S(2)}, u32[]{:S(2)}) collective-permute-start(bf16[2,8,16,128]{3,2,1,0:T(8,128)(2,1)S(1)} %get-tuple-element.49), channel_id=1, source_target_pairs={{0,6},{1,7},{2,0},{3,1},{4,2},{5,3},{6,4},{7,5},{8,14},{9,15},{10,... | collective-permute-start | bytes 196616 | tf_op jit(solution)/shard_map/ppermute | solution.py:510
  147.9 4.9 %inverse_transform.1 = (f32[8,16,48,128]{3,2,1,0:T(8,128)}, f32[8,16,16,128]{3,2,1,0:T(8,128)S(1)}) custom-call(s32[1]{0:T(128)} %bitcast.2.me_ref, f32[8]{0:T(128)S(1)} %dynamic-slice_multiply_fusion.bias_ref, f32[16,2,8,256]{3,2,1,0:T(8,128)S(1)} %constant_dynamic-update-slice_fusion.spec_ref, f32[16,256]{1,0:T(8,128)S(1)} %select_multiply_fusion.depth_ref, ...), custom_call_target="tpu_custom_call" | custom-call | flops 2000000000 | bytes 5000000 | tf_op jit(solution)/shard_map/inverse_transform/pallas_call | solution.py:407
  152.8 3.4 %finish_early.1 = (bf16[8,16,64,128]{3,2,1,0:T(8,128)(2,1)}, f32[8,16,48,128]{3,2,1,0:T(8,128)}) custom-call(bf16[16,8,48,128]{3,2,1,0:T(8,128)(2,1)S(1)} %all-to-all-done.1.coded_ref, f32[8,16,48,128]{3,2,1,0:T(8,128)} %get-tuple-element.53.inverse_ref), custom_call_target="tpu_custom_call", output_to_operand_aliasing={{1}: (1, {})} | custom-call | flops 30000000 | bytes 8000000 | tf_op jit(solution)/shard_map/finish_early/pallas_call | solution.py:459
  156.3 1.8 %finish_late.1 = bf16[8,16,64,128]{3,2,1,0:T(8,128)(2,1)} custom-call(s32[2]{0:T(128)S(1)} %pad_add_fusion.place_ref, f32[8,16,16,128]{3,2,1,0:T(8,128)S(1)} %get-tuple-element.40.inverse_ref, bf16[2,8,16,128]{3,2,1,0:T(8,128)(2,1)S(1)} %get-tuple-element.43.refs_0_, ...), custom_call_target="tpu_custom_call", output_to_operand_aliasing={{}: (10, {})} | custom-call | flops 4000000 | bytes 1200000 | tf_op jit(solution)/shard_map/finish_late/pallas_call | solution.py:494
  (83 shorter events, 16.4 us)
Async XLA Ops:
  3.5 12.2 %copy-start = (bf16[1,8,8,128,128]{4,3,2,1,0:T(8,128)(2,1)S(1)}, bf16[1,8,8,128,128]{4,3,2,1,0:T(8,128)(2,1)}, u32[]{:S(2)}) copy-start(bf16[1,8,8,128,128]{4,3,2,1,0:T(8,128)(2,1)} %param.8) | copy-start | bytes 6291460
  3.5 12.2 %copy-start.3 = (f32[256,32]{1,0:T(8,128)S(1)}, f32[256,32]{1,0:T(8,128)}, u32[]{:S(2)}) copy-start(f32[256,32]{1,0:T(8,128)} %constant.218.clone.table_y_ref.table_x_ref) | copy-start | bytes 98308
  3.5 49.7 %all-to-all-start = ((bf16[16,48,8,128]{3,2,1,0:T(8,128)(2,1)}), bf16[16,48,8,128]{3,2,1,0:T(8,128)(2,1)}, u32[]{:S(2)}, u32[]{:S(2)}) async-start(bf16[16,48,8,128]{3,2,1,0:T(8,128)(2,1)} %get-tuple-element.51), calls=%async_computation | async-start | bytes 3145728 | tf_op jit(solution)/shard_map/all_to_all | solution.py:523
  18.3 4.2 %collective-permute-start.1 = (f32[2,2,2,2,8,256]{5,4,3,2,0,1:T(8,128)S(1)}, f32[2,2,2,2,8,256]{5,4,3,2,0,1:T(8,128)S(1)}, u32[]{:S(2)}, u32[]{:S(2)}) collective-permute-start(f32[2,2,2,2,8,256]{5,4,3,2,0,1:T(8,128)S(1)} %bitcast.40), channel_id=1, source_target_pairs={{0,16},{16,0},{32,48},{48,32},{64,80},{80,64},{96,112},{112,96},{1... | collective-permute-start | bytes 393224 | tf_op jit(solution)/shard_map/ppermute | solution.py:80
  19.3 55.2 %collective-permute-start = (bf16[8,16,8,128]{3,2,1,0:T(8,128)(2,1)S(1)}, bf16[8,16,8,128]{3,2,1,0:T(8,128)(2,1)S(1)}, u32[]{:S(2)}, u32[]{:S(2)}) collective-permute-start(bf16[8,16,8,128]{3,2,1,0:T(8,128)(2,1)S(1)} %copy-done.7), channel_id=1, source_target_pairs={{0,8},{1,9},{2,10},{3,11},{4,12},{5,13},{6,14},{7,15},{8,0},{9,1},... | collective-permute-start | bytes 786440 | tf_op jit(solution)/shard_map/ppermute | solution.py:524
  22.5 5.1 %collective-permute-start.2 = (f32[2,2,2,8,256]{4,3,2,1,0:T(8,128)S(1)}, f32[2,2,2,8,256]{4,3,2,1,0:T(8,128)S(1)}, u32[]{:S(2)}, u32[]{:S(2)}) collective-permute-start(f32[2,2,2,8,256]{4,3,2,1,0:T(8,128)S(1)} %dynamic-slice_bitcast_fusion), channel_id=1, source_target_pairs={{0,64},{16,80},{32,96},{48,112},{64,0},{80,16},{96,32},{112,48},{1... | collective-permute-start | bytes 196616 | tf_op jit(solution)/shard_map/ppermute | solution.py:80
  56.6 17.9 %copy-start.2 = (bf16[8,16,8,128]{3,2,1,0:T(8,128)(2,1)S(1)}, bf16[8,16,8,128]{3,2,1,0:T(8,128)(2,1)}, u32[]{:S(2)}) copy-start(bf16[8,16,8,128]{3,2,1,0:T(8,128)(2,1)} %get-tuple-element.30.own_cells_ref) | copy-start | bytes 786436
  56.6 96.2 %all-to-all-start.1 = ((bf16[16,8,48,128]{3,2,1,0:T(8,128)(2,1)}), bf16[16,8,48,128]{3,2,1,0:T(8,128)(2,1)S(1)}, u32[]{:S(2)}, u32[]{:S(2)}) async-start(bf16[16,8,48,128]{3,2,1,0:T(8,128)(2,1)} %get-tuple-element.52), calls=%async_computation.1 | async-start | bytes 3145728 | tf_op jit(solution)/shard_map/all_to_all | solution.py:532
  63.4 54.4 %copy-start.8 = (f32[128]{0:T(128)S(1)}, f32[128]{0:T(128)}, u32[]{:S(2)}) copy-start(f32[128]{0:T(128)} %param.10) | copy-start | bytes 1540
  63.4 2.9 %collective-permute-start.3 = (f32[2,2,8,256]{3,2,1,0:T(8,128)S(1)}, f32[2,2,8,256]{3,2,1,0:T(8,128)S(1)}, u32[]{:S(2)}, u32[]{:S(2)}) collective-permute-start(f32[2,2,8,256]{3,2,1,0:T(8,128)S(1)} %dynamic-slice_bitcast_fusion.1), channel_id=1, source_target_pairs={{0,32},{16,48},{32,0},{48,16},{64,96},{80,112},{96,64},{112,80},{1... | collective-permute-start | bytes 98312 | tf_op jit(solution)/shard_map/ppermute | solution.py:80
  66.3 3.0 %collective-permute-start.4 = (f32[2,8,256]{2,1,0:T(8,128)S(1)}, f32[2,8,256]{2,1,0:T(8,128)S(1)}, u32[]{:S(2)}, u32[]{:S(2)}) collective-permute-start(f32[2,8,256]{2,1,0:T(8,128)S(1)} %dynamic-slice_bitcast_fusion.2), channel_id=1, source_target_pairs={{0,128},{16,144},{32,160},{48,176},{64,192},{80,208},{96,224},{112... | collective-permute-start | bytes 49160 | tf_op jit(solution)/shard_map/ppermute | solution.py:80
  69.3 5.2 %collective-permute-start.5 = (bf16[4,8,128]{2,1,0:T(8,128)(2,1)S(1)}, bf16[4,8,128]{2,1,0:T(8,128)(2,1)S(1)}, u32[]{:S(2)}, u32[]{:S(2)}) collective-permute-start(bf16[4,8,128]{2,1,0:T(8,128)(2,1)S(1)} %bitcast.38), channel_id=1, source_target_pairs={{0,8},{1,9},{2,10},{3,11},{4,12},{5,13},{6,14},{7,15},{8,0},{9,1},... | collective-permute-start | bytes 24584 | tf_op jit(solution)/shard_map/ppermute | solution.py:528
  75.1 26.3 %collective-permute-start.6 = (bf16[2,20,8,128]{3,2,1,0:T(8,128)(2,1)S(1)}, bf16[2,20,8,128]{3,2,1,0:T(8,128)(2,1)S(1)}, u32[]{:S(2)}, u32[]{:S(2)}) collective-permute-start(bf16[2,20,8,128]{3,2,1,0:T(8,128)(2,1)S(1)} %get-tuple-element.33), channel_id=1, source_target_pairs={{0,1},{1,2},{2,3},{3,4},{4,5},{5,6},{6,7},{7,0},{8,9},{9,10},{10,1... | collective-permute-start | bytes 245768 | tf_op jit(solution)/shard_map/ppermute | solution.py:510
  75.9 29.1 %collective-permute-start.7 = (bf16[2,20,8,128]{3,2,1,0:T(8,128)(2,1)S(1)}, bf16[2,20,8,128]{3,2,1,0:T(8,128)(2,1)S(1)}, u32[]{:S(2)}, u32[]{:S(2)}) collective-permute-start(bf16[2,20,8,128]{3,2,1,0:T(8,128)(2,1)S(1)} %get-tuple-element.34), channel_id=1, source_target_pairs={{0,2},{1,3},{2,4},{3,5},{4,6},{5,7},{6,0},{7,1},{8,10},{9,11},{10,... | collective-permute-start | bytes 245768 | tf_op jit(solution)/shard_map/ppermute | solution.py:510
  80.0 28.2 %collective-permute-start.8 = (bf16[2,20,8,128]{3,2,1,0:T(8,128)(2,1)S(1)}, bf16[2,20,8,128]{3,2,1,0:T(8,128)(2,1)S(1)}, u32[]{:S(2)}, u32[]{:S(2)}) collective-permute-start(bf16[2,20,8,128]{3,2,1,0:T(8,128)(2,1)S(1)} %get-tuple-element.35), channel_id=1, source_target_pairs={{0,3},{1,4},{2,5},{3,6},{4,7},{5,0},{6,1},{7,2},{8,11},{9,12},{10,... | collective-permute-start | bytes 245768 | tf_op jit(solution)/shard_map/ppermute | solution.py:510
  80.6 34.2 %collective-permute-start.9 = (bf16[2,20,8,128]{3,2,1,0:T(8,128)(2,1)S(1)}, bf16[2,20,8,128]{3,2,1,0:T(8,128)(2,1)S(1)}, u32[]{:S(2)}, u32[]{:S(2)}) collective-permute-start(bf16[2,20,8,128]{3,2,1,0:T(8,128)(2,1)S(1)} %get-tuple-element.36), channel_id=1, source_target_pairs={{0,4},{1,5},{2,6},{3,7},{4,0},{5,1},{6,2},{7,3},{8,12},{9,13},{10,... | collective-permute-start | bytes 245768 | tf_op jit(solution)/shard_map/ppermute | solution.py:510
  85.6 29.2 %collective-permute-start.10 = (bf16[2,20,8,128]{3,2,1,0:T(8,128)(2,1)S(1)}, bf16[2,20,8,128]{3,2,1,0:T(8,128)(2,1)S(1)}, u32[]{:S(2)}, u32[]{:S(2)}) collective-permute-start(bf16[2,20,8,128]{3,2,1,0:T(8,128)(2,1)S(1)} %get-tuple-element.37), channel_id=1, source_target_pairs={{0,5},{1,6},{2,7},{3,0},{4,1},{5,2},{6,3},{7,4},{8,13},{9,14},{10,... | collective-permute-start | bytes 245768 | tf_op jit(solution)/shard_map/ppermute | solution.py:510
  101.5 13.3 %collective-permute-start.11 = (bf16[2,20,8,128]{3,2,1,0:T(8,128)(2,1)S(1)}, bf16[2,20,8,128]{3,2,1,0:T(8,128)(2,1)S(1)}, u32[]{:S(2)}, u32[]{:S(2)}) collective-permute-start(bf16[2,20,8,128]{3,2,1,0:T(8,128)(2,1)S(1)} %get-tuple-element.38), channel_id=1, source_target_pairs={{0,6},{1,7},{2,0},{3,1},{4,2},{5,3},{6,4},{7,5},{8,14},{9,15},{10,... | collective-permute-start | bytes 245768 | tf_op jit(solution)/shard_map/ppermute | solution.py:510
  105.1 9.7 %collective-permute-start.12 = (bf16[2,20,8,128]{3,2,1,0:T(8,128)(2,1)S(1)}, bf16[2,20,8,128]{3,2,1,0:T(8,128)(2,1)S(1)}, u32[]{:S(2)}, u32[]{:S(2)}) collective-permute-start(bf16[2,20,8,128]{3,2,1,0:T(8,128)(2,1)S(1)} %get-tuple-element.39), channel_id=1, source_target_pairs={{0,7},{1,0},{2,1},{3,2},{4,3},{5,4},{6,5},{7,6},{8,15},{9,8},{10,9... | collective-permute-start | bytes 245768 | tf_op jit(solution)/shard_map/ppermute | solution.py:510
  116.4 31.6 %copy-start.5 = (f32[2,16,128]{2,1,0:T(8,128)S(1)}, f32[2,16,128]{2,1,0:T(8,128)}, u32[]{:S(2)}) copy-start(f32[2,16,128]{2,1,0:T(8,128)} %constant.219.clone.waves_y_ref) | copy-start | bytes 49156
  117.4 2.7 %collective-permute-start.13 = (f32[1,2,8,256]{3,2,1,0:T(8,128)S(1)}, f32[1,2,8,256]{3,2,1,0:T(8,128)S(1)}, u32[]{:S(2)}, u32[]{:S(2)}) collective-permute-start(f32[1,2,8,256]{3,2,1,0:T(8,128)S(1)} %bitcast.34), channel_id=1, source_target_pairs={{0,128},{16,144},{32,160},{48,176},{64,192},{80,208},{96,224},{112... | collective-permute-start | bytes 49160 | tf_op jit(solution)/shard_map/ppermute | solution.py:95
  120.1 4.9 %collective-permute-start.14 = (f32[2,2,8,256]{3,2,1,0:T(8,128)S(1)}, f32[2,2,8,256]{3,2,1,0:T(8,128)S(1)}, u32[]{:S(2)}, u32[]{:S(2)}) collective-permute-start(f32[2,2,8,256]{3,2,1,0:T(8,128)S(1)} %pad_maximum_fusion.2), channel_id=1, source_target_pairs={{0,32},{16,48},{32,0},{48,16},{64,96},{80,112},{96,64},{112,80},{1... | collective-permute-start | bytes 98312 | tf_op jit(solution)/shard_map/ppermute | solution.py:95
  122.5 12.8 %collective-permute-start.17 = (bf16[8,8,16,128]{3,2,1,0:T(8,128)(2,1)S(1)}, bf16[8,8,16,128]{3,2,1,0:T(8,128)(2,1)S(1)}, u32[]{:S(2)}, u32[]{:S(2)}) collective-permute-start(bf16[8,8,16,128]{3,2,1,0:T(8,128)(2,1)S(1)} %get-tuple-element.42), channel_id=1, source_target_pairs={{0,8},{1,9},{2,10},{3,11},{4,12},{5,13},{6,14},{7,15},{8,0},{9,1},... | collective-permute-start | bytes 786440 | tf_op jit(solution)/shard_map/ppermute | solution.py:535
  125.0 4.7 %collective-permute-start.15 = (f32[4,2,8,256]{3,2,1,0:T(8,128)S(1)}, f32[4,2,8,256]{3,2,1,0:T(8,128)S(1)}, u32[]{:S(2)}, u32[]{:S(2)}) collective-permute-start(f32[4,2,8,256]{3,2,1,0:T(8,128)S(1)} %pad_maximum_fusion.1), channel_id=1, source_target_pairs={{0,64},{16,80},{32,96},{48,112},{64,0},{80,16},{96,32},{112,48},{1... | collective-permute-start | bytes 196616 | tf_op jit(solution)/shard_map/ppermute | solution.py:95
  129.7 8.5 %collective-permute-start.16 = (f32[8,2,8,256]{3,2,1,0:T(8,128)S(1)}, f32[8,2,8,256]{3,2,1,0:T(8,128)S(1)}, u32[]{:S(2)}, u32[]{:S(2)}) collective-permute-start(f32[8,2,8,256]{3,2,1,0:T(8,128)S(1)} %pad_maximum_fusion), channel_id=1, source_target_pairs={{0,16},{16,0},{32,48},{48,32},{64,80},{80,64},{96,112},{112,96},{1... | collective-permute-start | bytes 393224 | tf_op jit(solution)/shard_map/ppermute | solution.py:95
  136.5 8.4 %collective-permute-start.18 = (bf16[2,8,16,128]{3,2,1,0:T(8,128)(2,1)S(1)}, bf16[2,8,16,128]{3,2,1,0:T(8,128)(2,1)S(1)}, u32[]{:S(2)}, u32[]{:S(2)}) collective-permute-start(bf16[2,8,16,128]{3,2,1,0:T(8,128)(2,1)S(1)} %get-tuple-element.44), channel_id=1, source_target_pairs={{0,1},{1,2},{2,3},{3,4},{4,5},{5,6},{6,7},{7,0},{8,9},{9,10},{10,1... | collective-permute-start | bytes 196616 | tf_op jit(solution)/shard_map/ppermute | solution.py:510
  136.5 10.0 %collective-permute-start.19 = (bf16[2,8,16,128]{3,2,1,0:T(8,128)(2,1)S(1)}, bf16[2,8,16,128]{3,2,1,0:T(8,128)(2,1)S(1)}, u32[]{:S(2)}, u32[]{:S(2)}) collective-permute-start(bf16[2,8,16,128]{3,2,1,0:T(8,128)(2,1)S(1)} %get-tuple-element.45), channel_id=1, source_target_pairs={{0,2},{1,3},{2,4},{3,5},{4,6},{5,7},{6,0},{7,1},{8,10},{9,11},{10,... | collective-permute-start | bytes 196616 | tf_op jit(solution)/shard_map/ppermute | solution.py:510
  138.3 17.9 %collective-permute-start.20 = (bf16[2,8,16,128]{3,2,1,0:T(8,128)(2,1)}, bf16[2,8,16,128]{3,2,1,0:T(8,128)(2,1)S(1)}, u32[]{:S(2)}, u32[]{:S(2)}) collective-permute-start(bf16[2,8,16,128]{3,2,1,0:T(8,128)(2,1)} %get-tuple-element.46), channel_id=1, source_target_pairs={{0,3},{1,4},{2,5},{3,6},{4,7},{5,0},{6,1},{7,2},{8,11},{9,12},{10,... | collective-permute-start | bytes 196616 | tf_op jit(solution)/shard_map/ppermute | solution.py:510
  140.7 15.6 %collective-permute-start.21 = (bf16[2,8,16,128]{3,2,1,0:T(8,128)(2,1)}, bf16[2,8,16,128]{3,2,1,0:T(8,128)(2,1)S(1)}, u32[]{:S(2)}, u32[]{:S(2)}) collective-permute-start(bf16[2,8,16,128]{3,2,1,0:T(8,128)(2,1)} %get-tuple-element.47), channel_id=1, source_target_pairs={{0,4},{1,5},{2,6},{3,7},{4,0},{5,1},{6,2},{7,3},{8,12},{9,13},{10,... | collective-permute-start | bytes 196616 | tf_op jit(solution)/shard_map/ppermute | solution.py:510
  142.9 13.3 %collective-permute-start.22 = (bf16[2,8,16,128]{3,2,1,0:T(8,128)(2,1)S(1)}, bf16[2,8,16,128]{3,2,1,0:T(8,128)(2,1)S(1)}, u32[]{:S(2)}, u32[]{:S(2)}) collective-permute-start(bf16[2,8,16,128]{3,2,1,0:T(8,128)(2,1)S(1)} %get-tuple-element.48), channel_id=1, source_target_pairs={{0,5},{1,6},{2,7},{3,0},{4,1},{5,2},{6,3},{7,4},{8,13},{9,14},{10,... | collective-permute-start | bytes 196616 | tf_op jit(solution)/shard_map/ppermute | solution.py:510
  144.9 11.4 %collective-permute-start.23 = (bf16[2,8,16,128]{3,2,1,0:T(8,128)(2,1)S(1)}, bf16[2,8,16,128]{3,2,1,0:T(8,128)(2,1)S(1)}, u32[]{:S(2)}, u32[]{:S(2)}) collective-permute-start(bf16[2,8,16,128]{3,2,1,0:T(8,128)(2,1)S(1)} %get-tuple-element.49), channel_id=1, source_target_pairs={{0,6},{1,7},{2,0},{3,1},{4,2},{5,3},{6,4},{7,5},{8,14},{9,15},{10,... | collective-permute-start | bytes 196616 | tf_op jit(solution)/shard_map/ppermute | solution.py:510
  146.5 9.8 %collective-permute-start.24 = (bf16[2,8,16,128]{3,2,1,0:T(8,128)(2,1)S(1)}, bf16[2,8,16,128]{3,2,1,0:T(8,128)(2,1)S(1)}, u32[]{:S(2)}, u32[]{:S(2)}) collective-permute-start(bf16[2,8,16,128]{3,2,1,0:T(8,128)(2,1)S(1)} %get-tuple-element.50), channel_id=1, source_target_pairs={{0,7},{1,0},{2,1},{3,2},{4,3},{5,4},{6,5},{7,6},{8,15},{9,8},{10,9... | collective-permute-start | bytes 196616 | tf_op jit(solution)/shard_map/ppermute | solution.py:510
  (4 other events, 28.0 us)

commit v5 on v4

--- a/solution.py
+++ b/solution.py
@@ -142,7 +142,7 @@
     )(field, table_x, table_y, depth)
 
 
-def cut_kernel(field_ref, early_ref, own_ref, other_ref, block_ref, turned_ref, late_ref, fetched, stored):
+def cut_kernel(field_ref, early_ref, own_ref, other_ref, block_ref, turned_ref, late_ref, fetched, stored, parted):
     x_hi = lax.shift_right_logical(lax.axis_index("chan"), 3)
     parts = fetched.shape[0]
     span = BLOCKS // parts
@@ -157,12 +157,20 @@
             block = block_ref[:, p].astype(jnp.float32)
             turned = block.transpose(1, 0, 2).astype(jnp.bfloat16)
             turned_ref[p] = turned[:EARLY]
-            late_ref[lax.bitwise_xor(x_hi, p // 8), p % 8] = turned[EARLY:]
+            late_ref[p // 8, p % 8] = turned[EARLY:]
         blocks = pl.ds(part * span, span)
         stores.append(pltpu.make_async_copy(turned_ref.at[blocks], early_ref.at[blocks], stored.at[part]))
         stores[part].start()
-    own_ref[...] = late_ref[0]
-    other_ref[...] = late_ref[1]
+        if (part + 1) % (parts // 2) == 0:
+            half = part // (parts // 2)
+            for target, side in ((own_ref, half), (other_ref, 1 - half)):
+
+                @pl.when(x_hi == side)
+                def _():
+                    pltpu.make_async_copy(late_ref.at[half], target, parted.at[half]).start()
+
+    for half in range(2):
+        stores.append(pltpu.make_async_copy(late_ref.at[half], own_ref, parted.at[half]))
     for store in stores:
         store.wait()
 
@@ -173,15 +181,16 @@
     return pl.pallas_call(
         cut_kernel,
         out_shape=[pltpu.HBM((BLOCKS, EARLY, 8, 128), jnp.bfloat16)]
-        + [jax.ShapeDtypeStruct((8, LATE, 8, 128), jnp.bfloat16)] * 2,
+        + [pltpu.HBM((8, LATE, 8, 128), jnp.bfloat16)] * 2,
         in_specs=[in_place],
-        out_specs=[in_place, WHOLE, WHOLE],
+        out_specs=[in_place] * 3,
         scratch_shapes=[
             pltpu.VMEM((8, BLOCKS, 64, 128), jnp.bfloat16),
             pltpu.VMEM((BLOCKS, EARLY, 8, 128), jnp.bfloat16),
             pltpu.VMEM((2, 8, LATE, 8, 128), jnp.bfloat16),
             pltpu.SemaphoreType.DMA((parts,)),
             pltpu.SemaphoreType.DMA((parts,)),
+            pltpu.SemaphoreType.DMA((2,)),
         ],
         cost_estimate=pl.CostEstimate(flops=1_000_000, bytes_accessed=4_000_000, transcendentals=0),
         compiler_params=pltpu.CompilerParams(vmem_limit_bytes=60 << 20),

time: 159 us -> 158 us (level)
  no operation moved by 1% of the time
where the time goes in v5:
time: 158 us
  starting transfers between devices  67.7 us (43%)
  waiting for transfers between devices  64.1 us (41%)
  Pallas kernels  22.8 us (14%)
  local copies, waits for them, and re-layouts  1.73 us (1%)
    ppermute x14, waiting for transfers between devices, z_letters(): arrived.append(lax.ppermute(letters[k], 'chan', chan_perm(0, k)))  26 us
    all_to_all x1, waiting for transfers between devices, on_device(): cells = lax.all_to_all(cells, 'chan', 0, 0, tiled=True)  25.6 us
    ppermute x14, starting transfers between devices, z_letters(): arrived.append(lax.ppermute(letters[k], 'chan', chan_perm(0, k)))  24.9 us
    all_to_all x1, starting transfers between devices, on_device(): cells = lax.all_to_all(cells, 'chan', 0, 0, tiled=True)  11.8 us
    ppermute x4, starting transfers between devices, slab_gather(): other = lax.ppermute(value, 'slab', slab_perm(*step))  9.9 us
    all_to_all x1, starting transfers between devices, on_device(): coded = lax.all_to_all(coded, 'chan', 0, 0, tiled=True)  6.76 us
    ppermute x4, waiting for transfers between devices, halve(): return own + lax.ppermute(other, 'slab', perm)  6.13 us
    ppermute x4, starting transfers between devices, halve(): return own + lax.ppermute(other, 'slab', perm)  5.83 us
  transfers between devices with their start and end apart: 27, of which 11 were waited for; matrix products, arithmetic and copies ran while one was open for 0% of the time, Pallas kernels for 12%

profile of v5, /device:TPU:1, one launch (start us, length us, event | category | flops | bytes accessed | tf_op | source)
XLA Modules:
  0.0 157.5 jit_solution(14430650723542898254)
XLA Ops:
  0.0 2.7 %cut.1 = (bf16[16,48,8,128]{3,2,1,0:T(8,128)(2,1)}, bf16[8,16,8,128]{3,2,1,0:T(8,128)(2,1)}, bf16[8,16,8,128]{3,2,1,0:T(8,128)(2,1)}) custom-call(bf16[8,16,64,128]{3,2,1,0:T(8,128)(2,1)} %bitcast.31), custom_call_target="tpu_custom_call" | custom-call | flops 1000000 | bytes 4000000 | tf_op jit(solution)/shard_map/cut/pallas_call | solution.py:181
  2.8 11.8 %all-to-all-start = ((bf16[16,48,8,128]{3,2,1,0:T(8,128)(2,1)}), bf16[16,48,8,128]{3,2,1,0:T(8,128)(2,1)}, u32[]{:S(2)}, u32[]{:S(2)}) async-start(bf16[16,48,8,128]{3,2,1,0:T(8,128)(2,1)} %get-tuple-element.51), calls=%async_computation | async-start | bytes 3145728 | tf_op jit(solution)/shard_map/all_to_all | solution.py:532
  14.9 2.6 %forward_transform.1 = f32[16,2,8,256]{3,2,1,0:T(8,128)S(1)} custom-call(bf16[8,8,128,128]{3,2,1,0:T(8,128)(2,1)S(1)} %bitcast.32, bf16[32,128]{1,0:T(8,128)(2,1)S(1)} %copy-done.4, f32[256,32]{1,0:T(8,128)S(1)} %copy-done.3, f32[16,512]{1,0:T(8,128)S(1)} %fusion.3.depth_ref), custom_call_target="tpu_custom_call" | custom-call | flops 200000000 | bytes 3000000 | tf_op jit(solution)/shard_map/forward_transform/pallas_call | solution.py:133
  18.6 3.1 %collective-permute-start = (bf16[8,16,8,128]{3,2,1,0:T(8,128)(2,1)S(1)}, bf16[8,16,8,128]{3,2,1,0:T(8,128)(2,1)S(1)}, u32[]{:S(2)}, u32[]{:S(2)}) collective-permute-start(bf16[8,16,8,128]{3,2,1,0:T(8,128)(2,1)S(1)} %copy-done.7), channel_id=1, source_target_pairs={{0,8},{1,9},{2,10},{3,11},{4,12},{5,13},{6,14},{7,15},{8,0},{9,1},... | collective-permute-start | bytes 786440 | tf_op jit(solution)/shard_map/ppermute | solution.py:533
  21.7 3.0 %collective-permute-start.2 = (f32[2,2,2,8,256]{4,3,2,1,0:T(8,128)S(1)}, f32[2,2,2,8,256]{4,3,2,1,0:T(8,128)S(1)}, u32[]{:S(2)}, u32[]{:S(2)}) collective-permute-start(f32[2,2,2,8,256]{4,3,2,1,0:T(8,128)S(1)} %dynamic-slice_bitcast_fusion), channel_id=1, source_target_pairs={{0,64},{16,80},{32,96},{48,112},{64,0},{80,16},{96,32},{112,48},{1... | collective-permute-start | bytes 196616 | tf_op jit(solution)/shard_map/ppermute | solution.py:80
  24.7 2.1 %collective-permute-done.2 = f32[2,2,2,8,256]{4,3,2,1,0:T(8,128)S(1)} collective-permute-done((f32[2,2,2,8,256]{4,3,2,1,0:T(8,128)S(1)}, f32[2,2,2,8,256]{4,3,2,1,0:T(8,128)S(1)}, u32[]{:S(2)}, u32[]{:S(2)}) %collective-permute-start.2) | collective-permute-done | bytes 65568 | tf_op jit(solution)/shard_map/ppermute | solution.py:80
  26.9 25.6 %all-to-all-done.cells_ref = bf16[16,48,8,128]{3,2,1,0:T(8,128)(2,1)} async-done(((bf16[16,48,8,128]{3,2,1,0:T(8,128)(2,1)}), bf16[16,48,8,128]{3,2,1,0:T(8,128)(2,1)}, u32[]{:S(2)}, u32[]{:S(2)}) %all-to-all-start) | async-done | bytes 1572896 | tf_op jit(solution)/shard_map/all_to_all | solution.py:532
  52.4 3.4 %map_early.1 = (bf16[16,8,48,128]{3,2,1,0:T(8,128)(2,1)}, bf16[16,48,8,128]{3,2,1,0:T(8,128)(2,1)}) custom-call(bf16[128,128]{1,0:T(8,128)(2,1)S(1)} %broadcast_multiply_fusion.weight_ref, bf16[16,48,8,128]{3,2,1,0:T(8,128)(2,1)} %all-to-all-done.cells_ref), custom_call_target="tpu_custom_call", output_to_operand_aliasing={{1}: (1, {})} | custom-call | flops 270000000 | bytes 4000000 | tf_op jit(solution)/shard_map/map_early/pallas_call | solution.py:235
  55.9 6.8 %all-to-all-start.1 = ((bf16[16,8,48,128]{3,2,1,0:T(8,128)(2,1)}), bf16[16,8,48,128]{3,2,1,0:T(8,128)(2,1)S(1)}, u32[]{:S(2)}, u32[]{:S(2)}) async-start(bf16[16,8,48,128]{3,2,1,0:T(8,128)(2,1)} %get-tuple-element.52), calls=%async_computation.1 | async-start | bytes 3145728 | tf_op jit(solution)/shard_map/all_to_all | solution.py:541
  65.9 2.6 %collective-permute-done.4 = f32[2,8,256]{2,1,0:T(8,128)S(1)} collective-permute-done((f32[2,8,256]{2,1,0:T(8,128)S(1)}, f32[2,8,256]{2,1,0:T(8,128)S(1)}, u32[]{:S(2)}, u32[]{:S(2)}) %collective-permute-start.4) | collective-permute-done | bytes 16416 | tf_op jit(solution)/shard_map/ppermute | solution.py:80
  68.5 3.0 %collective-permute-start.5 = (bf16[4,8,128]{2,1,0:T(8,128)(2,1)S(1)}, bf16[4,8,128]{2,1,0:T(8,128)(2,1)S(1)}, u32[]{:S(2)}, u32[]{:S(2)}) collective-permute-start(bf16[4,8,128]{2,1,0:T(8,128)(2,1)S(1)} %bitcast.38), channel_id=1, source_target_pairs={{0,8},{1,9},{2,10},{3,11},{4,12},{5,13},{6,14},{7,15},{8,0},{9,1},... | collective-permute-start | bytes 24584 | tf_op jit(solution)/shard_map/ppermute | solution.py:537
  71.6 2.2 %collective-permute-done.5.other_coef_ref = bf16[4,8,128]{2,1,0:T(8,128)(2,1)S(1)} collective-permute-done((bf16[4,8,128]{2,1,0:T(8,128)(2,1)S(1)}, bf16[4,8,128]{2,1,0:T(8,128)(2,1)S(1)}, u32[]{:S(2)}, u32[]{:S(2)}) %collective-permute-start.5) | collective-permute-done | bytes 8224 | tf_op jit(solution)/shard_map/ppermute | solution.py:537
  75.2 4.1 %collective-permute-start.7 = (bf16[2,20,8,128]{3,2,1,0:T(8,128)(2,1)S(1)}, bf16[2,20,8,128]{3,2,1,0:T(8,128)(2,1)S(1)}, u32[]{:S(2)}, u32[]{:S(2)}) collective-permute-start(bf16[2,20,8,128]{3,2,1,0:T(8,128)(2,1)S(1)} %get-tuple-element.34), channel_id=1, source_target_pairs={{0,2},{1,3},{2,4},{3,5},{4,6},{5,7},{6,0},{7,1},{8,10},{9,11},{10,... | collective-permute-start | bytes 245768 | tf_op jit(solution)/shard_map/ppermute | solution.py:519
  79.8 5.0 %collective-permute-start.9 = (bf16[2,20,8,128]{3,2,1,0:T(8,128)(2,1)S(1)}, bf16[2,20,8,128]{3,2,1,0:T(8,128)(2,1)S(1)}, u32[]{:S(2)}, u32[]{:S(2)}) collective-permute-start(bf16[2,20,8,128]{3,2,1,0:T(8,128)(2,1)S(1)} %get-tuple-element.36), channel_id=1, source_target_pairs={{0,4},{1,5},{2,6},{3,7},{4,0},{5,1},{6,2},{7,3},{8,12},{9,13},{10,... | collective-permute-start | bytes 245768 | tf_op jit(solution)/shard_map/ppermute | solution.py:519
  84.8 15.9 %collective-permute-done.6.refs_1_ = bf16[2,20,8,128]{3,2,1,0:T(8,128)(2,1)S(1)} collective-permute-done((bf16[2,20,8,128]{3,2,1,0:T(8,128)(2,1)S(1)}, bf16[2,20,8,128]{3,2,1,0:T(8,128)(2,1)S(1)}, u32[]{:S(2)}, u32[]{:S(2)}) %collective-permute-start.6) | collective-permute-done | bytes 81952 | tf_op jit(solution)/shard_map/ppermute | solution.py:519
  100.7 1.8 %collective-permute-start.11 = (bf16[2,20,8,128]{3,2,1,0:T(8,128)(2,1)S(1)}, bf16[2,20,8,128]{3,2,1,0:T(8,128)(2,1)S(1)}, u32[]{:S(2)}, u32[]{:S(2)}) collective-permute-start(bf16[2,20,8,128]{3,2,1,0:T(8,128)(2,1)S(1)} %get-tuple-element.38), channel_id=1, source_target_pairs={{0,6},{1,7},{2,0},{3,1},{4,2},{5,3},{6,4},{7,5},{8,14},{9,15},{10,... | collective-permute-start | bytes 245768 | tf_op jit(solution)/shard_map/ppermute | solution.py:519
  102.5 1.8 %collective-permute-done.7.refs_2_ = bf16[2,20,8,128]{3,2,1,0:T(8,128)(2,1)S(1)} collective-permute-done((bf16[2,20,8,128]{3,2,1,0:T(8,128)(2,1)S(1)}, bf16[2,20,8,128]{3,2,1,0:T(8,128)(2,1)S(1)}, u32[]{:S(2)}, u32[]{:S(2)}) %collective-permute-start.7) | collective-permute-done | bytes 81952 | tf_op jit(solution)/shard_map/ppermute | solution.py:519
  105.7 1.7 %collective-permute-done.8.refs_3_ = bf16[2,20,8,128]{3,2,1,0:T(8,128)(2,1)S(1)} collective-permute-done((bf16[2,20,8,128]{3,2,1,0:T(8,128)(2,1)S(1)}, bf16[2,20,8,128]{3,2,1,0:T(8,128)(2,1)S(1)}, u32[]{:S(2)}, u32[]{:S(2)}) %collective-permute-start.8) | collective-permute-done | bytes 81952 | tf_op jit(solution)/shard_map/ppermute | solution.py:519
  107.4 6.6 %collective-permute-done.9.refs_4_ = bf16[2,20,8,128]{3,2,1,0:T(8,128)(2,1)S(1)} collective-permute-done((bf16[2,20,8,128]{3,2,1,0:T(8,128)(2,1)S(1)}, bf16[2,20,8,128]{3,2,1,0:T(8,128)(2,1)S(1)}, u32[]{:S(2)}, u32[]{:S(2)}) %collective-permute-start.9) | collective-permute-done | bytes 81952 | tf_op jit(solution)/shard_map/ppermute | solution.py:519
  117.1 2.2 %collective-permute-done.13 = f32[1,2,8,256]{3,2,1,0:T(8,128)S(1)} collective-permute-done((f32[1,2,8,256]{3,2,1,0:T(8,128)S(1)}, f32[1,2,8,256]{3,2,1,0:T(8,128)S(1)}, u32[]{:S(2)}, u32[]{:S(2)}) %collective-permute-start.13) | collective-permute-done | bytes 16416 | tf_op jit(solution)/shard_map/ppermute | solution.py:95
  121.7 2.5 %collective-permute-start.17 = (bf16[8,8,16,128]{3,2,1,0:T(8,128)(2,1)S(1)}, bf16[8,8,16,128]{3,2,1,0:T(8,128)(2,1)S(1)}, u32[]{:S(2)}, u32[]{:S(2)}) collective-permute-start(bf16[8,8,16,128]{3,2,1,0:T(8,128)(2,1)S(1)} %get-tuple-element.42), channel_id=1, source_target_pairs={{0,8},{1,9},{2,10},{3,11},{4,12},{5,13},{6,14},{7,15},{8,0},{9,1},... | collective-permute-start | bytes 786440 | tf_op jit(solution)/shard_map/ppermute | solution.py:544
  124.3 2.7 %collective-permute-start.15 = (f32[4,2,8,256]{3,2,1,0:T(8,128)S(1)}, f32[4,2,8,256]{3,2,1,0:T(8,128)S(1)}, u32[]{:S(2)}, u32[]{:S(2)}) collective-permute-start(f32[4,2,8,256]{3,2,1,0:T(8,128)S(1)} %pad_maximum_fusion.1), channel_id=1, source_target_pairs={{0,64},{16,80},{32,96},{48,112},{64,0},{80,16},{96,32},{112,48},{1... | collective-permute-start | bytes 196616 | tf_op jit(solution)/shard_map/ppermute | solution.py:95
  127.0 2.0 %collective-permute-done.15 = f32[4,2,8,256]{3,2,1,0:T(8,128)S(1)} collective-permute-done((f32[4,2,8,256]{3,2,1,0:T(8,128)S(1)}, f32[4,2,8,256]{3,2,1,0:T(8,128)S(1)}, u32[]{:S(2)}, u32[]{:S(2)}) %collective-permute-start.15) | collective-permute-done | bytes 65568 | tf_op jit(solution)/shard_map/ppermute | solution.py:95
  129.0 5.5 %collective-permute-start.16 = (f32[8,2,8,256]{3,2,1,0:T(8,128)S(1)}, f32[8,2,8,256]{3,2,1,0:T(8,128)S(1)}, u32[]{:S(2)}, u32[]{:S(2)}) collective-permute-start(f32[8,2,8,256]{3,2,1,0:T(8,128)S(1)} %pad_maximum_fusion), channel_id=1, source_target_pairs={{0,16},{16,0},{32,48},{48,32},{64,80},{80,64},{96,112},{112,96},{1... | collective-permute-start | bytes 393224 | tf_op jit(solution)/shard_map/ppermute | solution.py:95
  135.7 1.8 %collective-permute-start.19 = (bf16[2,8,16,128]{3,2,1,0:T(8,128)(2,1)S(1)}, bf16[2,8,16,128]{3,2,1,0:T(8,128)(2,1)S(1)}, u32[]{:S(2)}, u32[]{:S(2)}) collective-permute-start(bf16[2,8,16,128]{3,2,1,0:T(8,128)(2,1)S(1)} %get-tuple-element.45), channel_id=1, source_target_pairs={{0,2},{1,3},{2,4},{3,5},{4,6},{5,7},{6,0},{7,1},{8,10},{9,11},{10,... | collective-permute-start | bytes 196616 | tf_op jit(solution)/shard_map/ppermute | solution.py:519
  137.5 2.4 %collective-permute-start.20 = (bf16[2,8,16,128]{3,2,1,0:T(8,128)(2,1)}, bf16[2,8,16,128]{3,2,1,0:T(8,128)(2,1)S(1)}, u32[]{:S(2)}, u32[]{:S(2)}) collective-permute-start(bf16[2,8,16,128]{3,2,1,0:T(8,128)(2,1)} %get-tuple-element.46), channel_id=1, source_target_pairs={{0,3},{1,4},{2,5},{3,6},{4,7},{5,0},{6,1},{7,2},{8,11},{9,12},{10,... | collective-permute-start | bytes 196616 | tf_op jit(solution)/shard_map/ppermute | solution.py:519
  139.9 2.3 %collective-permute-start.21 = (bf16[2,8,16,128]{3,2,1,0:T(8,128)(2,1)}, bf16[2,8,16,128]{3,2,1,0:T(8,128)(2,1)S(1)}, u32[]{:S(2)}, u32[]{:S(2)}) collective-permute-start(bf16[2,8,16,128]{3,2,1,0:T(8,128)(2,1)} %get-tuple-element.47), channel_id=1, source_target_pairs={{0,4},{1,5},{2,6},{3,7},{4,0},{5,1},{6,2},{7,3},{8,12},{9,13},{10,... | collective-permute-start | bytes 196616 | tf_op jit(solution)/shard_map/ppermute | solution.py:519
  142.2 1.9 %collective-permute-start.22 = (bf16[2,8,16,128]{3,2,1,0:T(8,128)(2,1)S(1)}, bf16[2,8,16,128]{3,2,1,0:T(8,128)(2,1)S(1)}, u32[]{:S(2)}, u32[]{:S(2)}) collective-permute-start(bf16[2,8,16,128]{3,2,1,0:T(8,128)(2,1)S(1)} %get-tuple-element.48), channel_id=1, source_target_pairs={{0,5},{1,6},{2,7},{3,0},{4,1},{5,2},{6,3},{7,4},{8,13},{9,14},{10,... | collective-permute-start | bytes 196616 | tf_op jit(solution)/shard_map/ppermute | solution.py:519
  144.1 1.6 %collective-permute-start.23 = (bf16[2,8,16,128]{3,2,1,0:T(8,128)(2,1)S(1)}, bf16[2,8,16,128]{3,2,1,0:T(8,128)(2,1)S(1)}, u32[]{:S(2)}, u32[]{:S(2)}) collective-permute-start(bf16[2,8,16,128]{3,2,1,0:T(8,128)(2,1)S(1)} %get-tuple-element.49), channel_id=1, source_target_pairs={{0,6},{1,7},{2,0},{3,1},{4,2},{5,3},{6,4},{7,5},{8,14},{9,15},{10,... | collective-permute-start | bytes 196616 | tf_op jit(solution)/shard_map/ppermute | solution.py:519
  147.2 4.9 %inverse_transform.1 = (f32[8,16,48,128]{3,2,1,0:T(8,128)}, f32[8,16,16,128]{3,2,1,0:T(8,128)S(1)}) custom-call(s32[1]{0:T(128)} %bitcast.2.me_ref, f32[8]{0:T(128)S(1)} %dynamic-slice_multiply_fusion.bias_ref, f32[16,2,8,256]{3,2,1,0:T(8,128)S(1)} %constant_dynamic-update-slice_fusion.spec_ref, f32[16,256]{1,0:T(8,128)S(1)} %select_multiply_fusion.depth_ref, ...), custom_call_target="tpu_custom_call" | custom-call | flops 2000000000 | bytes 5000000 | tf_op jit(solution)/shard_map/inverse_transform/pallas_call | solution.py:416
  152.1 3.4 %finish_early.1 = (bf16[8,16,64,128]{3,2,1,0:T(8,128)(2,1)}, f32[8,16,48,128]{3,2,1,0:T(8,128)}) custom-call(bf16[16,8,48,128]{3,2,1,0:T(8,128)(2,1)S(1)} %all-to-all-done.1.coded_ref, f32[8,16,48,128]{3,2,1,0:T(8,128)} %get-tuple-element.53.inverse_ref), custom_call_target="tpu_custom_call", output_to_operand_aliasing={{1}: (1, {})} | custom-call | flops 30000000 | bytes 8000000 | tf_op jit(solution)/shard_map/finish_early/pallas_call | solution.py:468
  155.5 1.8 %finish_late.1 = bf16[8,16,64,128]{3,2,1,0:T(8,128)(2,1)} custom-call(s32[2]{0:T(128)S(1)} %pad_add_fusion.place_ref, f32[8,16,16,128]{3,2,1,0:T(8,128)S(1)} %get-tuple-element.40.inverse_ref, bf16[2,8,16,128]{3,2,1,0:T(8,128)(2,1)S(1)} %get-tuple-element.43.refs_0_, ...), custom_call_target="tpu_custom_call", output_to_operand_aliasing={{}: (10, {})} | custom-call | flops 4000000 | bytes 1200000 | tf_op jit(solution)/shard_map/finish_late/pallas_call | solution.py:503
  (83 shorter events, 16.4 us)
Async XLA Ops:
  2.7 12.2 %copy-start = (bf16[1,8,8,128,128]{4,3,2,1,0:T(8,128)(2,1)S(1)}, bf16[1,8,8,128,128]{4,3,2,1,0:T(8,128)(2,1)}, u32[]{:S(2)}) copy-start(bf16[1,8,8,128,128]{4,3,2,1,0:T(8,128)(2,1)} %param.8) | copy-start | bytes 6291460
  2.7 12.2 %copy-start.3 = (f32[256,32]{1,0:T(8,128)S(1)}, f32[256,32]{1,0:T(8,128)}, u32[]{:S(2)}) copy-start(f32[256,32]{1,0:T(8,128)} %constant.218.clone.table_y_ref.table_x_ref) | copy-start | bytes 98308
  2.8 49.7 %all-to-all-start = ((bf16[16,48,8,128]{3,2,1,0:T(8,128)(2,1)}), bf16[16,48,8,128]{3,2,1,0:T(8,128)(2,1)}, u32[]{:S(2)}, u32[]{:S(2)}) async-start(bf16[16,48,8,128]{3,2,1,0:T(8,128)(2,1)} %get-tuple-element.51), calls=%async_computation | async-start | bytes 3145728 | tf_op jit(solution)/shard_map/all_to_all | solution.py:532
  17.5 4.2 %collective-permute-start.1 = (f32[2,2,2,2,8,256]{5,4,3,2,0,1:T(8,128)S(1)}, f32[2,2,2,2,8,256]{5,4,3,2,0,1:T(8,128)S(1)}, u32[]{:S(2)}, u32[]{:S(2)}) collective-permute-start(f32[2,2,2,2,8,256]{5,4,3,2,0,1:T(8,128)S(1)} %bitcast.40), channel_id=1, source_target_pairs={{0,16},{16,0},{32,48},{48,32},{64,80},{80,64},{96,112},{112,96},{1... | collective-permute-start | bytes 393224 | tf_op jit(solution)/shard_map/ppermute | solution.py:80
  18.6 55.2 %collective-permute-start = (bf16[8,16,8,128]{3,2,1,0:T(8,128)(2,1)S(1)}, bf16[8,16,8,128]{3,2,1,0:T(8,128)(2,1)S(1)}, u32[]{:S(2)}, u32[]{:S(2)}) collective-permute-start(bf16[8,16,8,128]{3,2,1,0:T(8,128)(2,1)S(1)} %copy-done.7), channel_id=1, source_target_pairs={{0,8},{1,9},{2,10},{3,11},{4,12},{5,13},{6,14},{7,15},{8,0},{9,1},... | collective-permute-start | bytes 786440 | tf_op jit(solution)/shard_map/ppermute | solution.py:533
  21.7 5.1 %collective-permute-start.2 = (f32[2,2,2,8,256]{4,3,2,1,0:T(8,128)S(1)}, f32[2,2,2,8,256]{4,3,2,1,0:T(8,128)S(1)}, u32[]{:S(2)}, u32[]{:S(2)}) collective-permute-start(f32[2,2,2,8,256]{4,3,2,1,0:T(8,128)S(1)} %dynamic-slice_bitcast_fusion), channel_id=1, source_target_pairs={{0,64},{16,80},{32,96},{48,112},{64,0},{80,16},{96,32},{112,48},{1... | collective-permute-start | bytes 196616 | tf_op jit(solution)/shard_map/ppermute | solution.py:80
  55.9 17.9 %copy-start.2 = (bf16[8,16,8,128]{3,2,1,0:T(8,128)(2,1)S(1)}, bf16[8,16,8,128]{3,2,1,0:T(8,128)(2,1)}, u32[]{:S(2)}) copy-start(bf16[8,16,8,128]{3,2,1,0:T(8,128)(2,1)} %get-tuple-element.30.own_cells_ref) | copy-start | bytes 786436
  55.9 96.2 %all-to-all-start.1 = ((bf16[16,8,48,128]{3,2,1,0:T(8,128)(2,1)}), bf16[16,8,48,128]{3,2,1,0:T(8,128)(2,1)S(1)}, u32[]{:S(2)}, u32[]{:S(2)}) async-start(bf16[16,8,48,128]{3,2,1,0:T(8,128)(2,1)} %get-tuple-element.52), calls=%async_computation.1 | async-start | bytes 3145728 | tf_op jit(solution)/shard_map/all_to_all | solution.py:541
  62.6 54.4 %copy-start.8 = (f32[128]{0:T(128)S(1)}, f32[128]{0:T(128)}, u32[]{:S(2)}) copy-start(f32[128]{0:T(128)} %param.10) | copy-start | bytes 1540
  62.7 2.9 %collective-permute-start.3 = (f32[2,2,8,256]{3,2,1,0:T(8,128)S(1)}, f32[2,2,8,256]{3,2,1,0:T(8,128)S(1)}, u32[]{:S(2)}, u32[]{:S(2)}) collective-permute-start(f32[2,2,8,256]{3,2,1,0:T(8,128)S(1)} %dynamic-slice_bitcast_fusion.1), channel_id=1, source_target_pairs={{0,32},{16,48},{32,0},{48,16},{64,96},{80,112},{96,64},{112,80},{1... | collective-permute-start | bytes 98312 | tf_op jit(solution)/shard_map/ppermute | solution.py:80
  65.5 3.0 %collective-permute-start.4 = (f32[2,8,256]{2,1,0:T(8,128)S(1)}, f32[2,8,256]{2,1,0:T(8,128)S(1)}, u32[]{:S(2)}, u32[]{:S(2)}) collective-permute-start(f32[2,8,256]{2,1,0:T(8,128)S(1)} %dynamic-slice_bitcast_fusion.2), channel_id=1, source_target_pairs={{0,128},{16,144},{32,160},{48,176},{64,192},{80,208},{96,224},{112... | collective-permute-start | bytes 49160 | tf_op jit(solution)/shard_map/ppermute | solution.py:80
  68.5 5.2 %collective-permute-start.5 = (bf16[4,8,128]{2,1,0:T(8,128)(2,1)S(1)}, bf16[4,8,128]{2,1,0:T(8,128)(2,1)S(1)}, u32[]{:S(2)}, u32[]{:S(2)}) collective-permute-start(bf16[4,8,128]{2,1,0:T(8,128)(2,1)S(1)} %bitcast.38), channel_id=1, source_target_pairs={{0,8},{1,9},{2,10},{3,11},{4,12},{5,13},{6,14},{7,15},{8,0},{9,1},... | collective-permute-start | bytes 24584 | tf_op jit(solution)/shard_map/ppermute | solution.py:537
  74.4 26.3 %collective-permute-start.6 = (bf16[2,20,8,128]{3,2,1,0:T(8,128)(2,1)S(1)}, bf16[2,20,8,128]{3,2,1,0:T(8,128)(2,1)S(1)}, u32[]{:S(2)}, u32[]{:S(2)}) collective-permute-start(bf16[2,20,8,128]{3,2,1,0:T(8,128)(2,1)S(1)} %get-tuple-element.33), channel_id=1, source_target_pairs={{0,1},{1,2},{2,3},{3,4},{4,5},{5,6},{6,7},{7,0},{8,9},{9,10},{10,1... | collective-permute-start | bytes 245768 | tf_op jit(solution)/shard_map/ppermute | solution.py:519
  75.2 29.1 %collective-permute-start.7 = (bf16[2,20,8,128]{3,2,1,0:T(8,128)(2,1)S(1)}, bf16[2,20,8,128]{3,2,1,0:T(8,128)(2,1)S(1)}, u32[]{:S(2)}, u32[]{:S(2)}) collective-permute-start(bf16[2,20,8,128]{3,2,1,0:T(8,128)(2,1)S(1)} %get-tuple-element.34), channel_id=1, source_target_pairs={{0,2},{1,3},{2,4},{3,5},{4,6},{5,7},{6,0},{7,1},{8,10},{9,11},{10,... | collective-permute-start | bytes 245768 | tf_op jit(solution)/shard_map/ppermute | solution.py:519
  79.2 28.2 %collective-permute-start.8 = (bf16[2,20,8,128]{3,2,1,0:T(8,128)(2,1)S(1)}, bf16[2,20,8,128]{3,2,1,0:T(8,128)(2,1)S(1)}, u32[]{:S(2)}, u32[]{:S(2)}) collective-permute-start(bf16[2,20,8,128]{3,2,1,0:T(8,128)(2,1)S(1)} %get-tuple-element.35), channel_id=1, source_target_pairs={{0,3},{1,4},{2,5},{3,6},{4,7},{5,0},{6,1},{7,2},{8,11},{9,12},{10,... | collective-permute-start | bytes 245768 | tf_op jit(solution)/shard_map/ppermute | solution.py:519
  79.8 34.2 %collective-permute-start.9 = (bf16[2,20,8,128]{3,2,1,0:T(8,128)(2,1)S(1)}, bf16[2,20,8,128]{3,2,1,0:T(8,128)(2,1)S(1)}, u32[]{:S(2)}, u32[]{:S(2)}) collective-permute-start(bf16[2,20,8,128]{3,2,1,0:T(8,128)(2,1)S(1)} %get-tuple-element.36), channel_id=1, source_target_pairs={{0,4},{1,5},{2,6},{3,7},{4,0},{5,1},{6,2},{7,3},{8,12},{9,13},{10,... | collective-permute-start | bytes 245768 | tf_op jit(solution)/shard_map/ppermute | solution.py:519
  84.8 29.2 %collective-permute-start.10 = (bf16[2,20,8,128]{3,2,1,0:T(8,128)(2,1)S(1)}, bf16[2,20,8,128]{3,2,1,0:T(8,128)(2,1)S(1)}, u32[]{:S(2)}, u32[]{:S(2)}) collective-permute-start(bf16[2,20,8,128]{3,2,1,0:T(8,128)(2,1)S(1)} %get-tuple-element.37), channel_id=1, source_target_pairs={{0,5},{1,6},{2,7},{3,0},{4,1},{5,2},{6,3},{7,4},{8,13},{9,14},{10,... | collective-permute-start | bytes 245768 | tf_op jit(solution)/shard_map/ppermute | solution.py:519
  100.7 13.3 %collective-permute-start.11 = (bf16[2,20,8,128]{3,2,1,0:T(8,128)(2,1)S(1)}, bf16[2,20,8,128]{3,2,1,0:T(8,128)(2,1)S(1)}, u32[]{:S(2)}, u32[]{:S(2)}) collective-permute-start(bf16[2,20,8,128]{3,2,1,0:T(8,128)(2,1)S(1)} %get-tuple-element.38), channel_id=1, source_target_pairs={{0,6},{1,7},{2,0},{3,1},{4,2},{5,3},{6,4},{7,5},{8,14},{9,15},{10,... | collective-permute-start | bytes 245768 | tf_op jit(solution)/shard_map/ppermute | solution.py:519
  104.3 9.7 %collective-permute-start.12 = (bf16[2,20,8,128]{3,2,1,0:T(8,128)(2,1)S(1)}, bf16[2,20,8,128]{3,2,1,0:T(8,128)(2,1)S(1)}, u32[]{:S(2)}, u32[]{:S(2)}) collective-permute-start(bf16[2,20,8,128]{3,2,1,0:T(8,128)(2,1)S(1)} %get-tuple-element.39), channel_id=1, source_target_pairs={{0,7},{1,0},{2,1},{3,2},{4,3},{5,4},{6,5},{7,6},{8,15},{9,8},{10,9... | collective-permute-start | bytes 245768 | tf_op jit(solution)/shard_map/ppermute | solution.py:519
  115.6 31.5 %copy-start.5 = (f32[2,16,128]{2,1,0:T(8,128)S(1)}, f32[2,16,128]{2,1,0:T(8,128)}, u32[]{:S(2)}) copy-start(f32[2,16,128]{2,1,0:T(8,128)} %constant.219.clone.waves_y_ref) | copy-start | bytes 49156
  116.6 2.7 %collective-permute-start.13 = (f32[1,2,8,256]{3,2,1,0:T(8,128)S(1)}, f32[1,2,8,256]{3,2,1,0:T(8,128)S(1)}, u32[]{:S(2)}, u32[]{:S(2)}) collective-permute-start(f32[1,2,8,256]{3,2,1,0:T(8,128)S(1)} %bitcast.34), channel_id=1, source_target_pairs={{0,128},{16,144},{32,160},{48,176},{64,192},{80,208},{96,224},{112... | collective-permute-start | bytes 49160 | tf_op jit(solution)/shard_map/ppermute | solution.py:95
  119.3 4.9 %collective-permute-start.14 = (f32[2,2,8,256]{3,2,1,0:T(8,128)S(1)}, f32[2,2,8,256]{3,2,1,0:T(8,128)S(1)}, u32[]{:S(2)}, u32[]{:S(2)}) collective-permute-start(f32[2,2,8,256]{3,2,1,0:T(8,128)S(1)} %pad_maximum_fusion.2), channel_id=1, source_target_pairs={{0,32},{16,48},{32,0},{48,16},{64,96},{80,112},{96,64},{112,80},{1... | collective-permute-start | bytes 98312 | tf_op jit(solution)/shard_map/ppermute | solution.py:95
  121.7 12.8 %collective-permute-start.17 = (bf16[8,8,16,128]{3,2,1,0:T(8,128)(2,1)S(1)}, bf16[8,8,16,128]{3,2,1,0:T(8,128)(2,1)S(1)}, u32[]{:S(2)}, u32[]{:S(2)}) collective-permute-start(bf16[8,8,16,128]{3,2,1,0:T(8,128)(2,1)S(1)} %get-tuple-element.42), channel_id=1, source_target_pairs={{0,8},{1,9},{2,10},{3,11},{4,12},{5,13},{6,14},{7,15},{8,0},{9,1},... | collective-permute-start | bytes 786440 | tf_op jit(solution)/shard_map/ppermute | solution.py:544
  124.3 4.7 %collective-permute-start.15 = (f32[4,2,8,256]{3,2,1,0:T(8,128)S(1)}, f32[4,2,8,256]{3,2,1,0:T(8,128)S(1)}, u32[]{:S(2)}, u32[]{:S(2)}) collective-permute-start(f32[4,2,8,256]{3,2,1,0:T(8,128)S(1)} %pad_maximum_fusion.1), channel_id=1, source_target_pairs={{0,64},{16,80},{32,96},{48,112},{64,0},{80,16},{96,32},{112,48},{1... | collective-permute-start | bytes 196616 | tf_op jit(solution)/shard_map/ppermute | solution.py:95
  129.0 8.5 %collective-permute-start.16 = (f32[8,2,8,256]{3,2,1,0:T(8,128)S(1)}, f32[8,2,8,256]{3,2,1,0:T(8,128)S(1)}, u32[]{:S(2)}, u32[]{:S(2)}) collective-permute-start(f32[8,2,8,256]{3,2,1,0:T(8,128)S(1)} %pad_maximum_fusion), channel_id=1, source_target_pairs={{0,16},{16,0},{32,48},{48,32},{64,80},{80,64},{96,112},{112,96},{1... | collective-permute-start | bytes 393224 | tf_op jit(solution)/shard_map/ppermute | solution.py:95
  135.7 8.4 %collective-permute-start.18 = (bf16[2,8,16,128]{3,2,1,0:T(8,128)(2,1)S(1)}, bf16[2,8,16,128]{3,2,1,0:T(8,128)(2,1)S(1)}, u32[]{:S(2)}, u32[]{:S(2)}) collective-permute-start(bf16[2,8,16,128]{3,2,1,0:T(8,128)(2,1)S(1)} %get-tuple-element.44), channel_id=1, source_target_pairs={{0,1},{1,2},{2,3},{3,4},{4,5},{5,6},{6,7},{7,0},{8,9},{9,10},{10,1... | collective-permute-start | bytes 196616 | tf_op jit(solution)/shard_map/ppermute | solution.py:519
  135.7 10.0 %collective-permute-start.19 = (bf16[2,8,16,128]{3,2,1,0:T(8,128)(2,1)S(1)}, bf16[2,8,16,128]{3,2,1,0:T(8,128)(2,1)S(1)}, u32[]{:S(2)}, u32[]{:S(2)}) collective-permute-start(bf16[2,8,16,128]{3,2,1,0:T(8,128)(2,1)S(1)} %get-tuple-element.45), channel_id=1, source_target_pairs={{0,2},{1,3},{2,4},{3,5},{4,6},{5,7},{6,0},{7,1},{8,10},{9,11},{10,... | collective-permute-start | bytes 196616 | tf_op jit(solution)/shard_map/ppermute | solution.py:519
  137.5 17.9 %collective-permute-start.20 = (bf16[2,8,16,128]{3,2,1,0:T(8,128)(2,1)}, bf16[2,8,16,128]{3,2,1,0:T(8,128)(2,1)S(1)}, u32[]{:S(2)}, u32[]{:S(2)}) collective-permute-start(bf16[2,8,16,128]{3,2,1,0:T(8,128)(2,1)} %get-tuple-element.46), channel_id=1, source_target_pairs={{0,3},{1,4},{2,5},{3,6},{4,7},{5,0},{6,1},{7,2},{8,11},{9,12},{10,... | collective-permute-start | bytes 196616 | tf_op jit(solution)/shard_map/ppermute | solution.py:519
  139.9 15.6 %collective-permute-start.21 = (bf16[2,8,16,128]{3,2,1,0:T(8,128)(2,1)}, bf16[2,8,16,128]{3,2,1,0:T(8,128)(2,1)S(1)}, u32[]{:S(2)}, u32[]{:S(2)}) collective-permute-start(bf16[2,8,16,128]{3,2,1,0:T(8,128)(2,1)} %get-tuple-element.47), channel_id=1, source_target_pairs={{0,4},{1,5},{2,6},{3,7},{4,0},{5,1},{6,2},{7,3},{8,12},{9,13},{10,... | collective-permute-start | bytes 196616 | tf_op jit(solution)/shard_map/ppermute | solution.py:519
  142.2 13.3 %collective-permute-start.22 = (bf16[2,8,16,128]{3,2,1,0:T(8,128)(2,1)S(1)}, bf16[2,8,16,128]{3,2,1,0:T(8,128)(2,1)S(1)}, u32[]{:S(2)}, u32[]{:S(2)}) collective-permute-start(bf16[2,8,16,128]{3,2,1,0:T(8,128)(2,1)S(1)} %get-tuple-element.48), channel_id=1, source_target_pairs={{0,5},{1,6},{2,7},{3,0},{4,1},{5,2},{6,3},{7,4},{8,13},{9,14},{10,... | collective-permute-start | bytes 196616 | tf_op jit(solution)/shard_map/ppermute | solution.py:519
  144.1 11.4 %collective-permute-start.23 = (bf16[2,8,16,128]{3,2,1,0:T(8,128)(2,1)S(1)}, bf16[2,8,16,128]{3,2,1,0:T(8,128)(2,1)S(1)}, u32[]{:S(2)}, u32[]{:S(2)}) collective-permute-start(bf16[2,8,16,128]{3,2,1,0:T(8,128)(2,1)S(1)} %get-tuple-element.49), channel_id=1, source_target_pairs={{0,6},{1,7},{2,0},{3,1},{4,2},{5,3},{6,4},{7,5},{8,14},{9,15},{10,... | collective-permute-start | bytes 196616 | tf_op jit(solution)/shard_map/ppermute | solution.py:519
  145.8 9.8 %collective-permute-start.24 = (bf16[2,8,16,128]{3,2,1,0:T(8,128)(2,1)S(1)}, bf16[2,8,16,128]{3,2,1,0:T(8,128)(2,1)S(1)}, u32[]{:S(2)}, u32[]{:S(2)}) collective-permute-start(bf16[2,8,16,128]{3,2,1,0:T(8,128)(2,1)S(1)} %get-tuple-element.50), channel_id=1, source_target_pairs={{0,7},{1,0},{2,1},{3,2},{4,3},{5,4},{6,5},{7,6},{8,15},{9,8},{10,9... | collective-permute-start | bytes 196616 | tf_op jit(solution)/shard_map/ppermute | solution.py:519
  (4 other events, 28.0 us)

commit v6 on v5

--- a/solution.py
+++ b/solution.py
@@ -14,7 +14,6 @@
 BLOCKS = 16
 LATE = 16
 EARLY = 64 - LATE
-PRECISE = lax.Precision.HIGHEST
 CELL_SCALE = 2.0**20
 COEF_SCALE = 2.0**6
 WHOLE = pl.BlockSpec(memory_space=pltpu.VMEM)
@@ -39,13 +38,17 @@
     return 2.0 * math.pi * turns.astype(jnp.float32) / GRID, row, lane
 
 
-def exact_dot(left, right):
-    return jnp.dot(left, right, precision=PRECISE, preferred_element_type=jnp.float32)
-
-
 def split(value):
     high = value.astype(jnp.bfloat16)
     return high, (value - high.astype(jnp.float32)).astype(jnp.bfloat16)
+
+
+def exact_dot(left, right):
+    left_high, left_low = split(left)
+    right_high, right_low = split(right)
+    total = jnp.dot(left_high, right_low, preferred_element_type=jnp.float32)
+    total += jnp.dot(left_low, right_high, preferred_element_type=jnp.float32)
+    return total + jnp.dot(left_high, right_high, preferred_element_type=jnp.float32)
 
 
 def encode(value, scale):

time: 158 us -> 158 us (level)
  transfers between devices with their start and end apart: 27 -> 27, of which waited for: 11 -> 13; matrix products, arithmetic and copies ran while one was open for 0% -> 0% of each run, Pallas kernels for 12% -> 11%
where the time goes in v6:
time: 158 us; the launch traced here: 157 us
  starting transfers between devices  67.7 us (43%)
  waiting for transfers between devices  64.9 us (41%)
  Pallas kernels  21.7 us (14%)
  local copies, waits for them, and re-layouts  1.73 us (1%)
    ppermute x14, waiting for transfers between devices, z_letters(): arrived.append(lax.ppermute(letters[k], 'chan', chan_perm(0, k)))  26.3 us
    all_to_all x1, waiting for transfers between devices, on_device(): cells = lax.all_to_all(cells, 'chan', 0, 0, tiled=True)  26.1 us
    ppermute x14, starting transfers between devices, z_letters(): arrived.append(lax.ppermute(letters[k], 'chan', chan_perm(0, k)))  24.9 us
    all_to_all x1, starting transfers between devices, on_device(): cells = lax.all_to_all(cells, 'chan', 0, 0, tiled=True)  11.8 us
    ppermute x4, starting transfers between devices, slab_gather(): other = lax.ppermute(value, 'slab', slab_perm(*step))  9.9 us
    all_to_all x1, starting transfers between devices, on_device(): coded = lax.all_to_all(coded, 'chan', 0, 0, tiled=True)  6.76 us
    ppermute x4, waiting for transfers between devices, halve(): return own + lax.ppermute(other, 'slab', perm)  6.13 us
    ppermute x4, starting transfers between devices, halve(): return own + lax.ppermute(other, 'slab', perm)  5.82 us
  transfers between devices with their start and end apart: 27, of which 13 were waited for; matrix products, arithmetic and copies ran while one was open for 0% of the time, Pallas kernels for 11%

profile of v6, /device:TPU:1, one launch (start us, length us, event | category | flops | bytes accessed | tf_op | source)
XLA Modules:
  0.0 157.2 jit_solution(13489265355043452019)
XLA Ops:
  0.0 2.7 %cut.1 = (bf16[16,48,8,128]{3,2,1,0:T(8,128)(2,1)}, bf16[8,16,8,128]{3,2,1,0:T(8,128)(2,1)}, bf16[8,16,8,128]{3,2,1,0:T(8,128)(2,1)}) custom-call(bf16[8,16,64,128]{3,2,1,0:T(8,128)(2,1)} %bitcast.31), custom_call_target="tpu_custom_call" | custom-call | flops 1000000 | bytes 4000000 | tf_op jit(solution)/shard_map/cut/pallas_call | solution.py:184
  2.8 11.8 %all-to-all-start = ((bf16[16,48,8,128]{3,2,1,0:T(8,128)(2,1)}), bf16[16,48,8,128]{3,2,1,0:T(8,128)(2,1)}, u32[]{:S(2)}, u32[]{:S(2)}) async-start(bf16[16,48,8,128]{3,2,1,0:T(8,128)(2,1)} %get-tuple-element.51), calls=%async_computation | async-start | bytes 3145728 | tf_op jit(solution)/shard_map/all_to_all | solution.py:535
  14.9 2.1 %forward_transform.1 = f32[16,2,8,256]{3,2,1,0:T(8,128)S(1)} custom-call(bf16[8,8,128,128]{3,2,1,0:T(8,128)(2,1)S(1)} %bitcast.32, bf16[32,128]{1,0:T(8,128)(2,1)S(1)} %copy-done.4, f32[256,32]{1,0:T(8,128)S(1)} %copy-done.3, f32[16,512]{1,0:T(8,128)S(1)} %fusion.3.depth_ref), custom_call_target="tpu_custom_call" | custom-call | flops 200000000 | bytes 3000000 | tf_op jit(solution)/shard_map/forward_transform/pallas_call | solution.py:136
  18.1 3.1 %collective-permute-start = (bf16[8,16,8,128]{3,2,1,0:T(8,128)(2,1)S(1)}, bf16[8,16,8,128]{3,2,1,0:T(8,128)(2,1)S(1)}, u32[]{:S(2)}, u32[]{:S(2)}) collective-permute-start(bf16[8,16,8,128]{3,2,1,0:T(8,128)(2,1)S(1)} %copy-done.7), channel_id=1, source_target_pairs={{0,8},{1,9},{2,10},{3,11},{4,12},{5,13},{6,14},{7,15},{8,0},{9,1},... | collective-permute-start | bytes 786440 | tf_op jit(solution)/shard_map/ppermute | solution.py:536
  21.2 3.0 %collective-permute-start.2 = (f32[2,2,2,8,256]{4,3,2,1,0:T(8,128)S(1)}, f32[2,2,2,8,256]{4,3,2,1,0:T(8,128)S(1)}, u32[]{:S(2)}, u32[]{:S(2)}) collective-permute-start(f32[2,2,2,8,256]{4,3,2,1,0:T(8,128)S(1)} %dynamic-slice_bitcast_fusion), channel_id=1, source_target_pairs={{0,64},{16,80},{32,96},{48,112},{64,0},{80,16},{96,32},{112,48},{1... | collective-permute-start | bytes 196616 | tf_op jit(solution)/shard_map/ppermute | solution.py:83
  24.2 2.1 %collective-permute-done.2 = f32[2,2,2,8,256]{4,3,2,1,0:T(8,128)S(1)} collective-permute-done((f32[2,2,2,8,256]{4,3,2,1,0:T(8,128)S(1)}, f32[2,2,2,8,256]{4,3,2,1,0:T(8,128)S(1)}, u32[]{:S(2)}, u32[]{:S(2)}) %collective-permute-start.2) | collective-permute-done | bytes 65568 | tf_op jit(solution)/shard_map/ppermute | solution.py:83
  26.3 26.1 %all-to-all-done.cells_ref = bf16[16,48,8,128]{3,2,1,0:T(8,128)(2,1)} async-done(((bf16[16,48,8,128]{3,2,1,0:T(8,128)(2,1)}), bf16[16,48,8,128]{3,2,1,0:T(8,128)(2,1)}, u32[]{:S(2)}, u32[]{:S(2)}) %all-to-all-start) | async-done | bytes 1572896 | tf_op jit(solution)/shard_map/all_to_all | solution.py:535
  52.4 3.4 %map_early.1 = (bf16[16,8,48,128]{3,2,1,0:T(8,128)(2,1)}, bf16[16,48,8,128]{3,2,1,0:T(8,128)(2,1)}) custom-call(bf16[128,128]{1,0:T(8,128)(2,1)S(1)} %broadcast_multiply_fusion.weight_ref, bf16[16,48,8,128]{3,2,1,0:T(8,128)(2,1)} %all-to-all-done.cells_ref), custom_call_target="tpu_custom_call", output_to_operand_aliasing={{1}: (1, {})} | custom-call | flops 270000000 | bytes 4000000 | tf_op jit(solution)/shard_map/map_early/pallas_call | solution.py:238
  55.9 6.8 %all-to-all-start.1 = ((bf16[16,8,48,128]{3,2,1,0:T(8,128)(2,1)}), bf16[16,8,48,128]{3,2,1,0:T(8,128)(2,1)S(1)}, u32[]{:S(2)}, u32[]{:S(2)}) async-start(bf16[16,8,48,128]{3,2,1,0:T(8,128)(2,1)} %get-tuple-element.52), calls=%async_computation.1 | async-start | bytes 3145728 | tf_op jit(solution)/shard_map/all_to_all | solution.py:544
  65.9 2.6 %collective-permute-done.4 = f32[2,8,256]{2,1,0:T(8,128)S(1)} collective-permute-done((f32[2,8,256]{2,1,0:T(8,128)S(1)}, f32[2,8,256]{2,1,0:T(8,128)S(1)}, u32[]{:S(2)}, u32[]{:S(2)}) %collective-permute-start.4) | collective-permute-done | bytes 16416 | tf_op jit(solution)/shard_map/ppermute | solution.py:83
  68.5 3.0 %collective-permute-start.5 = (bf16[4,8,128]{2,1,0:T(8,128)(2,1)S(1)}, bf16[4,8,128]{2,1,0:T(8,128)(2,1)S(1)}, u32[]{:S(2)}, u32[]{:S(2)}) collective-permute-start(bf16[4,8,128]{2,1,0:T(8,128)(2,1)S(1)} %bitcast.38), channel_id=1, source_target_pairs={{0,8},{1,9},{2,10},{3,11},{4,12},{5,13},{6,14},{7,15},{8,0},{9,1},... | collective-permute-start | bytes 24584 | tf_op jit(solution)/shard_map/ppermute | solution.py:540
  71.6 2.2 %collective-permute-done.5.other_coef_ref = bf16[4,8,128]{2,1,0:T(8,128)(2,1)S(1)} collective-permute-done((bf16[4,8,128]{2,1,0:T(8,128)(2,1)S(1)}, bf16[4,8,128]{2,1,0:T(8,128)(2,1)S(1)}, u32[]{:S(2)}, u32[]{:S(2)}) %collective-permute-start.5) | collective-permute-done | bytes 8224 | tf_op jit(solution)/shard_map/ppermute | solution.py:540
  75.2 4.1 %collective-permute-start.7 = (bf16[2,20,8,128]{3,2,1,0:T(8,128)(2,1)S(1)}, bf16[2,20,8,128]{3,2,1,0:T(8,128)(2,1)S(1)}, u32[]{:S(2)}, u32[]{:S(2)}) collective-permute-start(bf16[2,20,8,128]{3,2,1,0:T(8,128)(2,1)S(1)} %get-tuple-element.34), channel_id=1, source_target_pairs={{0,2},{1,3},{2,4},{3,5},{4,6},{5,7},{6,0},{7,1},{8,10},{9,11},{10,... | collective-permute-start | bytes 245768 | tf_op jit(solution)/shard_map/ppermute | solution.py:522
  79.8 5.0 %collective-permute-start.9 = (bf16[2,20,8,128]{3,2,1,0:T(8,128)(2,1)S(1)}, bf16[2,20,8,128]{3,2,1,0:T(8,128)(2,1)S(1)}, u32[]{:S(2)}, u32[]{:S(2)}) collective-permute-start(bf16[2,20,8,128]{3,2,1,0:T(8,128)(2,1)S(1)} %get-tuple-element.36), channel_id=1, source_target_pairs={{0,4},{1,5},{2,6},{3,7},{4,0},{5,1},{6,2},{7,3},{8,12},{9,13},{10,... | collective-permute-start | bytes 245768 | tf_op jit(solution)/shard_map/ppermute | solution.py:522
  84.8 15.9 %collective-permute-done.6.refs_1_ = bf16[2,20,8,128]{3,2,1,0:T(8,128)(2,1)S(1)} collective-permute-done((bf16[2,20,8,128]{3,2,1,0:T(8,128)(2,1)S(1)}, bf16[2,20,8,128]{3,2,1,0:T(8,128)(2,1)S(1)}, u32[]{:S(2)}, u32[]{:S(2)}) %collective-permute-start.6) | collective-permute-done | bytes 81952 | tf_op jit(solution)/shard_map/ppermute | solution.py:522
  100.7 1.8 %collective-permute-start.11 = (bf16[2,20,8,128]{3,2,1,0:T(8,128)(2,1)S(1)}, bf16[2,20,8,128]{3,2,1,0:T(8,128)(2,1)S(1)}, u32[]{:S(2)}, u32[]{:S(2)}) collective-permute-start(bf16[2,20,8,128]{3,2,1,0:T(8,128)(2,1)S(1)} %get-tuple-element.38), channel_id=1, source_target_pairs={{0,6},{1,7},{2,0},{3,1},{4,2},{5,3},{6,4},{7,5},{8,14},{9,15},{10,... | collective-permute-start | bytes 245768 | tf_op jit(solution)/shard_map/ppermute | solution.py:522
  102.5 1.8 %collective-permute-done.7.refs_2_ = bf16[2,20,8,128]{3,2,1,0:T(8,128)(2,1)S(1)} collective-permute-done((bf16[2,20,8,128]{3,2,1,0:T(8,128)(2,1)S(1)}, bf16[2,20,8,128]{3,2,1,0:T(8,128)(2,1)S(1)}, u32[]{:S(2)}, u32[]{:S(2)}) %collective-permute-start.7) | collective-permute-done | bytes 81952 | tf_op jit(solution)/shard_map/ppermute | solution.py:522
  105.7 1.7 %collective-permute-done.8.refs_3_ = bf16[2,20,8,128]{3,2,1,0:T(8,128)(2,1)S(1)} collective-permute-done((bf16[2,20,8,128]{3,2,1,0:T(8,128)(2,1)S(1)}, bf16[2,20,8,128]{3,2,1,0:T(8,128)(2,1)S(1)}, u32[]{:S(2)}, u32[]{:S(2)}) %collective-permute-start.8) | collective-permute-done | bytes 81952 | tf_op jit(solution)/shard_map/ppermute | solution.py:522
  107.4 6.6 %collective-permute-done.9.refs_4_ = bf16[2,20,8,128]{3,2,1,0:T(8,128)(2,1)S(1)} collective-permute-done((bf16[2,20,8,128]{3,2,1,0:T(8,128)(2,1)S(1)}, bf16[2,20,8,128]{3,2,1,0:T(8,128)(2,1)S(1)}, u32[]{:S(2)}, u32[]{:S(2)}) %collective-permute-start.9) | collective-permute-done | bytes 81952 | tf_op jit(solution)/shard_map/ppermute | solution.py:522
  117.1 2.2 %collective-permute-done.13 = f32[1,2,8,256]{3,2,1,0:T(8,128)S(1)} collective-permute-done((f32[1,2,8,256]{3,2,1,0:T(8,128)S(1)}, f32[1,2,8,256]{3,2,1,0:T(8,128)S(1)}, u32[]{:S(2)}, u32[]{:S(2)}) %collective-permute-start.13) | collective-permute-done | bytes 16416 | tf_op jit(solution)/shard_map/ppermute | solution.py:98
  121.7 2.5 %collective-permute-start.17 = (bf16[8,8,16,128]{3,2,1,0:T(8,128)(2,1)S(1)}, bf16[8,8,16,128]{3,2,1,0:T(8,128)(2,1)S(1)}, u32[]{:S(2)}, u32[]{:S(2)}) collective-permute-start(bf16[8,8,16,128]{3,2,1,0:T(8,128)(2,1)S(1)} %get-tuple-element.42), channel_id=1, source_target_pairs={{0,8},{1,9},{2,10},{3,11},{4,12},{5,13},{6,14},{7,15},{8,0},{9,1},... | collective-permute-start | bytes 786440 | tf_op jit(solution)/shard_map/ppermute | solution.py:547
  124.3 2.7 %collective-permute-start.15 = (f32[4,2,8,256]{3,2,1,0:T(8,128)S(1)}, f32[4,2,8,256]{3,2,1,0:T(8,128)S(1)}, u32[]{:S(2)}, u32[]{:S(2)}) collective-permute-start(f32[4,2,8,256]{3,2,1,0:T(8,128)S(1)} %pad_maximum_fusion.1), channel_id=1, source_target_pairs={{0,64},{16,80},{32,96},{48,112},{64,0},{80,16},{96,32},{112,48},{1... | collective-permute-start | bytes 196616 | tf_op jit(solution)/shard_map/ppermute | solution.py:98
  127.0 2.0 %collective-permute-done.15 = f32[4,2,8,256]{3,2,1,0:T(8,128)S(1)} collective-permute-done((f32[4,2,8,256]{3,2,1,0:T(8,128)S(1)}, f32[4,2,8,256]{3,2,1,0:T(8,128)S(1)}, u32[]{:S(2)}, u32[]{:S(2)}) %collective-permute-start.15) | collective-permute-done | bytes 65568 | tf_op jit(solution)/shard_map/ppermute | solution.py:98
  129.0 5.5 %collective-permute-start.16 = (f32[8,2,8,256]{3,2,1,0:T(8,128)S(1)}, f32[8,2,8,256]{3,2,1,0:T(8,128)S(1)}, u32[]{:S(2)}, u32[]{:S(2)}) collective-permute-start(f32[8,2,8,256]{3,2,1,0:T(8,128)S(1)} %pad_maximum_fusion), channel_id=1, source_target_pairs={{0,16},{16,0},{32,48},{48,32},{64,80},{80,64},{96,112},{112,96},{1... | collective-permute-start | bytes 393224 | tf_op jit(solution)/shard_map/ppermute | solution.py:98
  135.7 1.8 %collective-permute-start.19 = (bf16[2,8,16,128]{3,2,1,0:T(8,128)(2,1)S(1)}, bf16[2,8,16,128]{3,2,1,0:T(8,128)(2,1)S(1)}, u32[]{:S(2)}, u32[]{:S(2)}) collective-permute-start(bf16[2,8,16,128]{3,2,1,0:T(8,128)(2,1)S(1)} %get-tuple-element.45), channel_id=1, source_target_pairs={{0,2},{1,3},{2,4},{3,5},{4,6},{5,7},{6,0},{7,1},{8,10},{9,11},{10,... | collective-permute-start | bytes 196616 | tf_op jit(solution)/shard_map/ppermute | solution.py:522
  137.5 2.4 %collective-permute-start.20 = (bf16[2,8,16,128]{3,2,1,0:T(8,128)(2,1)}, bf16[2,8,16,128]{3,2,1,0:T(8,128)(2,1)S(1)}, u32[]{:S(2)}, u32[]{:S(2)}) collective-permute-start(bf16[2,8,16,128]{3,2,1,0:T(8,128)(2,1)} %get-tuple-element.46), channel_id=1, source_target_pairs={{0,3},{1,4},{2,5},{3,6},{4,7},{5,0},{6,1},{7,2},{8,11},{9,12},{10,... | collective-permute-start | bytes 196616 | tf_op jit(solution)/shard_map/ppermute | solution.py:522
  139.9 2.3 %collective-permute-start.21 = (bf16[2,8,16,128]{3,2,1,0:T(8,128)(2,1)}, bf16[2,8,16,128]{3,2,1,0:T(8,128)(2,1)S(1)}, u32[]{:S(2)}, u32[]{:S(2)}) collective-permute-start(bf16[2,8,16,128]{3,2,1,0:T(8,128)(2,1)} %get-tuple-element.47), channel_id=1, source_target_pairs={{0,4},{1,5},{2,6},{3,7},{4,0},{5,1},{6,2},{7,3},{8,12},{9,13},{10,... | collective-permute-start | bytes 196616 | tf_op jit(solution)/shard_map/ppermute | solution.py:522
  142.2 1.9 %collective-permute-start.22 = (bf16[2,8,16,128]{3,2,1,0:T(8,128)(2,1)S(1)}, bf16[2,8,16,128]{3,2,1,0:T(8,128)(2,1)S(1)}, u32[]{:S(2)}, u32[]{:S(2)}) collective-permute-start(bf16[2,8,16,128]{3,2,1,0:T(8,128)(2,1)S(1)} %get-tuple-element.48), channel_id=1, source_target_pairs={{0,5},{1,6},{2,7},{3,0},{4,1},{5,2},{6,3},{7,4},{8,13},{9,14},{10,... | collective-permute-start | bytes 196616 | tf_op jit(solution)/shard_map/ppermute | solution.py:522
  144.1 1.6 %collective-permute-start.23 = (bf16[2,8,16,128]{3,2,1,0:T(8,128)(2,1)S(1)}, bf16[2,8,16,128]{3,2,1,0:T(8,128)(2,1)S(1)}, u32[]{:S(2)}, u32[]{:S(2)}) collective-permute-start(bf16[2,8,16,128]{3,2,1,0:T(8,128)(2,1)S(1)} %get-tuple-element.49), channel_id=1, source_target_pairs={{0,6},{1,7},{2,0},{3,1},{4,2},{5,3},{6,4},{7,5},{8,14},{9,15},{10,... | collective-permute-start | bytes 196616 | tf_op jit(solution)/shard_map/ppermute | solution.py:522
  147.2 4.3 %inverse_transform.1 = (f32[8,16,48,128]{3,2,1,0:T(8,128)}, f32[8,16,16,128]{3,2,1,0:T(8,128)S(1)}) custom-call(s32[1]{0:T(128)} %bitcast.2.me_ref, f32[8]{0:T(128)S(1)} %dynamic-slice_multiply_fusion.bias_ref, f32[16,2,8,256]{3,2,1,0:T(8,128)S(1)} %constant_dynamic-update-slice_fusion.spec_ref, f32[16,256]{1,0:T(8,128)S(1)} %select_multiply_fusion.depth_ref, ...), custom_call_target="tpu_custom_call" | custom-call | flops 2000000000 | bytes 5000000 | tf_op jit(solution)/shard_map/inverse_transform/pallas_call | solution.py:419
  151.5 3.4 %finish_early.1 = (bf16[8,16,64,128]{3,2,1,0:T(8,128)(2,1)}, f32[8,16,48,128]{3,2,1,0:T(8,128)}) custom-call(bf16[16,8,48,128]{3,2,1,0:T(8,128)(2,1)S(1)} %all-to-all-done.1.coded_ref, f32[8,16,48,128]{3,2,1,0:T(8,128)} %get-tuple-element.53.inverse_ref), custom_call_target="tpu_custom_call", output_to_operand_aliasing={{1}: (1, {})} | custom-call | flops 30000000 | bytes 8000000 | tf_op jit(solution)/shard_map/finish_early/pallas_call | solution.py:471
  155.2 1.8 %finish_late.1 = bf16[8,16,64,128]{3,2,1,0:T(8,128)(2,1)} custom-call(s32[2]{0:T(128)S(1)} %pad_add_fusion.place_ref, f32[8,16,16,128]{3,2,1,0:T(8,128)S(1)} %get-tuple-element.40.inverse_ref, bf16[2,8,16,128]{3,2,1,0:T(8,128)(2,1)S(1)} %get-tuple-element.43.refs_0_, ...), custom_call_target="tpu_custom_call", output_to_operand_aliasing={{}: (10, {})} | custom-call | flops 4000000 | bytes 1200000 | tf_op jit(solution)/shard_map/finish_late/pallas_call | solution.py:506
  (83 shorter events, 16.7 us)
Async XLA Ops:
  2.7 12.2 %copy-start = (bf16[1,8,8,128,128]{4,3,2,1,0:T(8,128)(2,1)S(1)}, bf16[1,8,8,128,128]{4,3,2,1,0:T(8,128)(2,1)}, u32[]{:S(2)}) copy-start(bf16[1,8,8,128,128]{4,3,2,1,0:T(8,128)(2,1)} %param.8) | copy-start | bytes 6291460
  2.7 12.2 %copy-start.3 = (f32[256,32]{1,0:T(8,128)S(1)}, f32[256,32]{1,0:T(8,128)}, u32[]{:S(2)}) copy-start(f32[256,32]{1,0:T(8,128)} %constant.218.clone.table_y_ref.table_x_ref) | copy-start | bytes 98308
  2.8 49.7 %all-to-all-start = ((bf16[16,48,8,128]{3,2,1,0:T(8,128)(2,1)}), bf16[16,48,8,128]{3,2,1,0:T(8,128)(2,1)}, u32[]{:S(2)}, u32[]{:S(2)}) async-start(bf16[16,48,8,128]{3,2,1,0:T(8,128)(2,1)} %get-tuple-element.51), calls=%async_computation | async-start | bytes 3145728 | tf_op jit(solution)/shard_map/all_to_all | solution.py:535
  17.0 4.2 %collective-permute-start.1 = (f32[2,2,2,2,8,256]{5,4,3,2,0,1:T(8,128)S(1)}, f32[2,2,2,2,8,256]{5,4,3,2,0,1:T(8,128)S(1)}, u32[]{:S(2)}, u32[]{:S(2)}) collective-permute-start(f32[2,2,2,2,8,256]{5,4,3,2,0,1:T(8,128)S(1)} %bitcast.40), channel_id=1, source_target_pairs={{0,16},{16,0},{32,48},{48,32},{64,80},{80,64},{96,112},{112,96},{1... | collective-permute-start | bytes 393224 | tf_op jit(solution)/shard_map/ppermute | solution.py:83
  18.1 55.7 %collective-permute-start = (bf16[8,16,8,128]{3,2,1,0:T(8,128)(2,1)S(1)}, bf16[8,16,8,128]{3,2,1,0:T(8,128)(2,1)S(1)}, u32[]{:S(2)}, u32[]{:S(2)}) collective-permute-start(bf16[8,16,8,128]{3,2,1,0:T(8,128)(2,1)S(1)} %copy-done.7), channel_id=1, source_target_pairs={{0,8},{1,9},{2,10},{3,11},{4,12},{5,13},{6,14},{7,15},{8,0},{9,1},... | collective-permute-start | bytes 786440 | tf_op jit(solution)/shard_map/ppermute | solution.py:536
  21.2 5.1 %collective-permute-start.2 = (f32[2,2,2,8,256]{4,3,2,1,0:T(8,128)S(1)}, f32[2,2,2,8,256]{4,3,2,1,0:T(8,128)S(1)}, u32[]{:S(2)}, u32[]{:S(2)}) collective-permute-start(f32[2,2,2,8,256]{4,3,2,1,0:T(8,128)S(1)} %dynamic-slice_bitcast_fusion), channel_id=1, source_target_pairs={{0,64},{16,80},{32,96},{48,112},{64,0},{80,16},{96,32},{112,48},{1... | collective-permute-start | bytes 196616 | tf_op jit(solution)/shard_map/ppermute | solution.py:83
  55.9 17.9 %copy-start.2 = (bf16[8,16,8,128]{3,2,1,0:T(8,128)(2,1)S(1)}, bf16[8,16,8,128]{3,2,1,0:T(8,128)(2,1)}, u32[]{:S(2)}) copy-start(bf16[8,16,8,128]{3,2,1,0:T(8,128)(2,1)} %get-tuple-element.30.own_cells_ref) | copy-start | bytes 786436
  55.9 95.7 %all-to-all-start.1 = ((bf16[16,8,48,128]{3,2,1,0:T(8,128)(2,1)}), bf16[16,8,48,128]{3,2,1,0:T(8,128)(2,1)S(1)}, u32[]{:S(2)}, u32[]{:S(2)}) async-start(bf16[16,8,48,128]{3,2,1,0:T(8,128)(2,1)} %get-tuple-element.52), calls=%async_computation.1 | async-start | bytes 3145728 | tf_op jit(solution)/shard_map/all_to_all | solution.py:544
  62.6 54.4 %copy-start.8 = (f32[128]{0:T(128)S(1)}, f32[128]{0:T(128)}, u32[]{:S(2)}) copy-start(f32[128]{0:T(128)} %param.10) | copy-start | bytes 1540
  62.7 2.9 %collective-permute-start.3 = (f32[2,2,8,256]{3,2,1,0:T(8,128)S(1)}, f32[2,2,8,256]{3,2,1,0:T(8,128)S(1)}, u32[]{:S(2)}, u32[]{:S(2)}) collective-permute-start(f32[2,2,8,256]{3,2,1,0:T(8,128)S(1)} %dynamic-slice_bitcast_fusion.1), channel_id=1, source_target_pairs={{0,32},{16,48},{32,0},{48,16},{64,96},{80,112},{96,64},{112,80},{1... | collective-permute-start | bytes 98312 | tf_op jit(solution)/shard_map/ppermute | solution.py:83
  65.5 3.0 %collective-permute-start.4 = (f32[2,8,256]{2,1,0:T(8,128)S(1)}, f32[2,8,256]{2,1,0:T(8,128)S(1)}, u32[]{:S(2)}, u32[]{:S(2)}) collective-permute-start(f32[2,8,256]{2,1,0:T(8,128)S(1)} %dynamic-slice_bitcast_fusion.2), channel_id=1, source_target_pairs={{0,128},{16,144},{32,160},{48,176},{64,192},{80,208},{96,224},{112... | collective-permute-start | bytes 49160 | tf_op jit(solution)/shard_map/ppermute | solution.py:83
  68.5 5.2 %collective-permute-start.5 = (bf16[4,8,128]{2,1,0:T(8,128)(2,1)S(1)}, bf16[4,8,128]{2,1,0:T(8,128)(2,1)S(1)}, u32[]{:S(2)}, u32[]{:S(2)}) collective-permute-start(bf16[4,8,128]{2,1,0:T(8,128)(2,1)S(1)} %bitcast.38), channel_id=1, source_target_pairs={{0,8},{1,9},{2,10},{3,11},{4,12},{5,13},{6,14},{7,15},{8,0},{9,1},... | collective-permute-start | bytes 24584 | tf_op jit(solution)/shard_map/ppermute | solution.py:540
  74.4 26.3 %collective-permute-start.6 = (bf16[2,20,8,128]{3,2,1,0:T(8,128)(2,1)S(1)}, bf16[2,20,8,128]{3,2,1,0:T(8,128)(2,1)S(1)}, u32[]{:S(2)}, u32[]{:S(2)}) collective-permute-start(bf16[2,20,8,128]{3,2,1,0:T(8,128)(2,1)S(1)} %get-tuple-element.33), channel_id=1, source_target_pairs={{0,1},{1,2},{2,3},{3,4},{4,5},{5,6},{6,7},{7,0},{8,9},{9,10},{10,1... | collective-permute-start | bytes 245768 | tf_op jit(solution)/shard_map/ppermute | solution.py:522
  75.2 29.1 %collective-permute-start.7 = (bf16[2,20,8,128]{3,2,1,0:T(8,128)(2,1)S(1)}, bf16[2,20,8,128]{3,2,1,0:T(8,128)(2,1)S(1)}, u32[]{:S(2)}, u32[]{:S(2)}) collective-permute-start(bf16[2,20,8,128]{3,2,1,0:T(8,128)(2,1)S(1)} %get-tuple-element.34), channel_id=1, source_target_pairs={{0,2},{1,3},{2,4},{3,5},{4,6},{5,7},{6,0},{7,1},{8,10},{9,11},{10,... | collective-permute-start | bytes 245768 | tf_op jit(solution)/shard_map/ppermute | solution.py:522
  79.2 28.2 %collective-permute-start.8 = (bf16[2,20,8,128]{3,2,1,0:T(8,128)(2,1)S(1)}, bf16[2,20,8,128]{3,2,1,0:T(8,128)(2,1)S(1)}, u32[]{:S(2)}, u32[]{:S(2)}) collective-permute-start(bf16[2,20,8,128]{3,2,1,0:T(8,128)(2,1)S(1)} %get-tuple-element.35), channel_id=1, source_target_pairs={{0,3},{1,4},{2,5},{3,6},{4,7},{5,0},{6,1},{7,2},{8,11},{9,12},{10,... | collective-permute-start | bytes 245768 | tf_op jit(solution)/shard_map/ppermute | solution.py:522
  79.8 34.2 %collective-permute-start.9 = (bf16[2,20,8,128]{3,2,1,0:T(8,128)(2,1)S(1)}, bf16[2,20,8,128]{3,2,1,0:T(8,128)(2,1)S(1)}, u32[]{:S(2)}, u32[]{:S(2)}) collective-permute-start(bf16[2,20,8,128]{3,2,1,0:T(8,128)(2,1)S(1)} %get-tuple-element.36), channel_id=1, source_target_pairs={{0,4},{1,5},{2,6},{3,7},{4,0},{5,1},{6,2},{7,3},{8,12},{9,13},{10,... | collective-permute-start | bytes 245768 | tf_op jit(solution)/shard_map/ppermute | solution.py:522
  84.8 29.2 %collective-permute-start.10 = (bf16[2,20,8,128]{3,2,1,0:T(8,128)(2,1)S(1)}, bf16[2,20,8,128]{3,2,1,0:T(8,128)(2,1)S(1)}, u32[]{:S(2)}, u32[]{:S(2)}) collective-permute-start(bf16[2,20,8,128]{3,2,1,0:T(8,128)(2,1)S(1)} %get-tuple-element.37), channel_id=1, source_target_pairs={{0,5},{1,6},{2,7},{3,0},{4,1},{5,2},{6,3},{7,4},{8,13},{9,14},{10,... | collective-permute-start | bytes 245768 | tf_op jit(solution)/shard_map/ppermute | solution.py:522
  100.7 13.3 %collective-permute-start.11 = (bf16[2,20,8,128]{3,2,1,0:T(8,128)(2,1)S(1)}, bf16[2,20,8,128]{3,2,1,0:T(8,128)(2,1)S(1)}, u32[]{:S(2)}, u32[]{:S(2)}) collective-permute-start(bf16[2,20,8,128]{3,2,1,0:T(8,128)(2,1)S(1)} %get-tuple-element.38), channel_id=1, source_target_pairs={{0,6},{1,7},{2,0},{3,1},{4,2},{5,3},{6,4},{7,5},{8,14},{9,15},{10,... | collective-permute-start | bytes 245768 | tf_op jit(solution)/shard_map/ppermute | solution.py:522
  104.3 9.7 %collective-permute-start.12 = (bf16[2,20,8,128]{3,2,1,0:T(8,128)(2,1)S(1)}, bf16[2,20,8,128]{3,2,1,0:T(8,128)(2,1)S(1)}, u32[]{:S(2)}, u32[]{:S(2)}) collective-permute-start(bf16[2,20,8,128]{3,2,1,0:T(8,128)(2,1)S(1)} %get-tuple-element.39), channel_id=1, source_target_pairs={{0,7},{1,0},{2,1},{3,2},{4,3},{5,4},{6,5},{7,6},{8,15},{9,8},{10,9... | collective-permute-start | bytes 245768 | tf_op jit(solution)/shard_map/ppermute | solution.py:522
  115.6 31.5 %copy-start.5 = (f32[2,16,128]{2,1,0:T(8,128)S(1)}, f32[2,16,128]{2,1,0:T(8,128)}, u32[]{:S(2)}) copy-start(f32[2,16,128]{2,1,0:T(8,128)} %constant.219.clone.waves_y_ref) | copy-start | bytes 49156
  116.6 2.7 %collective-permute-start.13 = (f32[1,2,8,256]{3,2,1,0:T(8,128)S(1)}, f32[1,2,8,256]{3,2,1,0:T(8,128)S(1)}, u32[]{:S(2)}, u32[]{:S(2)}) collective-permute-start(f32[1,2,8,256]{3,2,1,0:T(8,128)S(1)} %bitcast.34), channel_id=1, source_target_pairs={{0,128},{16,144},{32,160},{48,176},{64,192},{80,208},{96,224},{112... | collective-permute-start | bytes 49160 | tf_op jit(solution)/shard_map/ppermute | solution.py:98
  119.3 4.9 %collective-permute-start.14 = (f32[2,2,8,256]{3,2,1,0:T(8,128)S(1)}, f32[2,2,8,256]{3,2,1,0:T(8,128)S(1)}, u32[]{:S(2)}, u32[]{:S(2)}) collective-permute-start(f32[2,2,8,256]{3,2,1,0:T(8,128)S(1)} %pad_maximum_fusion.2), channel_id=1, source_target_pairs={{0,32},{16,48},{32,0},{48,16},{64,96},{80,112},{96,64},{112,80},{1... | collective-permute-start | bytes 98312 | tf_op jit(solution)/shard_map/ppermute | solution.py:98
  121.7 12.8 %collective-permute-start.17 = (bf16[8,8,16,128]{3,2,1,0:T(8,128)(2,1)S(1)}, bf16[8,8,16,128]{3,2,1,0:T(8,128)(2,1)S(1)}, u32[]{:S(2)}, u32[]{:S(2)}) collective-permute-start(bf16[8,8,16,128]{3,2,1,0:T(8,128)(2,1)S(1)} %get-tuple-element.42), channel_id=1, source_target_pairs={{0,8},{1,9},{2,10},{3,11},{4,12},{5,13},{6,14},{7,15},{8,0},{9,1},... | collective-permute-start | bytes 786440 | tf_op jit(solution)/shard_map/ppermute | solution.py:547
  124.3 4.7 %collective-permute-start.15 = (f32[4,2,8,256]{3,2,1,0:T(8,128)S(1)}, f32[4,2,8,256]{3,2,1,0:T(8,128)S(1)}, u32[]{:S(2)}, u32[]{:S(2)}) collective-permute-start(f32[4,2,8,256]{3,2,1,0:T(8,128)S(1)} %pad_maximum_fusion.1), channel_id=1, source_target_pairs={{0,64},{16,80},{32,96},{48,112},{64,0},{80,16},{96,32},{112,48},{1... | collective-permute-start | bytes 196616 | tf_op jit(solution)/shard_map/ppermute | solution.py:98
  129.0 8.5 %collective-permute-start.16 = (f32[8,2,8,256]{3,2,1,0:T(8,128)S(1)}, f32[8,2,8,256]{3,2,1,0:T(8,128)S(1)}, u32[]{:S(2)}, u32[]{:S(2)}) collective-permute-start(f32[8,2,8,256]{3,2,1,0:T(8,128)S(1)} %pad_maximum_fusion), channel_id=1, source_target_pairs={{0,16},{16,0},{32,48},{48,32},{64,80},{80,64},{96,112},{112,96},{1... | collective-permute-start | bytes 393224 | tf_op jit(solution)/shard_map/ppermute | solution.py:98
  135.7 8.4 %collective-permute-start.18 = (bf16[2,8,16,128]{3,2,1,0:T(8,128)(2,1)S(1)}, bf16[2,8,16,128]{3,2,1,0:T(8,128)(2,1)S(1)}, u32[]{:S(2)}, u32[]{:S(2)}) collective-permute-start(bf16[2,8,16,128]{3,2,1,0:T(8,128)(2,1)S(1)} %get-tuple-element.44), channel_id=1, source_target_pairs={{0,1},{1,2},{2,3},{3,4},{4,5},{5,6},{6,7},{7,0},{8,9},{9,10},{10,1... | collective-permute-start | bytes 196616 | tf_op jit(solution)/shard_map/ppermute | solution.py:522
  135.7 10.0 %collective-permute-start.19 = (bf16[2,8,16,128]{3,2,1,0:T(8,128)(2,1)S(1)}, bf16[2,8,16,128]{3,2,1,0:T(8,128)(2,1)S(1)}, u32[]{:S(2)}, u32[]{:S(2)}) collective-permute-start(bf16[2,8,16,128]{3,2,1,0:T(8,128)(2,1)S(1)} %get-tuple-element.45), channel_id=1, source_target_pairs={{0,2},{1,3},{2,4},{3,5},{4,6},{5,7},{6,0},{7,1},{8,10},{9,11},{10,... | collective-permute-start | bytes 196616 | tf_op jit(solution)/shard_map/ppermute | solution.py:522
  137.5 17.4 %collective-permute-start.20 = (bf16[2,8,16,128]{3,2,1,0:T(8,128)(2,1)}, bf16[2,8,16,128]{3,2,1,0:T(8,128)(2,1)S(1)}, u32[]{:S(2)}, u32[]{:S(2)}) collective-permute-start(bf16[2,8,16,128]{3,2,1,0:T(8,128)(2,1)} %get-tuple-element.46), channel_id=1, source_target_pairs={{0,3},{1,4},{2,5},{3,6},{4,7},{5,0},{6,1},{7,2},{8,11},{9,12},{10,... | collective-permute-start | bytes 196616 | tf_op jit(solution)/shard_map/ppermute | solution.py:522
  139.9 15.0 %collective-permute-start.21 = (bf16[2,8,16,128]{3,2,1,0:T(8,128)(2,1)}, bf16[2,8,16,128]{3,2,1,0:T(8,128)(2,1)S(1)}, u32[]{:S(2)}, u32[]{:S(2)}) collective-permute-start(bf16[2,8,16,128]{3,2,1,0:T(8,128)(2,1)} %get-tuple-element.47), channel_id=1, source_target_pairs={{0,4},{1,5},{2,6},{3,7},{4,0},{5,1},{6,2},{7,3},{8,12},{9,13},{10,... | collective-permute-start | bytes 196616 | tf_op jit(solution)/shard_map/ppermute | solution.py:522
  142.2 12.8 %collective-permute-start.22 = (bf16[2,8,16,128]{3,2,1,0:T(8,128)(2,1)S(1)}, bf16[2,8,16,128]{3,2,1,0:T(8,128)(2,1)S(1)}, u32[]{:S(2)}, u32[]{:S(2)}) collective-permute-start(bf16[2,8,16,128]{3,2,1,0:T(8,128)(2,1)S(1)} %get-tuple-element.48), channel_id=1, source_target_pairs={{0,5},{1,6},{2,7},{3,0},{4,1},{5,2},{6,3},{7,4},{8,13},{9,14},{10,... | collective-permute-start | bytes 196616 | tf_op jit(solution)/shard_map/ppermute | solution.py:522
  144.1 11.0 %collective-permute-start.23 = (bf16[2,8,16,128]{3,2,1,0:T(8,128)(2,1)S(1)}, bf16[2,8,16,128]{3,2,1,0:T(8,128)(2,1)S(1)}, u32[]{:S(2)}, u32[]{:S(2)}) collective-permute-start(bf16[2,8,16,128]{3,2,1,0:T(8,128)(2,1)S(1)} %get-tuple-element.49), channel_id=1, source_target_pairs={{0,6},{1,7},{2,0},{3,1},{4,2},{5,3},{6,4},{7,5},{8,14},{9,15},{10,... | collective-permute-start | bytes 196616 | tf_op jit(solution)/shard_map/ppermute | solution.py:522
  145.8 9.5 %collective-permute-start.24 = (bf16[2,8,16,128]{3,2,1,0:T(8,128)(2,1)S(1)}, bf16[2,8,16,128]{3,2,1,0:T(8,128)(2,1)S(1)}, u32[]{:S(2)}, u32[]{:S(2)}) collective-permute-start(bf16[2,8,16,128]{3,2,1,0:T(8,128)(2,1)S(1)} %get-tuple-element.50), channel_id=1, source_target_pairs={{0,7},{1,0},{2,1},{3,2},{4,3},{5,4},{6,5},{7,6},{8,15},{9,8},{10,9... | collective-permute-start | bytes 196616 | tf_op jit(solution)/shard_map/ppermute | solution.py:522
  (4 other events, 27.0 us)
